TPU v7x, 512 devices: a whole 4x4x16 slice. The times are simulated.
512 devices in a mesh: seq: 64 (over z, x), head: 8 (over y, core).
Axes of the slice: x: 4, y: 4, z: 16, core: 2. Of those that a mesh axis runs over, the one named last changes fastest.
Arguments:
- act: bfloat16 [32768, 4608], P('seq', 'head'), may hold values from -6 to 6
- query_rows: bfloat16 [32768, 2048], P('seq', 'head'), may hold values from -6 to 6
- key_rows: bfloat16 [32768, 1024], P('seq', 'head'), may hold values from -6 to 6
- out_adjoint: bfloat16 [32768, 2048], P('seq', 'head'), may hold values from -0.59765625 to 0.59765625
- basis_input: bfloat16 [4608, 4608], P('seq', 'head'), may hold values from -0.09375 to 0.09375
- basis_grad: bfloat16 [8, 128, 128], P('head'), may hold values from -0.5 to 0.5
- eigvals: bfloat16 [4608, 1024], P('head'), may hold values from 0.0019 to 30.5, as said below
- query_act: bfloat16 [64, 4608], P(None, 'head'), may hold values from -6 to 6
- query_adj: bfloat16 [64, 1024], P(None, 'head'), may hold values from -6 to 6
Outputs:
- influence: float32 [32768], P('seq')
Inputs may be any that keep to these rules, and one draw needn't show every extreme that they name: eigvals are positive.
All inputs are finite; a program needn't handle non-finite values.
Results may differ from a plain program's by a relative error of at most 0.018.
Values may be sent and summed in bfloat16 or wider, within the bound.
No kernel may reach another device: no remote copies, remote signals or barrier semaphores. Data moves between devices by JAX's collectives and lax.ppermute only.
A program may use at most 64 MiB of HBM per device.

v0:
```python
import jax
import jax.numpy as jnp
from jax import lax
from jax.sharding import PartitionSpec as P

WINDOW = 4096


SCORE_SCALE = 1.0 / 12.0
SOFT_CAP = 50.0
DAMP_FACTOR = 0.1


def shifted(value, axis, by):
    size = lax.axis_size(axis)
    pairs = [(i, i + by) for i in range(size) if 0 <= i + by < size]
    return lax.ppermute(value, axis, pairs)


def attend(query_head, key_head, adjoint_head, seq_index, key_span):
    local_rows = query_head.shape[0]
    raw = (
        jnp.einsum("ad,otd->aot", query_head, key_head, preferred_element_type=jnp.float32)
        * SCORE_SCALE
    )
    capped = SOFT_CAP * jnp.tanh(raw / SOFT_CAP)
    query_pos = seq_index * local_rows + jnp.arange(local_rows, dtype=jnp.int32)
    offsets = jnp.arange(key_span + 1, dtype=jnp.int32)
    key_pos = (seq_index - offsets)[:, None] * local_rows + jnp.arange(local_rows, dtype=jnp.int32)[
        None, :
    ]
    gap_pos = query_pos[:, None, None] - key_pos[None, :, :]
    valid = (key_pos[None, :, :] >= 0) & (gap_pos >= 0) & (gap_pos < WINDOW)
    weights = jnp.where(valid, jnp.exp(capped), jnp.zeros_like(capped))
    totals = jnp.sum(weights, axis=(1, 2), keepdims=True)
    probs = (weights / totals).astype(jnp.bfloat16)
    return jnp.einsum("aot,ad->otd", probs, adjoint_head, preferred_element_type=jnp.float32)


def rotate_heads(matrix, basis_grad):
    row_count = matrix.shape[0]
    split_heads = matrix.reshape(row_count, basis_grad.shape[0], basis_grad.shape[1])
    turned = jnp.einsum("the,hef->thf", split_heads, basis_grad, preferred_element_type=jnp.float32)
    return turned.reshape(row_count, -1).astype(jnp.bfloat16)


def on_device(
    act, query_rows, key_rows, out_adjoint, basis_input, basis_grad, eigvals, query_act, query_adj
):
    local_rows = act.shape[0]
    head_width = basis_grad.shape[1]
    key_span = WINDOW // local_rows
    seq_index = lax.axis_index("seq")
    earlier = [key_rows]
    for offset in range(1, key_span + 1):
        earlier.append(shifted(key_rows, "seq", offset))
    key_stack = jnp.stack(earlier, axis=0)
    group_sum = None
    for member in range(2):
        q_lower = member * head_width
        q_upper = q_lower + head_width
        term = attend(
            query_rows[:, q_lower:q_upper],
            key_stack,
            out_adjoint[:, q_lower:q_upper],
            seq_index,
            key_span,
        )
        group_sum = term if group_sum is None else group_sum + term
    pieces = group_sum.astype(jnp.bfloat16)
    adjoint_sum = pieces[0].astype(jnp.float32)
    for offset in range(1, key_span + 1):
        arrived = shifted(pieces[offset], "seq", -offset)
        adjoint_sum = adjoint_sum + arrived.astype(jnp.float32)
    value_adjoint = adjoint_sum.astype(jnp.bfloat16)
    turned_tokens = rotate_heads(value_adjoint, basis_grad)
    turned_query = rotate_heads(query_adj, basis_grad)
    all_turned, all_query_turned = (
        lax.all_gather(turned_tokens, "head", axis=1, tiled=True),
        lax.all_gather(turned_query, "head", axis=1, tiled=True),
    )
    full_act, full_query_act = (
        lax.all_gather(act, "head", axis=1, tiled=True),
        lax.all_gather(query_act, "head", axis=1, tiled=True),
    )
    piece = lax.all_gather(basis_input, "seq", axis=0, tiled=True)
    rotated_tokens = jnp.dot(full_act, piece, preferred_element_type=jnp.float32)
    rotated_query = jnp.dot(full_query_act, piece, preferred_element_type=jnp.float32)
    rotated_tokens = rotated_tokens.astype(jnp.bfloat16)
    rotated_query = rotated_query.astype(jnp.bfloat16)
    query_grad = (
        jnp.dot(rotated_query.T, all_query_turned, preferred_element_type=jnp.float32)
        / query_act.shape[0]
    )
    local_total = jnp.sum(eigvals, dtype=jnp.float32)
    eigen_total = lax.psum(local_total, "head")
    damping = (
        DAMP_FACTOR * eigen_total / (eigvals.shape[0] * lax.axis_size("head") * eigvals.shape[1])
    )
    scaled = (query_grad / (eigvals.astype(jnp.float32) + damping)).astype(jnp.bfloat16)
    mapped = jnp.dot(rotated_tokens, scaled, preferred_element_type=jnp.float32)
    partial_score = jnp.sum(mapped * all_turned.astype(jnp.float32), axis=1)
    return lax.psum(partial_score, "head")


def solution(mesh):
    return jax.shard_map(
        on_device,
        mesh=mesh,
        in_specs=(
            P("seq", "head"),
            P("seq", "head"),
            P("seq", "head"),
            P("seq", "head"),
            P("seq", "head"),
            P("head", None, None),
            P("head", None),
            P(None, "head"),
            P(None, "head"),
        ),
        out_specs=P("seq"),
        check_vma=False,
    )
```

profile of v0, /device:TPU:1, one launch (start us, length us, event | category | flops | bytes accessed | tf_op | source)
XLA Modules:
  0.0 271.4 jit_solution(7622759506121470838)
XLA Ops:
  6.5 0.0 copy-start
  6.5 0.7 all-gather.8.cloned.1.call-update
  7.3 0.0 all-gather.10.cloned.1.call-start
  7.3 3.9 %collective-permute-start = (bf16[512,128]{1,0:T(8,128)(2,1)}, bf16[512,128]{1,0:T(8,128)(2,1)S(1)}, u32[]{:S(2)}, u32[]{:S(2)}) collective-permute-start(bf16[512,128]{1,0:T(8,128)(2,1)} %param.11), channel_id=1, source_target_pairs={{0,8},{8,16},{16,24},{24,32},{32,40},{40,48},{48,56},{56,64},{64,7... | collective-permute-start | bytes 393224 | tf_op jit(solution)/shard_map/ppermute | solution.py:17
  11.3 4.4 %collective-permute-start.1 = (bf16[512,128]{1,0:T(8,128)(2,1)}, bf16[512,128]{1,0:T(8,128)(2,1)S(1)}, u32[]{:S(2)}, u32[]{:S(2)}) collective-permute-start(bf16[512,128]{1,0:T(8,128)(2,1)} %param.11), channel_id=1, source_target_pairs={{0,16},{8,24},{16,32},{24,40},{32,48},{40,56},{48,64},{56,72},{64,... | collective-permute-start | bytes 393224 | tf_op jit(solution)/shard_map/ppermute | solution.py:17
  15.6 4.4 %collective-permute-start.2 = (bf16[512,128]{1,0:T(8,128)(2,1)}, bf16[512,128]{1,0:T(8,128)(2,1)S(1)}, u32[]{:S(2)}, u32[]{:S(2)}) collective-permute-start(bf16[512,128]{1,0:T(8,128)(2,1)} %param.11), channel_id=1, source_target_pairs={{0,24},{8,32},{16,40},{24,48},{32,56},{40,64},{48,72},{56,80},{64,... | collective-permute-start | bytes 393224 | tf_op jit(solution)/shard_map/ppermute | solution.py:17
  20.1 3.5 %collective-permute-start.3 = (bf16[512,128]{1,0:T(8,128)(2,1)}, bf16[512,128]{1,0:T(8,128)(2,1)S(1)}, u32[]{:S(2)}, u32[]{:S(2)}) collective-permute-start(bf16[512,128]{1,0:T(8,128)(2,1)} %param.11), channel_id=1, source_target_pairs={{0,32},{8,40},{16,48},{24,56},{32,64},{40,72},{48,80},{56,88},{64,... | collective-permute-start | bytes 393224 | tf_op jit(solution)/shard_map/ppermute | solution.py:17
  23.6 3.6 %collective-permute-start.4 = (bf16[512,128]{1,0:T(8,128)(2,1)}, bf16[512,128]{1,0:T(8,128)(2,1)S(1)}, u32[]{:S(2)}, u32[]{:S(2)}) collective-permute-start(bf16[512,128]{1,0:T(8,128)(2,1)} %param.11), channel_id=1, source_target_pairs={{0,40},{8,48},{16,56},{24,64},{32,72},{40,80},{48,88},{56,96},{64,... | collective-permute-start | bytes 393224 | tf_op jit(solution)/shard_map/ppermute | solution.py:17
  27.2 0.1 iota_add_fusion
  27.3 0.9 bitcast_dynamic-update-slice_fusion.8
  28.2 0.1 broadcast_compare_fusion
  28.3 0.0 collective-permute-done
  28.3 6.3 %collective-permute-start.5 = (bf16[512,128]{1,0:T(8,128)(2,1)}, bf16[512,128]{1,0:T(8,128)(2,1)S(1)}, u32[]{:S(2)}, u32[]{:S(2)}) collective-permute-start(bf16[512,128]{1,0:T(8,128)(2,1)} %param.11), channel_id=1, source_target_pairs={{0,48},{8,56},{16,64},{24,72},{32,80},{40,88},{48,96},{56,104},{64... | collective-permute-start | bytes 393224 | tf_op jit(solution)/shard_map/ppermute | solution.py:17
  34.7 0.0 collective-permute-done.1
  34.7 6.1 %collective-permute-start.6 = (bf16[512,128]{1,0:T(8,128)(2,1)}, bf16[512,128]{1,0:T(8,128)(2,1)S(1)}, u32[]{:S(2)}, u32[]{:S(2)}) collective-permute-start(bf16[512,128]{1,0:T(8,128)(2,1)} %param.11), channel_id=1, source_target_pairs={{0,56},{8,64},{16,72},{24,80},{32,88},{40,96},{48,104},{56,112},{6... | collective-permute-start | bytes 393224 | tf_op jit(solution)/shard_map/ppermute | solution.py:17
  40.8 0.0 collective-permute-done.2
  40.8 5.2 %collective-permute-start.7 = (bf16[512,128]{1,0:T(8,128)(2,1)}, bf16[512,128]{1,0:T(8,128)(2,1)S(1)}, u32[]{:S(2)}, u32[]{:S(2)}) collective-permute-start(bf16[512,128]{1,0:T(8,128)(2,1)} %param.11), channel_id=1, source_target_pairs={{0,64},{8,72},{16,80},{24,88},{32,96},{40,104},{48,112},{56,120},{... | collective-permute-start | bytes 393224 | tf_op jit(solution)/shard_map/ppermute | solution.py:17
  46.1 0.0 collective-permute-done.3
  46.1 0.0 collective-permute-done.4
  46.1 0.0 collective-permute-done.5
  46.2 0.0 collective-permute-done.6
  46.2 2.5 collective-permute-done.7
  48.8 1.4 fusion.22
  50.2 0.0 copy-start.5
  50.2 7.3 %fusion.3 = (f32[512]{0:T(512)S(1)}, f32[512]{0:T(512)S(1)}, f32[9,512,512]{2,1,0:T(8,128)S(1)}) fusion(s32[9,512]{1,0:T(8,128)S(1)} %iota_add_fusion, s32[512]{0:T(512)S(1)} %iota_add_fusion.1, pred[9,512]{1,0:T(8,128)(4,1)S(1)} %broadcast_compare_fusion, f32[9,512,512]{2,1,0:T(8,128)S(1)} %fusion.22, ...), kind=kOutput, calls=%fused_computation.9 | convolution fusion | flops 634649600 | bytes 20232192 | tf_op jit(solution)/shard_map/ad,otd->aot/dot_general | solution.py:23
  57.5 5.1 %fusion.4 = f32[9,512,128]{2,1,0:T(8,128)S(1)} fusion(f32[9,512,512]{2,1,0:T(8,128)S(1)} %fusion.22, f32[512]{0:T(512)S(1)} %get-tuple-element.6, bf16[512,256]{1,0:T(8,128)(2,1)S(1)} %copy-done.5, s32[9,512]{1,0:T(8,128)S(1)} %iota_add_fusion, s32[512]{0:T(512)S(1)} %iota_add_fusion.1, pred[9,512]{1,0:T(8,128)(4,1)S(1)} %broadcast_compare_fusion), kind=kOutput, calls=%fused_computation.10 | convolution fusion | flops 627572736 | bytes 11972608 | tf_op jit(solution)/shard_map/aot,ad->otd/dot_general | solution.py:37
  62.7 5.6 %add_convert_fusion = bf16[9,512,128]{2,1,0:T(8,128)(2,1)S(1)} fusion(f32[9,512,128]{2,1,0:T(8,128)S(1)} %fusion.4, f32[9,512,512]{2,1,0:T(8,128)S(1)} %get-tuple-element.15, f32[512]{0:T(512)S(1)} %get-tuple-element.5, bf16[512,256]{1,0:T(8,128)(2,1)S(1)} %copy-done.5, s32[9,512]{1,0:T(8,128)S(1)} %iota_add_fusion, s32[512]{0:T(512)S(1)} %iota_add_fusion.1, ...), kind=kOutput, calls=%fused_computation.16 | convolution fusion | flops 628752384 | bytes 13152256 | tf_op jit(solution)/shard_map/aot,ad->otd/dot_general | solution.py:37
  68.3 0.0 copy-start.1
  68.3 0.0 copy-start.2
  68.3 0.1 slice_bitcast_fusion.7
  68.4 1.4 collective-permute-start.10
  69.8 1.3 collective-permute-start.11
  71.1 1.3 collective-permute-start.12
  72.4 1.3 collective-permute-start.13
  73.7 1.3 collective-permute-start.14
  75.0 0.8 collective-permute-done.10
  75.8 1.3 collective-permute-start.15
  77.1 5.3 %collective-permute-done.11 = bf16[512,128]{1,0:T(8,128)(2,1)S(1)} collective-permute-done((bf16[512,128]{1,0:T(8,128)(2,1)S(1)}, bf16[512,128]{1,0:T(8,128)(2,1)S(1)}, u32[]{:S(2)}, u32[]{:S(2)}) %collective-permute-start.11) | collective-permute-done | bytes 131104 | tf_op jit(solution)/shard_map/ppermute | solution.py:17
  82.4 1.3 collective-permute-start.8
  83.7 4.0 %collective-permute-done.12 = bf16[512,128]{1,0:T(8,128)(2,1)S(1)} collective-permute-done((bf16[512,128]{1,0:T(8,128)(2,1)S(1)}, bf16[512,128]{1,0:T(8,128)(2,1)S(1)}, u32[]{:S(2)}, u32[]{:S(2)}) %collective-permute-start.12) | collective-permute-done | bytes 131104 | tf_op jit(solution)/shard_map/ppermute | solution.py:17
  87.7 1.3 collective-permute-start.9
  89.0 2.4 collective-permute-done.13
  91.4 3.4 %collective-permute-done.14 = bf16[512,128]{1,0:T(8,128)(2,1)S(1)} collective-permute-done((bf16[512,128]{1,0:T(8,128)(2,1)S(1)}, bf16[512,128]{1,0:T(8,128)(2,1)S(1)}, u32[]{:S(2)}, u32[]{:S(2)}) %collective-permute-start.14) | collective-permute-done | bytes 131104 | tf_op jit(solution)/shard_map/ppermute | solution.py:17
  94.8 10.6 %collective-permute-done.15 = bf16[512,128]{1,0:T(8,128)(2,1)S(1)} collective-permute-done((bf16[512,128]{1,0:T(8,128)(2,1)S(1)}, bf16[512,128]{1,0:T(8,128)(2,1)S(1)}, u32[]{:S(2)}, u32[]{:S(2)}) %collective-permute-start.15) | collective-permute-done | bytes 131104 | tf_op jit(solution)/shard_map/ppermute | solution.py:17
  105.4 0.0 collective-permute-done.8
  105.4 0.0 collective-permute-done.9
  105.4 0.9 convolution_convert_fusion.1
  106.3 0.0 all-gather.10.cloned.1.call-update
  106.3 0.0 all-gather.6.cloned.1.call-start
  106.4 0.7 all-gather.6.cloned.1.call-update
  107.1 0.0 copy-start.4
  107.1 1.2 convert_reduce_fusion
  108.3 19.5 %psum.14 = f32[]{:T(128)} all-reduce(f32[]{:T(128)} %convert_reduce_fusion), channel_id=1, replica_groups=mesh['seq'=64,'head'=8] {'head'}, use_global_device_ids=true, to_apply=%region_1.2 | all-reduce | flops 1 | bytes 8 | tf_op jit(solution)/shard_map/psum | solution.py:96
  127.8 13.9 %all-gather.1 = bf16[8,576,64]{1,2,0:T(8,128)(2,1)S(1)} all-gather(bf16[1,576,64]{1,2,0:T(8,128)(2,1)S(1)} %bitcast.95), channel_id=1, replica_groups=mesh['seq'=64,'head'=8] {'head'}, dimensions={0}, use_global_device_ids=true | all-gather | bytes 663552 | tf_op jit(solution)/shard_map/all_gather | solution.py:84
  141.7 0.4 copy.11
  142.1 0.4 reshape.72
  143.2 0.1 fusion.8
  143.3 11.3 %all-gather = bf16[64,1,1024]{2,0,1:T(8,128)(2,1)S(1)} all-gather(bf16[64,1,128]{2,0,1:T(8,128)(2,1)S(1)} %fusion.8), channel_id=2, replica_groups=mesh['seq'=64,'head'=8] {'head'}, dimensions={2}, use_global_device_ids=true | all-gather | bytes 147456 | tf_op jit(solution)/shard_map/all_gather | solution.py:80
  154.6 6.9 %all-gather.8.cloned.1.call-done = bf16[4608,576]{1,0:T(8,128)(2,1)} async-done(((bf16[72,576]{1,0:T(8,128)(2,1)}), bf16[4608,576]{1,0:T(8,128)(2,1)}) %all-gather.8.cloned.1.call-update) | async-done | bytes 5308432 | tf_op jit(solution)/shard_map/all_gather | solution.py:86
  161.5 4.2 %fusion.7 = bf16[576,1024]{1,0:T(8,128)(2,1)S(1)} fusion(bf16[576,1024]{1,0:T(8,128)(2,1)S(1)} %copy-done.1, f32[]{:T(128)S(6)} %div.38, bf16[4608,64]{0,1:T(8,128)(2,1)S(1)} %reshape.72, bf16[4608,576]{1,0:T(8,128)(2,1)} %all-gather.8.cloned.1.call-done, bf16[64,1,1024]{2,0,1:T(8,128)(2,1)S(1)} %all-gather), kind=kOutput, calls=%fused_computation.15 | convolution fusion | flops 418222080 | bytes 8388612 | tf_op jit(solution)/shard_map/dot_general | solution.py:92
  165.7 33.2 %all-gather.10.cloned.1.call-done = bf16[512,1024]{1,0:T(8,128)(2,1)} async-done(((bf16[512,128]{1,0:T(8,128)(2,1)}), bf16[512,1024]{1,0:T(8,128)(2,1)}) %all-gather.10.cloned.1.call-update) | async-done | bytes 1048592 | tf_op jit(solution)/shard_map/all_gather | solution.py:79
  198.9 45.1 %all-gather.6.cloned.1.call-done = bf16[512,4608]{0,1:T(8,128)(2,1)} async-done(((bf16[512,576]{0,1:T(8,128)(2,1)}), bf16[512,4608]{0,1:T(8,128)(2,1)}) %all-gather.6.cloned.1.call-update) | async-done | bytes 4718608 | tf_op jit(solution)/shard_map/all_gather | solution.py:83
  244.0 8.2 %multiply_reduce_fusion = f32[512]{0:T(512)S(1)} fusion(bf16[512,1024]{1,0:T(8,128)(2,1)} %all-gather.10.cloned.1.call-done, bf16[576,1024]{1,0:T(8,128)(2,1)S(1)} %fusion.7, bf16[512,4608]{0,1:T(8,128)(2,1)} %all-gather.6.cloned.1.call-done, bf16[4608,576]{1,0:T(8,128)(2,1)} %all-gather.8.cloned.1.call-done), kind=kOutput, calls=%fused_computation.17 | convolution fusion | flops 3323756032 | bytes 12257280 | tf_op jit(solution)/shard_map/dot_general | solution.py:101
  252.2 12.6 %psum.15 = f32[512]{0:T(512)} all-reduce(f32[512]{0:T(512)S(1)} %multiply_reduce_fusion), channel_id=1, replica_groups=mesh['seq'=64,'head'=8] {'head'}, use_global_device_ids=true, to_apply=%region_5.6 | all-reduce | flops 512 | bytes 4096 | tf_op jit(solution)/shard_map/psum | solution.py:103
  (18 shorter events, 0.2 us)
Async XLA Ops:
  6.5 98.8 %copy-start = (bf16[1,128,128]{2,1,0:T(8,128)(2,1)S(1)}, bf16[1,128,128]{2,1,0:T(8,128)(2,1)}, u32[]{:S(2)}) copy-start(bf16[1,128,128]{2,1,0:T(8,128)(2,1)} %param.14) | copy-start | bytes 98308
  6.5 42.2 %copy-start.3 = (bf16[512,256]{1,0:T(8,128)(2,1)S(1)}, bf16[512,256]{1,0:T(8,128)(2,1)}, u32[]{:S(2)}) copy-start(bf16[512,256]{1,0:T(8,128)(2,1)} %param.10) | copy-start | bytes 786436
  6.5 155.0 %all-gather.8.cloned.1.call-start = ((), (), s32[]{:S(2)}) async-start(), calls=%async_computation.1 | async-start | bytes 5990400 | tf_op jit(solution)/shard_map/all_gather | solution.py:86
  7.3 191.6 %all-gather.10.cloned.1.call-start = ((), (), s32[]{:S(2)}) async-start(), calls=%async_computation.2 | async-start | bytes 1179648 | tf_op jit(solution)/shard_map/all_gather | solution.py:79
  7.3 21.0 %collective-permute-start = (bf16[512,128]{1,0:T(8,128)(2,1)}, bf16[512,128]{1,0:T(8,128)(2,1)S(1)}, u32[]{:S(2)}, u32[]{:S(2)}) collective-permute-start(bf16[512,128]{1,0:T(8,128)(2,1)} %param.11), channel_id=1, source_target_pairs={{0,8},{8,16},{16,24},{24,32},{32,40},{40,48},{48,56},{56,64},{64,7... | collective-permute-start | bytes 393224 | tf_op jit(solution)/shard_map/ppermute | solution.py:17
  11.3 23.4 %collective-permute-start.1 = (bf16[512,128]{1,0:T(8,128)(2,1)}, bf16[512,128]{1,0:T(8,128)(2,1)S(1)}, u32[]{:S(2)}, u32[]{:S(2)}) collective-permute-start(bf16[512,128]{1,0:T(8,128)(2,1)} %param.11), channel_id=1, source_target_pairs={{0,16},{8,24},{16,32},{24,40},{32,48},{40,56},{48,64},{56,72},{64,... | collective-permute-start | bytes 393224 | tf_op jit(solution)/shard_map/ppermute | solution.py:17
  15.6 25.2 %collective-permute-start.2 = (bf16[512,128]{1,0:T(8,128)(2,1)}, bf16[512,128]{1,0:T(8,128)(2,1)S(1)}, u32[]{:S(2)}, u32[]{:S(2)}) collective-permute-start(bf16[512,128]{1,0:T(8,128)(2,1)} %param.11), channel_id=1, source_target_pairs={{0,24},{8,32},{16,40},{24,48},{32,56},{40,64},{48,72},{56,80},{64,... | collective-permute-start | bytes 393224 | tf_op jit(solution)/shard_map/ppermute | solution.py:17
  20.1 26.0 %collective-permute-start.3 = (bf16[512,128]{1,0:T(8,128)(2,1)}, bf16[512,128]{1,0:T(8,128)(2,1)S(1)}, u32[]{:S(2)}, u32[]{:S(2)}) collective-permute-start(bf16[512,128]{1,0:T(8,128)(2,1)} %param.11), channel_id=1, source_target_pairs={{0,32},{8,40},{16,48},{24,56},{32,64},{40,72},{48,80},{56,88},{64,... | collective-permute-start | bytes 393224 | tf_op jit(solution)/shard_map/ppermute | solution.py:17
  23.6 22.5 %collective-permute-start.4 = (bf16[512,128]{1,0:T(8,128)(2,1)}, bf16[512,128]{1,0:T(8,128)(2,1)S(1)}, u32[]{:S(2)}, u32[]{:S(2)}) collective-permute-start(bf16[512,128]{1,0:T(8,128)(2,1)} %param.11), channel_id=1, source_target_pairs={{0,40},{8,48},{16,56},{24,64},{32,72},{40,80},{48,88},{56,96},{64,... | collective-permute-start | bytes 393224 | tf_op jit(solution)/shard_map/ppermute | solution.py:17
  28.3 17.9 %collective-permute-start.5 = (bf16[512,128]{1,0:T(8,128)(2,1)}, bf16[512,128]{1,0:T(8,128)(2,1)S(1)}, u32[]{:S(2)}, u32[]{:S(2)}) collective-permute-start(bf16[512,128]{1,0:T(8,128)(2,1)} %param.11), channel_id=1, source_target_pairs={{0,48},{8,56},{16,64},{24,72},{32,80},{40,88},{48,96},{56,104},{64... | collective-permute-start | bytes 393224 | tf_op jit(solution)/shard_map/ppermute | solution.py:17
  34.7 11.5 %collective-permute-start.6 = (bf16[512,128]{1,0:T(8,128)(2,1)}, bf16[512,128]{1,0:T(8,128)(2,1)S(1)}, u32[]{:S(2)}, u32[]{:S(2)}) collective-permute-start(bf16[512,128]{1,0:T(8,128)(2,1)} %param.11), channel_id=1, source_target_pairs={{0,56},{8,64},{16,72},{24,80},{32,88},{40,96},{48,104},{56,112},{6... | collective-permute-start | bytes 393224 | tf_op jit(solution)/shard_map/ppermute | solution.py:17
  40.8 7.9 %collective-permute-start.7 = (bf16[512,128]{1,0:T(8,128)(2,1)}, bf16[512,128]{1,0:T(8,128)(2,1)S(1)}, u32[]{:S(2)}, u32[]{:S(2)}) collective-permute-start(bf16[512,128]{1,0:T(8,128)(2,1)} %param.11), channel_id=1, source_target_pairs={{0,64},{8,72},{16,80},{24,88},{32,96},{40,104},{48,112},{56,120},{... | collective-permute-start | bytes 393224 | tf_op jit(solution)/shard_map/ppermute | solution.py:17
  50.2 7.4 %copy-start.5 = (bf16[512,256]{1,0:T(8,128)(2,1)S(1)}, bf16[512,256]{1,0:T(8,128)(2,1)}, u32[]{:S(2)}) copy-start(bf16[512,256]{1,0:T(8,128)(2,1)} %param.12) | copy-start | bytes 786436
  68.3 38.8 %copy-start.1 = (bf16[576,1024]{1,0:T(8,128)(2,1)S(1)}, bf16[576,1024]{1,0:T(8,128)(2,1)}, u32[]{:S(2)}) copy-start(bf16[576,1024]{1,0:T(8,128)(2,1)} %param.15) | copy-start | bytes 3538948
  68.3 59.4 %copy-start.2 = (bf16[64,576]{1,0:T(8,128)(2,1)S(1)}, bf16[64,576]{1,0:T(8,128)(2,1)}, u32[]{:S(2)}) copy-start(bf16[64,576]{1,0:T(8,128)(2,1)} %param.16) | copy-start | bytes 221188
  68.4 7.4 %collective-permute-start.10 = (bf16[512,128]{1,0:T(8,128)(2,1)S(1)}, bf16[512,128]{1,0:T(8,128)(2,1)S(1)}, u32[]{:S(2)}, u32[]{:S(2)}) collective-permute-start(bf16[512,128]{1,0:T(8,128)(2,1)S(1)} %get-tuple-element.13), channel_id=1, source_target_pairs={{24,0},{32,8},{40,16},{48,24},{56,32},{64,40},{72,48},{80,56},{88,... | collective-permute-start | bytes 393224 | tf_op jit(solution)/shard_map/ppermute | solution.py:17
  69.8 12.5 %collective-permute-start.11 = (bf16[512,128]{1,0:T(8,128)(2,1)S(1)}, bf16[512,128]{1,0:T(8,128)(2,1)S(1)}, u32[]{:S(2)}, u32[]{:S(2)}) collective-permute-start(bf16[512,128]{1,0:T(8,128)(2,1)S(1)} %get-tuple-element.12), channel_id=1, source_target_pairs={{32,0},{40,8},{48,16},{56,24},{64,32},{72,40},{80,48},{88,56},{96,... | collective-permute-start | bytes 393224 | tf_op jit(solution)/shard_map/ppermute | solution.py:17
  71.1 16.6 %collective-permute-start.12 = (bf16[512,128]{1,0:T(8,128)(2,1)S(1)}, bf16[512,128]{1,0:T(8,128)(2,1)S(1)}, u32[]{:S(2)}, u32[]{:S(2)}) collective-permute-start(bf16[512,128]{1,0:T(8,128)(2,1)S(1)} %get-tuple-element.11), channel_id=1, source_target_pairs={{40,0},{48,8},{56,16},{64,24},{72,32},{80,40},{88,48},{96,56},{104... | collective-permute-start | bytes 393224 | tf_op jit(solution)/shard_map/ppermute | solution.py:17
  72.4 18.9 %collective-permute-start.13 = (bf16[512,128]{1,0:T(8,128)(2,1)S(1)}, bf16[512,128]{1,0:T(8,128)(2,1)S(1)}, u32[]{:S(2)}, u32[]{:S(2)}) collective-permute-start(bf16[512,128]{1,0:T(8,128)(2,1)S(1)} %get-tuple-element.10), channel_id=1, source_target_pairs={{48,0},{56,8},{64,16},{72,24},{80,32},{88,40},{96,48},{104,56},{11... | collective-permute-start | bytes 393224 | tf_op jit(solution)/shard_map/ppermute | solution.py:17
  73.7 21.0 %collective-permute-start.14 = (bf16[512,128]{1,0:T(8,128)(2,1)S(1)}, bf16[512,128]{1,0:T(8,128)(2,1)S(1)}, u32[]{:S(2)}, u32[]{:S(2)}) collective-permute-start(bf16[512,128]{1,0:T(8,128)(2,1)S(1)} %get-tuple-element.9), channel_id=1, source_target_pairs={{56,0},{64,8},{72,16},{80,24},{88,32},{96,40},{104,48},{112,56},{1... | collective-permute-start | bytes 393224 | tf_op jit(solution)/shard_map/ppermute | solution.py:17
  75.8 29.6 %collective-permute-start.15 = (bf16[512,128]{1,0:T(8,128)(2,1)S(1)}, bf16[512,128]{1,0:T(8,128)(2,1)S(1)}, u32[]{:S(2)}, u32[]{:S(2)}) collective-permute-start(bf16[512,128]{1,0:T(8,128)(2,1)S(1)} %get-tuple-element.8), channel_id=1, source_target_pairs={{64,0},{72,8},{80,16},{88,24},{96,32},{104,40},{112,48},{120,56},{... | collective-permute-start | bytes 393224 | tf_op jit(solution)/shard_map/ppermute | solution.py:17
  82.4 23.0 %collective-permute-start.8 = (bf16[512,128]{1,0:T(8,128)(2,1)S(1)}, bf16[512,128]{1,0:T(8,128)(2,1)S(1)}, u32[]{:S(2)}, u32[]{:S(2)}) collective-permute-start(bf16[512,128]{1,0:T(8,128)(2,1)S(1)} %get-tuple-element.7), channel_id=1, source_target_pairs={{8,0},{16,8},{24,16},{32,24},{40,32},{48,40},{56,48},{64,56},{72,6... | collective-permute-start | bytes 393224 | tf_op jit(solution)/shard_map/ppermute | solution.py:17
  87.7 17.7 %collective-permute-start.9 = (bf16[512,128]{1,0:T(8,128)(2,1)S(1)}, bf16[512,128]{1,0:T(8,128)(2,1)S(1)}, u32[]{:S(2)}, u32[]{:S(2)}) collective-permute-start(bf16[512,128]{1,0:T(8,128)(2,1)S(1)} %get-tuple-element.14), channel_id=1, source_target_pairs={{16,0},{24,8},{32,16},{40,24},{48,32},{56,40},{64,48},{72,56},{80,... | collective-permute-start | bytes 393224 | tf_op jit(solution)/shard_map/ppermute | solution.py:17
  106.3 137.7 %all-gather.6.cloned.1.call-start = ((), (), s32[]{:S(2)}) async-start(), calls=%async_computation | async-start | bytes 5308416 | tf_op jit(solution)/shard_map/all_gather | solution.py:83
  107.1 36.1 %copy-start.4 = (bf16[64,128]{1,0:T(8,128)(2,1)S(1)}, bf16[64,128]{1,0:T(8,128)(2,1)}, u32[]{:S(2)}) copy-start(bf16[64,128]{1,0:T(8,128)(2,1)} %param.17) | copy-start | bytes 49156
Sparse Core Ops, SparseCore 0:
  10.3 151.1 all-gather.7
  163.6 35.2 all-gather.9
  201.0 42.9 all-gather.5
where the time goes:
time: 272 us; the launch traced here: 271 us
  waiting for transfers between devices  116 us (43%)
  blocking collectives  57.3 us (21%)
  starting transfers between devices  48 us (18%)
  matrix products  33 us (12%)
  between operations  14.1 us (5%)
    ppermute x16, starting transfers between devices, shifted(): return lax.ppermute(value, axis, pairs)  47.9 us
    all_gather x1, waiting for transfers between devices, on_device(): lax.all_gather(act, 'head', axis=1, tiled=True)  45.1 us
    all_gather x1, waiting for transfers between devices, on_device(): lax.all_gather(turned_tokens, 'head', axis=1, tiled=True)  33.2 us
    ppermute x16, waiting for transfers between devices, shifted(): return lax.ppermute(value, axis, pairs)  29 us
    psum x1, blocking collectives, on_device(): eigen_total = lax.psum(local_total, 'head')  19.5 us
    all_gather x1, blocking collectives, on_device(): lax.all_gather(query_act, 'head', axis=1, tiled=True)  13.9 us
    psum x1, blocking collectives, on_device(): return lax.psum(partial_score, 'head')  12.6 us
    all_gather x1, blocking collectives, on_device(): lax.all_gather(turned_query, 'head', axis=1, tiled=True)  11.3 us
  transfers between devices with their start and end apart: 19, of which 10 were waited for; matrix products, arithmetic and copies ran while one was open for 10% of the time, Pallas kernels for 0%

commit v1 on v0

v1 whole, which is shorter than its diff:
```python
import functools

import jax
import jax.numpy as jnp
from jax import lax
from jax.experimental import pallas as pl
from jax.experimental.pallas import tpu as pltpu
from jax.sharding import PartitionSpec as P

WINDOW = 4096
SCORE_SCALE = 1.0 / 12.0
SOFT_CAP = 50.0
DAMP_FACTOR = 0.1
LOG2E = 1.4426950408889634
NX = 4
NC = 4
BF = jnp.bfloat16
F32 = jnp.float32
NT = (((1,), (1,)), ((), ()))
TN = (((0,), (0,)), ((), ()))
INTERPRET = False


def vmem(n):
    return [pl.BlockSpec(memory_space=pltpu.VMEM) for _ in range(n)]


def shift_z(value, by, wrap):
    size = lax.axis_size("seq")
    pairs = [(i, (i + by * NX) % size) for i in range(size) if wrap or 0 <= i + by * NX < size]
    return lax.ppermute(value, "seq", pairs)


def shift_x(value, by):
    size = lax.axis_size("seq")
    pairs = [(i, i // NX * NX + (i % NX + by) % NX) for i in range(size)]
    return lax.ppermute(value, "seq", pairs)


def shift_h(value, to):
    size = lax.axis_size("head")
    return lax.ppermute(value, "head", [(i, to(i, size)) for i in range(size)])


def x_groups():
    size = lax.axis_size("seq")
    return [[z * NX + x for x in range(NX)] for z in range(size // NX)]


def c_groups():
    size = lax.axis_size("seq")
    return [
        [(b * NC + c) * NX + x for c in range(NC)]
        for b in range(size // NX // NC)
        for x in range(NX)
    ]


def attend_kernel(span, s_ref, q_ref, a_ref, z2, z1, z0, p1, p2, p3, own, b1, b2, b3, kbuf, w, tot, adjt):
    rows, hd = z0.shape
    s = s_ref[0]
    pairs = (p1, p2, p3)
    kbuf[0] = z0[...]
    kbuf[4] = z1[...]
    kbuf[8] = z2[...]
    for k in range(1, 4):
        kbuf[k + 4] = pairs[k - 1][0]
        kbuf[k] = pairs[k - 1][1]
    tot[...] = jnp.zeros_like(tot)
    half = rows // 2

    def block(o, mode):
        for piece in range(2):
            lo = piece * half
            keys = kbuf[o, lo : lo + half, :]
            for m in range(2):
                raw = lax.dot_general(
                    keys, q_ref[:, m * hd : (m + 1) * hd], NT, preferred_element_type=F32
                )
                e = jnp.exp2(jnp.tanh(raw * (SCORE_SCALE / SOFT_CAP)) * (SOFT_CAP * LOG2E))
                if mode != 0:
                    key_i = lo + lax.broadcasted_iota(jnp.int32, e.shape, 0)
                    query_i = lax.broadcasted_iota(jnp.int32, e.shape, 1)
                    keep = key_i <= query_i if mode < 0 else key_i > query_i
                    e = jnp.where(keep, e, 0.0)
                tot[m] += jnp.sum(e.reshape(half // 8, 8, rows), axis=0)
                w[o, lo : lo + half, m * rows : (m + 1) * rows] = e.astype(BF)

    block(0, -1)

    def step(o, carry):
        block(o, 0)
        return carry

    lax.fori_loop(1, jnp.minimum(s, span - 1) + 1, step, 0)

    @pl.when(s >= span)
    def _():
        block(span, 1)

    @pl.when(s < span)
    def _():
        def clear(o, carry):
            w[o] = jnp.zeros(w.shape[1:], BF)
            return carry

        lax.fori_loop(s + 1, span + 1, clear, 0)

    for m in range(2):
        inv = 1.0 / jnp.sum(tot[m], axis=0, keepdims=True)
        turned = a_ref[:, m * hd : (m + 1) * hd].astype(F32).T
        adjt[:, m * rows : (m + 1) * rows] = (turned * inv).astype(BF)
    for o in range(span + 1):
        piece = lax.dot_general(w[o], adjt[...], NT, preferred_element_type=F32).astype(BF)
        if o % 4 == 0:
            own[2 - o // 4] = piece
        else:
            (b1, b2, b3)[o % 4 - 1][1 - o // 4] = piece


def attend(s, q, a, keys, pairs, span):
    rows, hd = keys[0].shape
    pair = jax.ShapeDtypeStruct((2, rows, hd), BF)
    return pl.pallas_call(
        functools.partial(attend_kernel, span),
        out_shape=(jax.ShapeDtypeStruct((3, rows, hd), BF), pair, pair, pair),
        in_specs=[pl.BlockSpec(memory_space=pltpu.SMEM)] + vmem(8),
        out_specs=tuple(vmem(4)),
        scratch_shapes=[
            pltpu.VMEM((span + 1, rows, hd), BF),
            pltpu.VMEM((span + 1, rows, 2 * rows), BF),
            pltpu.VMEM((2, 8, rows), F32),
            pltpu.VMEM((hd, 2 * rows), BF),
        ],
        interpret=INTERPRET,
        name="attend",
    )(s, q, a, *keys, *pairs)


def rotate_query_kernel(hd, h_ref, pack, *refs):
    *blocks, out = refs
    acc = None
    for j, block in enumerate(blocks):
        chunk = pack[h_ref[j]][:, hd : hd + block.shape[0]]
        term = jnp.dot(chunk, block[...], preferred_element_type=F32)
        acc = term if acc is None else acc + term
    acc = acc.astype(BF)
    for i in range(out.shape[0]):
        out[i] = acc


def rotate_query(h_index, pack, blocks, hd):
    return pl.pallas_call(
        functools.partial(rotate_query_kernel, hd),
        out_shape=jax.ShapeDtypeStruct((NX, pack.shape[1], blocks[0].shape[1]), BF),
        in_specs=[pl.BlockSpec(memory_space=pltpu.SMEM)] + vmem(1 + len(blocks)),
        out_specs=vmem(1)[0],
        interpret=INTERPRET,
        name="rotate_query",
    )(h_index, pack, *blocks)


def spread_kernel(damp_ref, rq, pack, eig, *refs):
    *blocks, out = refs
    hd = eig.shape[1]
    total = rq[0].astype(F32)
    for i in range(1, rq.shape[0]):
        total = total + rq[i].astype(F32)
    grad = lax.dot_general(
        total.astype(BF), pack[0][:, :hd], TN, preferred_element_type=F32
    ) * (1.0 / rq.shape[1])
    scaled = (grad / (eig[...].astype(F32) + damp_ref[0])).astype(BF)
    for j, block in enumerate(blocks):
        out[0, j] = jnp.dot(block[...], scaled, preferred_element_type=F32).astype(BF)


def spread(damping, rq, pack, eig, blocks, hd):
    heads = pack.shape[0]
    rows, cols = blocks[0].shape
    return pl.pallas_call(
        spread_kernel,
        grid=(heads,),
        out_shape=jax.ShapeDtypeStruct((heads, len(blocks), rows, hd), BF),
        in_specs=[
            pl.BlockSpec(memory_space=pltpu.SMEM),
            pl.BlockSpec(rq.shape, lambda g: (0, 0, 0)),
            pl.BlockSpec((1,) + pack.shape[1:], lambda g: (g, 0, 0)),
            pl.BlockSpec((cols, hd), lambda g: (0, g)),
        ]
        + [pl.BlockSpec((rows, cols), lambda g: (0, 0)) for _ in blocks],
        out_specs=pl.BlockSpec((1, len(blocks), rows, hd), lambda g: (g, 0, 0, 0)),
        interpret=INTERPRET,
        name="spread",
    )(damping, rq, pack, eig, *blocks)


def map_tokens_kernel(i_ref, n_ref, bg_ref, partner, *refs):
    *mine, out = refs
    acc = None
    for i, ref in enumerate(mine):
        term = lax.dot_general(n_ref[i_ref[i]], ref[...], TN, preferred_element_type=F32)
        acc = term if acc is None else acc + term
    for i in range(partner.shape[0]):
        acc = acc + lax.dot_general(
            n_ref[i_ref[len(mine) + i]], partner[i], TN, preferred_element_type=F32
        )
    turned = jnp.dot(bg_ref[...], acc.astype(BF), preferred_element_type=F32)
    out[...] = turned.T


def map_tokens(index, n8, bg, mine, partner):
    cols, rows = mine[0].shape
    hd = bg.shape[0]
    steps = 4 if rows % 512 == 0 else 1
    tile = rows // steps
    return pl.pallas_call(
        map_tokens_kernel,
        grid=(steps,),
        out_shape=jax.ShapeDtypeStruct((rows, hd), F32),
        in_specs=[
            pl.BlockSpec(memory_space=pltpu.SMEM),
            pl.BlockSpec(n8.shape, lambda g: (0, 0, 0)),
            pl.BlockSpec(bg.shape, lambda g: (0, 0)),
            pl.BlockSpec((partner.shape[0], cols, tile), lambda g: (0, 0, g)),
        ]
        + [pl.BlockSpec((cols, tile), lambda g: (0, g)) for _ in mine],
        out_specs=pl.BlockSpec((tile, hd), lambda g: (g, 0)),
        interpret=INTERPRET,
        name="map_tokens",
    )(index, n8, bg, partner, *mine)


def rounded(value):
    return lax.reduce_precision(value, 8, 7)


def on_device(
    act, query_rows, key_rows, out_adjoint, basis_input, basis_grad, eigvals, query_act, query_adj
):
    rows, cols = act.shape
    hd = basis_grad.shape[1]
    heads = lax.axis_size("head")
    n_seq = lax.axis_size("seq")
    n_z = n_seq // NX
    n_m = n_z // NC
    z_per_head = n_z // heads
    kr = basis_input.shape[0]
    lq = query_act.shape[0]
    span = WINDOW // rows
    s = lax.axis_index("seq")
    h = lax.axis_index("head")
    z, x = s >> 2, s & 3
    b = z >> 2

    key_1 = shift_z(key_rows, 1, False)
    key_2 = shift_z(key_rows, 2, False)
    ahead = [x + k < NX for k in range(4)]
    pairs = []
    for k in range(1, 4):
        pair = jnp.stack(
            [jnp.where(ahead[k], key_1, key_2), jnp.where(ahead[k], key_rows, key_1)]
        )
        pairs.append(shift_x(pair, k))

    basis = [basis_input] + [shift_z(basis_input, -NC * j, True) for j in range(1, n_m)]

    n_y = heads // 2
    act_t = act.T
    mine = [act_t] + [shift_h(act_t, lambda i, n, j=j: (i + 2 * j) % n) for j in range(1, n_y)]
    partner = shift_h(jnp.stack(mine), lambda i, n: i ^ 1)

    turned_query = jnp.dot(query_adj, basis_grad[0], preferred_element_type=F32).astype(BF)
    local = jnp.sum(eigvals, dtype=F32)
    high = rounded(local)
    mid = rounded(local - high)
    low = local - high - mid
    parts = jnp.stack([high, mid, low]).astype(BF)
    offset = ((z & (z_per_head - 1)) * NX + x) * kr
    chunk = lax.dynamic_slice_in_dim(query_act, offset, kr, 1)
    pack = jnp.concatenate(
        [
            turned_query,
            chunk,
            jnp.broadcast_to(parts[None], (lq, 3)),
            jnp.zeros((lq, hd - kr - 3), BF),
        ],
        axis=1,
    )
    pack = lax.all_to_all(jnp.broadcast_to(pack[None], (heads,) + pack.shape), "head", 0, 0)
    eigen_total = jnp.sum(pack[:, 0, hd + kr : hd + kr + 3].astype(F32))
    damping = DAMP_FACTOR * eigen_total / (cols * heads * eigvals.shape[1])

    h_index = ((z + NC * jnp.arange(n_m, dtype=jnp.int32)) & (n_z - 1)) // z_per_head
    rq = rotate_query(h_index, pack, basis, hd)
    rq = lax.all_to_all(rq, "seq", 0, 0, axis_index_groups=x_groups())
    rq = jnp.sum(rq.astype(F32), axis=0).astype(BF)
    rq = jnp.broadcast_to(rq[None], (NC,) + rq.shape)
    rq = lax.all_to_all(rq, "seq", 0, 0, axis_index_groups=c_groups())

    n = spread(damping[None], rq, pack, eigvals, basis, hd)
    n = lax.all_to_all(n, "head", 0, 0)
    n = jnp.sum(n.astype(F32), axis=0).astype(BF)
    n = jnp.broadcast_to(n[None], (NC,) + n.shape)
    n = lax.all_to_all(n, "seq", 0, 0, axis_index_groups=c_groups())
    n = jnp.broadcast_to(n[None], (NX,) + n.shape)
    n = lax.all_to_all(n, "seq", 0, 0, axis_index_groups=x_groups())
    n = n.transpose(2, 1, 0, 3, 4).reshape(heads, cols, hd)
    j = jnp.arange(n_y, dtype=jnp.int32)
    order = (h + 2 * (n_y - j)) & (heads - 1)
    order = jnp.concatenate([order, order ^ 1])
    index = 2 * (((order >> 1) - b) & (n_m - 1)) + (order & 1)
    mapped = map_tokens(index, n, basis_grad[0], mine, partner)

    own, *back = attend(
        s[None], query_rows, out_adjoint, (key_2, key_1, key_rows), pairs, span
    )
    own = own.astype(F32)
    sum_0, sum_1, sum_2 = own[2], own[1], own[0]
    for k in range(1, 4):
        got = shift_x(back[k - 1], -k).astype(F32)
        sum_0 = sum_0 + jnp.where(ahead[k], got[1], 0.0)
        sum_1 = sum_1 + jnp.where(ahead[k], got[0], got[1])
        sum_2 = sum_2 + jnp.where(ahead[k], 0.0, got[0])
    got_1 = shift_z(sum_1.astype(BF), -1, False)
    got_2 = shift_z(sum_2.astype(BF), -2, False)
    value_adjoint = sum_0 + got_1.astype(F32) + got_2.astype(F32)
    partial = jnp.sum(mapped * value_adjoint, axis=1)
    partial = jnp.broadcast_to(partial.reshape(1, -1, 128), (heads, rows // 128, 128))
    partial = lax.all_to_all(partial, "head", 0, 0)
    return jnp.sum(partial, axis=0).reshape(rows)


def solution(mesh):
    return jax.shard_map(
        on_device,
        mesh=mesh,
        in_specs=(
            P("seq", "head"),
            P("seq", "head"),
            P("seq", "head"),
            P("seq", "head"),
            P("seq", "head"),
            P("head", None, None),
            P("head", None),
            P(None, "head"),
            P(None, "head"),
        ),
        out_specs=P("seq"),
        check_vma=False,
    )
```

time: 272 us -> 219 us (0.81); the launches traced: 271 us -> 214 us
  waiting for transfers between devices: 116 us -> 40.3 us
  starting transfers between devices: 48 us -> 102 us
  matrix products: 33 us -> 0.9 us
  blocking collectives: 57.3 us -> 25.6 us
  Pallas kernels: 0 us -> 22 us
  other arithmetic: 1.36 us -> 10.4 us
  between operations: 14.1 us -> 5.93 us
  local copies, waits for them, and re-layouts: 1.98 us -> 7.59 us
    all_gather x3 -> x0, waiting for transfers between devices: 85.2 us -> none  [the longest x1 45.1 us: on_device(): lax.all_gather(act, 'head', axis=1, tiled=True)]
    all_to_all x0 -> x5, starting transfers between devices: none -> 36.5 us  [the longest x1 10.2 us: on_device(): lax.all_to_all(jnp.broadcast_to(pack[None], (heads,) + pack.shape), 'head...]
    dot_general x8 -> x1, matrix products: 33 us -> 0.9 us  [on_device(): jnp.dot(query_adj, basis_grad[0], preferred_element_type=F32).astype(BF)]
    psum x2 -> x0, blocking collectives: 32.1 us -> none  [the longest x1 19.5 us: on_device(): eigen_total = lax.psum(local_total, 'head')]
    all_to_all x0 -> x2, blocking collectives: none -> 25.6 us  [the longest x1 13.8 us: on_device(): n = lax.all_to_all(n, 'head', 0, 0)]
    all_gather x2 -> x0, blocking collectives: 25.2 us -> none  [the longest x1 13.9 us: on_device(): lax.all_gather(query_act, 'head', axis=1, tiled=True)]
    pallas_call x0 -> x4, Pallas kernels: none -> 22 us  [the longest x1 7.56 us: spread(): pl.pallas_call(spread_kernel, grid=(heads,), out_shape=jax.ShapeDtypeStru...]
    ppermute x16 -> x17, starting transfers between devices: 47.9 us -> 65.2 us  [the longest x7 30.4 us: shift_z(): return lax.ppermute(value, 'seq', pairs)]
  transfers between devices with their start and end apart: 19 -> 22, of which waited for: 10 -> 9; matrix products, arithmetic and copies ran while one was open for 10% -> 5% of each run, Pallas kernels for 0% -> 9%
where the time goes in v1:
time: 219 us; the launch traced here: 214 us
  starting transfers between devices  102 us (47%)
  waiting for transfers between devices  40.3 us (18%)
  blocking collectives  25.6 us (12%)
  Pallas kernels  22 us (10%)
  other arithmetic  10.4 us (5%)
  local copies, waits for them, and re-layouts  7.59 us (3%)
  between operations  5.93 us (3%)
    ppermute x7, starting transfers between devices, shift_z(): return lax.ppermute(value, 'seq', pairs)  30.4 us
    ppermute x6, starting transfers between devices, shift_x(): return lax.ppermute(value, 'seq', pairs)  22.8 us
    ppermute x4, waiting for transfers between devices, shift_h(): return lax.ppermute(value, 'head', [(i, to(i, size)) for i in range(size)])  15.8 us
    ppermute x7, waiting for transfers between devices, shift_z(): return lax.ppermute(value, 'seq', pairs)  15.6 us
    all_to_all x1, blocking collectives, on_device(): n = lax.all_to_all(n, 'head', 0, 0)  13.8 us
    ppermute x4, starting transfers between devices, shift_h(): return lax.ppermute(value, 'head', [(i, to(i, size)) for i in range(size)])  12 us
    all_to_all x1, blocking collectives, on_device(): partial = lax.all_to_all(partial, 'head', 0, 0)  11.8 us
    all_to_all x1, starting transfers between devices, on_device(): lax.all_to_all(jnp.broadcast_to(pack[None], (heads,) + pack.shape), 'head...  10.2 us
  transfers between devices with their start and end apart: 22, of which 9 were waited for; matrix products, arithmetic and copies ran while one was open for 5% of the time, Pallas kernels for 9%

profile of v1, /device:TPU:1, one launch (start us, length us, event | category | flops | bytes accessed | tf_op | source)
XLA Modules:
  0.0 214.4 jit_solution(14352044616208112207)
XLA Ops:
  0.0 2.5 %convert_reduce_fusion = f32[]{:T(128)} fusion(bf16[576,1024]{1,0:T(8,128)(2,1)} %eig.1), kind=kLoop, calls=%fused_computation.1 | loop fusion | flops 1179647 | bytes 1179652 | tf_op jit(solution)/shard_map/reduce_sum | solution.py:273
  7.5 0.1 constant_dynamic-slice_fusion
  7.5 0.9 convolution_convert_fusion
  8.4 0.1 pad.13.clone
  8.5 0.1 pad_maximum_fusion.4
  8.6 0.7 broadcast_in_dim.58
  9.4 10.2 %all-to-all-start = ((bf16[8,64,256]{2,1,0:T(8,128)(2,1)}), bf16[8,64,256]{2,1,0:T(8,128)(2,1)S(1)}, u32[]{:S(2)}, u32[]{:S(2)}) async-start(bf16[8,64,256]{2,1,0:T(8,128)(2,1)} %broadcast_in_dim.58), calls=%async_computation | async-start | bytes 524288 | tf_op jit(solution)/shard_map/all_to_all | solution.py:289
  19.5 8.3 %collective-permute-start = (bf16[72,576]{1,0:T(8,128)(2,1)}, bf16[72,576]{1,0:T(8,128)(2,1)S(1)}, u32[]{:S(2)}, u32[]{:S(2)}) collective-permute-start(bf16[72,576]{1,0:T(8,128)(2,1)} %refs_0_.3), channel_id=1, source_target_pairs={{0,384},{8,392},{16,400},{24,408},{32,416},{40,424},{48,432},{56,4... | collective-permute-start | bytes 248840 | tf_op jit(solution)/shard_map/ppermute | solution.py:31
  27.8 4.9 %collective-permute-start.1 = (bf16[72,576]{1,0:T(8,128)(2,1)}, bf16[72,576]{1,0:T(8,128)(2,1)S(1)}, u32[]{:S(2)}, u32[]{:S(2)}) collective-permute-start(bf16[72,576]{1,0:T(8,128)(2,1)} %refs_0_.3), channel_id=1, source_target_pairs={{0,256},{8,264},{16,272},{24,280},{32,288},{40,296},{48,304},{56,3... | collective-permute-start | bytes 248840 | tf_op jit(solution)/shard_map/ppermute | solution.py:31
  32.7 7.3 %collective-permute-start.2 = (bf16[72,576]{1,0:T(8,128)(2,1)}, bf16[72,576]{1,0:T(8,128)(2,1)S(1)}, u32[]{:S(2)}, u32[]{:S(2)}) collective-permute-start(bf16[72,576]{1,0:T(8,128)(2,1)} %refs_0_.3), channel_id=1, source_target_pairs={{0,128},{8,136},{16,144},{24,152},{32,160},{40,168},{48,176},{56,1... | collective-permute-start | bytes 248840 | tf_op jit(solution)/shard_map/ppermute | solution.py:31
  40.0 0.6 and_select_fusion.h_ref
  40.6 0.0 collective-permute-done.refs_1_
  40.6 2.2 %collective-permute-done.1.refs_2_ = bf16[72,576]{1,0:T(8,128)(2,1)S(1)} collective-permute-done((bf16[72,576]{1,0:T(8,128)(2,1)}, bf16[72,576]{1,0:T(8,128)(2,1)S(1)}, u32[]{:S(2)}, u32[]{:S(2)}) %collective-permute-start.1) | collective-permute-done | bytes 82976 | tf_op jit(solution)/shard_map/ppermute | solution.py:31
  42.7 4.4 %collective-permute-done.2.refs_3_ = bf16[72,576]{1,0:T(8,128)(2,1)S(1)} collective-permute-done((bf16[72,576]{1,0:T(8,128)(2,1)}, bf16[72,576]{1,0:T(8,128)(2,1)S(1)}, u32[]{:S(2)}, u32[]{:S(2)}) %collective-permute-start.2) | collective-permute-done | bytes 82976 | tf_op jit(solution)/shard_map/ppermute | solution.py:31
  47.1 0.6 copy-done.13
  47.7 0.7 copy-done.2
  48.4 2.1 rotate_query.1
  50.5 3.5 %all-to-all-start.1 = ((bf16[4,64,576]{2,1,0:T(8,128)(2,1)}), bf16[4,64,576]{2,1,0:T(8,128)(2,1)S(1)}, u32[]{:S(2)}, u32[]{:S(2)}) async-start(bf16[4,64,576]{2,1,0:T(8,128)(2,1)} %rotate_query.1), calls=%async_computation.1 | async-start | bytes 655360 | tf_op jit(solution)/shard_map/all_to_all | solution.py:295
  54.0 4.6 %collective-permute-start.5 = (bf16[576,512]{1,0:T(8,128)(2,1)S(1)}, bf16[576,512]{1,0:T(8,128)(2,1)S(1)}, u32[]{:S(2)}, u32[]{:S(2)}) collective-permute-start(bf16[576,512]{1,0:T(8,128)(2,1)S(1)} %bitcast.48), channel_id=1, source_target_pairs={{0,6},{1,7},{2,0},{3,1},{4,2},{5,3},{6,4},{7,5},{8,14},{9,15},{10,... | collective-permute-start | bytes 1769480 | tf_op jit(solution)/shard_map/ppermute | solution.py:42
  58.6 2.5 %collective-permute-start.4 = (bf16[576,512]{1,0:T(8,128)(2,1)S(1)}, bf16[576,512]{1,0:T(8,128)(2,1)S(1)}, u32[]{:S(2)}, u32[]{:S(2)}) collective-permute-start(bf16[576,512]{1,0:T(8,128)(2,1)S(1)} %bitcast.49), channel_id=1, source_target_pairs={{0,4},{1,5},{2,6},{3,7},{4,0},{5,1},{6,2},{7,3},{8,12},{9,13},{10,... | collective-permute-start | bytes 1769480 | tf_op jit(solution)/shard_map/ppermute | solution.py:42
  61.1 2.5 %collective-permute-start.3 = (bf16[576,512]{1,0:T(8,128)(2,1)S(1)}, bf16[576,512]{1,0:T(8,128)(2,1)S(1)}, u32[]{:S(2)}, u32[]{:S(2)}) collective-permute-start(bf16[576,512]{1,0:T(8,128)(2,1)S(1)} %bitcast.50), channel_id=1, source_target_pairs={{0,2},{1,3},{2,4},{3,5},{4,6},{5,7},{6,0},{7,1},{8,10},{9,11},{10,... | collective-permute-start | bytes 1769480 | tf_op jit(solution)/shard_map/ppermute | solution.py:42
  63.6 0.1 reduce_sum.62
  63.7 0.8 broadcast_in_dim.60
  64.4 9.7 %all-to-all-start.2 = ((bf16[4,64,576]{2,1,0:T(8,128)(2,1)}), bf16[4,64,576]{2,1,0:T(8,128)(2,1)S(1)}, u32[]{:S(2)}, u32[]{:S(2)}) async-start(bf16[4,64,576]{2,1,0:T(8,128)(2,1)} %broadcast_in_dim.60), calls=%async_computation.2 | async-start | bytes 655360 | tf_op jit(solution)/shard_map/all_to_all | solution.py:298
  74.1 1.7 collective-permute-done.4.refs_2_
  75.8 14.1 %collective-permute-done.3.refs_1_ = bf16[576,512]{1,0:T(8,128)(2,1)S(1)} collective-permute-done((bf16[576,512]{1,0:T(8,128)(2,1)S(1)}, bf16[576,512]{1,0:T(8,128)(2,1)S(1)}, u32[]{:S(2)}, u32[]{:S(2)}) %collective-permute-start.3) | collective-permute-done | bytes 589856 | tf_op jit(solution)/shard_map/ppermute | solution.py:42
  89.9 1.8 pad_maximum_fusion
  91.7 2.4 %collective-permute-start.6 = (bf16[4,576,512]{2,1,0:T(8,128)(2,1)}, bf16[4,576,512]{2,1,0:T(8,128)(2,1)}, u32[]{:S(2)}, u32[]{:S(2)}) collective-permute-start(bf16[4,576,512]{2,1,0:T(8,128)(2,1)} %pad_maximum_fusion), channel_id=1, source_target_pairs={{0,1},{1,0},{2,3},{3,2},{4,5},{5,4},{6,7},{7,6},{8,9},{9,8},{10,11... | collective-permute-start | bytes 7077896 | tf_op jit(solution)/shard_map/ppermute | solution.py:42
  94.1 1.4 fusion.15
  96.2 0.7 copy-done.7
  96.9 7.6 %spread.1 = bf16[8,4,72,128]{3,2,1,0:T(8,128)(2,1)} custom-call(f32[1]{0:T(128)} %bitcast.4.damp_ref, bf16[4,64,576]{2,1,0:T(8,128)(2,1)} %copy-done.7, bf16[8,64,256]{2,1,0:T(8,128)(2,1)} %copy-done.2, bf16[576,1024]{1,0:T(8,128)(2,1)} %eig.1, bf16[72,576]{1,0:T(8,128)(2,1)} %refs_0_.3, bf16[72,576]{1,0:T(8,128)(2,1)} %copy-done.11, ...), custom_call_target="tpu_custom_call" | custom-call | tf_op jit(solution)/shard_map/spread/pallas_call | solution.py:180
  104.4 13.8 %all_to_all.35 = bf16[8,4,72,128]{3,2,1,0:T(8,128)(2,1)S(1)} all-to-all(bf16[8,4,72,128]{3,2,1,0:T(8,128)(2,1)} %spread.1), channel_id=1, replica_groups=mesh['seq'=64,'head'=8] {'head'}, dimensions={0} | all-to-all | bytes 1179648 | tf_op jit(solution)/shard_map/all_to_all | solution.py:301
  118.2 0.1 reduce_sum.63
  118.3 0.8 broadcast_in_dim.61
  119.1 9.7 %all-to-all-start.4 = ((bf16[4,4,72,128]{3,2,1,0:T(8,128)(2,1)}), bf16[4,4,72,128]{3,2,1,0:T(8,128)(2,1)S(1)}, u32[]{:S(2)}, u32[]{:S(2)}) async-start(bf16[4,4,72,128]{3,2,1,0:T(8,128)(2,1)} %broadcast_in_dim.61), calls=%async_computation.4 | async-start | bytes 589824 | tf_op jit(solution)/shard_map/all_to_all | solution.py:304
  128.8 4.3 %collective-permute-start.7 = (bf16[512,128]{1,0:T(8,128)(2,1)S(1)}, bf16[512,128]{1,0:T(8,128)(2,1)S(1)}, u32[]{:S(2)}, u32[]{:S(2)}) collective-permute-start(bf16[512,128]{1,0:T(8,128)(2,1)S(1)} %copy-done.8), channel_id=1, source_target_pairs={{0,64},{8,72},{16,80},{24,88},{32,96},{40,104},{48,112},{56,120},{... | collective-permute-start | bytes 393224 | tf_op jit(solution)/shard_map/ppermute | solution.py:31
  133.0 3.1 %collective-permute-start.8 = (bf16[512,128]{1,0:T(8,128)(2,1)S(1)}, bf16[512,128]{1,0:T(8,128)(2,1)S(1)}, u32[]{:S(2)}, u32[]{:S(2)}) collective-permute-start(bf16[512,128]{1,0:T(8,128)(2,1)S(1)} %copy-done.8), channel_id=1, source_target_pairs={{0,32},{8,40},{16,48},{24,56},{32,64},{40,72},{48,80},{56,88},{64,... | collective-permute-start | bytes 393224 | tf_op jit(solution)/shard_map/ppermute | solution.py:31
  136.2 2.3 %collective-permute-done.8.z1 = bf16[512,128]{1,0:T(8,128)(2,1)S(1)} collective-permute-done((bf16[512,128]{1,0:T(8,128)(2,1)S(1)}, bf16[512,128]{1,0:T(8,128)(2,1)S(1)}, u32[]{:S(2)}, u32[]{:S(2)}) %collective-permute-start.8) | collective-permute-done | bytes 131104 | tf_op jit(solution)/shard_map/ppermute | solution.py:31
  138.4 0.1 select_bitcast_fusion.1
  138.5 3.4 %collective-permute-start.9 = (bf16[2,512,128]{2,1,0:T(8,128)(2,1)S(1)}, bf16[2,512,128]{2,1,0:T(8,128)(2,1)S(1)}, u32[]{:S(2)}, u32[]{:S(2)}) collective-permute-start(bf16[2,512,128]{2,1,0:T(8,128)(2,1)S(1)} %pad_maximum_fusion.1), channel_id=1, source_target_pairs={{0,8},{8,16},{16,24},{24,0},{32,40},{40,48},{48,56},{56,32},{64,72... | collective-permute-start | bytes 786440 | tf_op jit(solution)/shard_map/ppermute | solution.py:37
  141.9 4.3 %collective-permute-start.10 = (bf16[2,512,128]{2,1,0:T(8,128)(2,1)S(1)}, bf16[2,512,128]{2,1,0:T(8,128)(2,1)S(1)}, u32[]{:S(2)}, u32[]{:S(2)}) collective-permute-start(bf16[2,512,128]{2,1,0:T(8,128)(2,1)S(1)} %pad_maximum_fusion.2), channel_id=1, source_target_pairs={{0,16},{8,24},{16,0},{24,8},{32,48},{40,56},{48,32},{56,40},{64,80... | collective-permute-start | bytes 786440 | tf_op jit(solution)/shard_map/ppermute | solution.py:37
  146.3 3.1 %collective-permute-start.11 = (bf16[2,512,128]{2,1,0:T(8,128)(2,1)S(1)}, bf16[2,512,128]{2,1,0:T(8,128)(2,1)S(1)}, u32[]{:S(2)}, u32[]{:S(2)}) collective-permute-start(bf16[2,512,128]{2,1,0:T(8,128)(2,1)S(1)} %pad_maximum_fusion.3), channel_id=1, source_target_pairs={{0,24},{8,0},{16,8},{24,16},{32,56},{40,32},{48,40},{56,48},{64,88... | collective-permute-start | bytes 786440 | tf_op jit(solution)/shard_map/ppermute | solution.py:37
  149.4 1.2 broadcast_in_dim.62
  150.6 3.5 %all-to-all-start.5 = ((bf16[4,4,4,72,128]{4,3,1,2,0:T(8,128)(2,1)}), bf16[4,4,4,72,128]{4,3,1,2,0:T(8,128)(2,1)S(1)}, u32[]{:S(2)}, u32[]{:S(2)}) async-start(bf16[4,4,4,72,128]{4,3,1,2,0:T(8,128)(2,1)} %broadcast_in_dim.62), calls=%async_computation.5 | async-start | bytes 2359296 | tf_op jit(solution)/shard_map/all_to_all | solution.py:306
  154.2 0.0 collective-permute-done.10.p2
  154.2 2.3 %collective-permute-done.11.p3 = bf16[2,512,128]{2,1,0:T(8,128)(2,1)S(1)} collective-permute-done((bf16[2,512,128]{2,1,0:T(8,128)(2,1)S(1)}, bf16[2,512,128]{2,1,0:T(8,128)(2,1)S(1)}, u32[]{:S(2)}, u32[]{:S(2)}) %collective-permute-start.11) | collective-permute-done | bytes 262176 | tf_op jit(solution)/shard_map/ppermute | solution.py:37
  156.5 0.7 copy-done.16
  157.2 6.1 %attend.1 = (bf16[3,512,128]{2,1,0:T(8,128)(2,1)}, bf16[2,512,128]{2,1,0:T(8,128)(2,1)}, bf16[2,512,128]{2,1,0:T(8,128)(2,1)}, bf16[2,512,128]{2,1,0:T(8,128)(2,1)}) custom-call(s32[1]{0:T(128)} %bitcast.12.s_ref, bf16[512,256]{1,0:T(8,128)(2,1)} %q_ref.1, bf16[512,256]{1,0:T(8,128)(2,1)} %a_ref.1, bf16[512,128]{1,0:T(8,128)(2,1)} %copy-done.9, ...), custom_call_target="tpu_custom_call" | custom-call | tf_op jit(solution)/shard_map/attend/pallas_call | solution.py:124
  163.3 5.8 %collective-permute-start.14 = (bf16[2,512,128]{2,1,0:T(8,128)(2,1)}, bf16[2,512,128]{2,1,0:T(8,128)(2,1)S(1)}, u32[]{:S(2)}, u32[]{:S(2)}) collective-permute-start(bf16[2,512,128]{2,1,0:T(8,128)(2,1)} %get-tuple-element.12), channel_id=1, source_target_pairs={{0,8},{8,16},{16,24},{24,0},{32,40},{40,48},{48,56},{56,32},{64,72... | collective-permute-start | bytes 786440 | tf_op jit(solution)/shard_map/ppermute | solution.py:37
  169.2 3.6 %collective-permute-start.13 = (bf16[2,512,128]{2,1,0:T(8,128)(2,1)}, bf16[2,512,128]{2,1,0:T(8,128)(2,1)S(1)}, u32[]{:S(2)}, u32[]{:S(2)}) collective-permute-start(bf16[2,512,128]{2,1,0:T(8,128)(2,1)} %get-tuple-element.11), channel_id=1, source_target_pairs={{0,16},{8,24},{16,0},{24,8},{32,48},{40,56},{48,32},{56,40},{64,80... | collective-permute-start | bytes 786440 | tf_op jit(solution)/shard_map/ppermute | solution.py:37
  172.7 2.7 %collective-permute-start.12 = (bf16[2,512,128]{2,1,0:T(8,128)(2,1)}, bf16[2,512,128]{2,1,0:T(8,128)(2,1)S(1)}, u32[]{:S(2)}, u32[]{:S(2)}) collective-permute-start(bf16[2,512,128]{2,1,0:T(8,128)(2,1)} %get-tuple-element.10), channel_id=1, source_target_pairs={{0,24},{8,0},{16,8},{24,16},{32,56},{40,32},{48,40},{56,48},{64,88... | collective-permute-start | bytes 786440 | tf_op jit(solution)/shard_map/ppermute | solution.py:37
  175.4 1.0 convert_element_type.42
  176.5 3.6 %collective-permute-done.13 = bf16[2,512,128]{2,1,0:T(8,128)(2,1)S(1)} collective-permute-done((bf16[2,512,128]{2,1,0:T(8,128)(2,1)}, bf16[2,512,128]{2,1,0:T(8,128)(2,1)S(1)}, u32[]{:S(2)}, u32[]{:S(2)}) %collective-permute-start.13) | collective-permute-done | bytes 262176 | tf_op jit(solution)/shard_map/ppermute | solution.py:37
  180.1 3.0 %collective-permute-done.12 = bf16[2,512,128]{2,1,0:T(8,128)(2,1)S(1)} collective-permute-done((bf16[2,512,128]{2,1,0:T(8,128)(2,1)}, bf16[2,512,128]{2,1,0:T(8,128)(2,1)S(1)}, u32[]{:S(2)}, u32[]{:S(2)}) %collective-permute-start.12) | collective-permute-done | bytes 262176 | tf_op jit(solution)/shard_map/ppermute | solution.py:37
  183.2 0.1 fusion.14
  183.4 1.3 collective-permute-start.16
  184.7 1.3 collective-permute-start.15
  186.0 0.6 and_add_fusion.i_ref
  186.6 1.2 copy.15
  187.7 6.3 %map_tokens.1 = f32[512,128]{1,0:T(8,128)} custom-call(s32[8]{0:T(128)} %and_add_fusion.i_ref, bf16[8,576,128]{2,1,0:T(8,128)(2,1)} %bitcast.45, bf16[128,128]{1,0:T(8,128)(2,1)} %bitcast.55, bf16[4,576,512]{2,1,0:T(8,128)(2,1)} %collective-permute-done.6.partner, bf16[576,512]{1,0:T(8,128)(2,1)} %bitcast.47, bf16[576,512]{1,0:T(8,128)(2,1)} %copy-done.6, ...), custom_call_target="tpu_custom_call" | custom-call | tf_op jit(solution)/shard_map/map_tokens/pallas_call | solution.py:216
  194.0 6.8 %collective-permute-done.16 = bf16[512,128]{1,0:T(8,128)(2,1)S(1)} collective-permute-done((bf16[512,128]{1,0:T(8,128)(2,1)S(1)}, bf16[512,128]{1,0:T(8,128)(2,1)S(1)}, u32[]{:S(2)}, u32[]{:S(2)}) %collective-permute-start.16) | collective-permute-done | bytes 131104 | tf_op jit(solution)/shard_map/ppermute | solution.py:31
  200.8 1.2 fusion.12
  202.0 11.8 %all_to_all.36 = f32[8,4,128]{2,1,0:T(4,128)S(1)} all-to-all(f32[8,4,128]{2,1,0:T(4,128)S(1)} %broadcast_in_dim.66), channel_id=1, replica_groups=mesh['seq'=64,'head'=8] {'head'}, dimensions={0} | all-to-all | bytes 32768 | tf_op jit(solution)/shard_map/all_to_all | solution.py:329
  213.8 0.6 reduce_sum.65
  (52 shorter events, 0.3 us)
Async XLA Ops:
  0.0 7.4 %copy-start = (bf16[64,576]{1,0:T(8,128)(2,1)S(1)}, bf16[64,576]{1,0:T(8,128)(2,1)}, u32[]{:S(2)}) copy-start(bf16[64,576]{1,0:T(8,128)(2,1)} %param.16) | copy-start | bytes 221188
  0.0 54.0 %copy-start.3 = (bf16[512,576]{0,1:T(8,128)(2,1)S(1)}, bf16[512,576]{0,1:T(8,128)(2,1)}, u32[]{:S(2)}) copy-start(bf16[512,576]{0,1:T(8,128)(2,1)} %param.9) | copy-start | bytes 1769476
  9.4 37.7 %all-to-all-start = ((bf16[8,64,256]{2,1,0:T(8,128)(2,1)}), bf16[8,64,256]{2,1,0:T(8,128)(2,1)S(1)}, u32[]{:S(2)}, u32[]{:S(2)}) async-start(bf16[8,64,256]{2,1,0:T(8,128)(2,1)} %broadcast_in_dim.58), calls=%async_computation | async-start | bytes 524288 | tf_op jit(solution)/shard_map/all_to_all | solution.py:289
  19.5 21.1 %collective-permute-start = (bf16[72,576]{1,0:T(8,128)(2,1)}, bf16[72,576]{1,0:T(8,128)(2,1)S(1)}, u32[]{:S(2)}, u32[]{:S(2)}) collective-permute-start(bf16[72,576]{1,0:T(8,128)(2,1)} %refs_0_.3), channel_id=1, source_target_pairs={{0,384},{8,392},{16,400},{24,408},{32,416},{40,424},{48,432},{56,4... | collective-permute-start | bytes 248840 | tf_op jit(solution)/shard_map/ppermute | solution.py:31
  27.8 15.0 %collective-permute-start.1 = (bf16[72,576]{1,0:T(8,128)(2,1)}, bf16[72,576]{1,0:T(8,128)(2,1)S(1)}, u32[]{:S(2)}, u32[]{:S(2)}) collective-permute-start(bf16[72,576]{1,0:T(8,128)(2,1)} %refs_0_.3), channel_id=1, source_target_pairs={{0,256},{8,264},{16,272},{24,280},{32,288},{40,296},{48,304},{56,3... | collective-permute-start | bytes 248840 | tf_op jit(solution)/shard_map/ppermute | solution.py:31
  32.7 14.4 %collective-permute-start.2 = (bf16[72,576]{1,0:T(8,128)(2,1)}, bf16[72,576]{1,0:T(8,128)(2,1)S(1)}, u32[]{:S(2)}, u32[]{:S(2)}) collective-permute-start(bf16[72,576]{1,0:T(8,128)(2,1)} %refs_0_.3), channel_id=1, source_target_pairs={{0,128},{8,136},{16,144},{24,152},{32,160},{40,168},{48,176},{56,1... | collective-permute-start | bytes 248840 | tf_op jit(solution)/shard_map/ppermute | solution.py:31
  40.6 6.5 %copy-start.11 = (bf16[72,576]{1,0:T(8,128)(2,1)}, bf16[72,576]{1,0:T(8,128)(2,1)S(1)}, u32[]{:S(2)}) copy-start(bf16[72,576]{1,0:T(8,128)(2,1)S(1)} %collective-permute-done.refs_1_) | copy-start | bytes 248836
  42.7 4.4 %copy-start.12 = (bf16[72,576]{1,0:T(8,128)(2,1)}, bf16[72,576]{1,0:T(8,128)(2,1)S(1)}, u32[]{:S(2)}) copy-start(bf16[72,576]{1,0:T(8,128)(2,1)S(1)} %collective-permute-done.1.refs_2_) | copy-start | bytes 248836
  47.1 0.6 copy-start.13
  47.7 0.7 copy-start.2
  50.5 13.1 %all-to-all-start.1 = ((bf16[4,64,576]{2,1,0:T(8,128)(2,1)}), bf16[4,64,576]{2,1,0:T(8,128)(2,1)S(1)}, u32[]{:S(2)}, u32[]{:S(2)}) async-start(bf16[4,64,576]{2,1,0:T(8,128)(2,1)} %rotate_query.1), calls=%async_computation.1 | async-start | bytes 655360 | tf_op jit(solution)/shard_map/all_to_all | solution.py:295
  54.0 20.2 %collective-permute-start.5 = (bf16[576,512]{1,0:T(8,128)(2,1)S(1)}, bf16[576,512]{1,0:T(8,128)(2,1)S(1)}, u32[]{:S(2)}, u32[]{:S(2)}) collective-permute-start(bf16[576,512]{1,0:T(8,128)(2,1)S(1)} %bitcast.48), channel_id=1, source_target_pairs={{0,6},{1,7},{2,0},{3,1},{4,2},{5,3},{6,4},{7,5},{8,14},{9,15},{10,... | collective-permute-start | bytes 1769480 | tf_op jit(solution)/shard_map/ppermute | solution.py:42
  58.6 17.2 %collective-permute-start.4 = (bf16[576,512]{1,0:T(8,128)(2,1)S(1)}, bf16[576,512]{1,0:T(8,128)(2,1)S(1)}, u32[]{:S(2)}, u32[]{:S(2)}) collective-permute-start(bf16[576,512]{1,0:T(8,128)(2,1)S(1)} %bitcast.49), channel_id=1, source_target_pairs={{0,4},{1,5},{2,6},{3,7},{4,0},{5,1},{6,2},{7,3},{8,12},{9,13},{10,... | collective-permute-start | bytes 1769480 | tf_op jit(solution)/shard_map/ppermute | solution.py:42
  61.1 28.8 %collective-permute-start.3 = (bf16[576,512]{1,0:T(8,128)(2,1)S(1)}, bf16[576,512]{1,0:T(8,128)(2,1)S(1)}, u32[]{:S(2)}, u32[]{:S(2)}) collective-permute-start(bf16[576,512]{1,0:T(8,128)(2,1)S(1)} %bitcast.50), channel_id=1, source_target_pairs={{0,2},{1,3},{2,4},{3,5},{4,6},{5,7},{6,0},{7,1},{8,10},{9,11},{10,... | collective-permute-start | bytes 1769480 | tf_op jit(solution)/shard_map/ppermute | solution.py:42
  64.4 31.7 %all-to-all-start.2 = ((bf16[4,64,576]{2,1,0:T(8,128)(2,1)}), bf16[4,64,576]{2,1,0:T(8,128)(2,1)S(1)}, u32[]{:S(2)}, u32[]{:S(2)}) async-start(bf16[4,64,576]{2,1,0:T(8,128)(2,1)} %broadcast_in_dim.60), calls=%async_computation.2 | async-start | bytes 655360 | tf_op jit(solution)/shard_map/all_to_all | solution.py:298
  74.1 17.5 %copy-start.4 = (bf16[576,512]{1,0:T(8,128)(2,1)}, bf16[576,512]{1,0:T(8,128)(2,1)S(1)}, u32[]{:S(2)}) copy-start(bf16[576,512]{1,0:T(8,128)(2,1)S(1)} %collective-permute-done.5.refs_3_) | copy-start | bytes 1769476
  75.8 15.9 %copy-start.5 = (bf16[576,512]{1,0:T(8,128)(2,1)}, bf16[576,512]{1,0:T(8,128)(2,1)S(1)}, u32[]{:S(2)}) copy-start(bf16[576,512]{1,0:T(8,128)(2,1)S(1)} %collective-permute-done.4.refs_2_) | copy-start | bytes 1769476
  89.9 1.8 copy-start.6
  91.7 96.1 %collective-permute-start.6 = (bf16[4,576,512]{2,1,0:T(8,128)(2,1)}, bf16[4,576,512]{2,1,0:T(8,128)(2,1)}, u32[]{:S(2)}, u32[]{:S(2)}) collective-permute-start(bf16[4,576,512]{2,1,0:T(8,128)(2,1)} %pad_maximum_fusion), channel_id=1, source_target_pairs={{0,1},{1,0},{2,3},{3,2},{4,5},{5,4},{6,7},{7,6},{8,9},{9,8},{10,11... | collective-permute-start | bytes 7077896 | tf_op jit(solution)/shard_map/ppermute | solution.py:42
  96.2 0.7 copy-start.7
  96.9 31.9 %copy-start.8 = (bf16[512,128]{1,0:T(8,128)(2,1)S(1)}, bf16[512,128]{1,0:T(8,128)(2,1)}, u32[]{:S(2)}) copy-start(bf16[512,128]{1,0:T(8,128)(2,1)} %z0.1) | copy-start | bytes 393220
  119.1 30.3 %all-to-all-start.4 = ((bf16[4,4,72,128]{3,2,1,0:T(8,128)(2,1)}), bf16[4,4,72,128]{3,2,1,0:T(8,128)(2,1)S(1)}, u32[]{:S(2)}, u32[]{:S(2)}) async-start(bf16[4,4,72,128]{3,2,1,0:T(8,128)(2,1)} %broadcast_in_dim.61), calls=%async_computation.4 | async-start | bytes 589824 | tf_op jit(solution)/shard_map/all_to_all | solution.py:304
  128.8 7.4 %collective-permute-start.7 = (bf16[512,128]{1,0:T(8,128)(2,1)S(1)}, bf16[512,128]{1,0:T(8,128)(2,1)S(1)}, u32[]{:S(2)}, u32[]{:S(2)}) collective-permute-start(bf16[512,128]{1,0:T(8,128)(2,1)S(1)} %copy-done.8), channel_id=1, source_target_pairs={{0,64},{8,72},{16,80},{24,88},{32,96},{40,104},{48,112},{56,120},{... | collective-permute-start | bytes 393224 | tf_op jit(solution)/shard_map/ppermute | solution.py:31
  133.0 5.4 %collective-permute-start.8 = (bf16[512,128]{1,0:T(8,128)(2,1)S(1)}, bf16[512,128]{1,0:T(8,128)(2,1)S(1)}, u32[]{:S(2)}, u32[]{:S(2)}) collective-permute-start(bf16[512,128]{1,0:T(8,128)(2,1)S(1)} %copy-done.8), channel_id=1, source_target_pairs={{0,32},{8,40},{16,48},{24,56},{32,64},{40,72},{48,80},{56,88},{64,... | collective-permute-start | bytes 393224 | tf_op jit(solution)/shard_map/ppermute | solution.py:31
  136.2 14.5 %copy-start.9 = (bf16[512,128]{1,0:T(8,128)(2,1)}, bf16[512,128]{1,0:T(8,128)(2,1)S(1)}, u32[]{:S(2)}) copy-start(bf16[512,128]{1,0:T(8,128)(2,1)S(1)} %collective-permute-done.7.z2) | copy-start | bytes 393220
  138.4 12.2 %copy-start.10 = (bf16[512,128]{1,0:T(8,128)(2,1)}, bf16[512,128]{1,0:T(8,128)(2,1)S(1)}, u32[]{:S(2)}) copy-start(bf16[512,128]{1,0:T(8,128)(2,1)S(1)} %collective-permute-done.8.z1) | copy-start | bytes 393220
  138.5 15.6 %collective-permute-start.9 = (bf16[2,512,128]{2,1,0:T(8,128)(2,1)S(1)}, bf16[2,512,128]{2,1,0:T(8,128)(2,1)S(1)}, u32[]{:S(2)}, u32[]{:S(2)}) collective-permute-start(bf16[2,512,128]{2,1,0:T(8,128)(2,1)S(1)} %pad_maximum_fusion.1), channel_id=1, source_target_pairs={{0,8},{8,16},{16,24},{24,0},{32,40},{40,48},{48,56},{56,32},{64,72... | collective-permute-start | bytes 786440 | tf_op jit(solution)/shard_map/ppermute | solution.py:37
  141.9 12.3 %collective-permute-start.10 = (bf16[2,512,128]{2,1,0:T(8,128)(2,1)S(1)}, bf16[2,512,128]{2,1,0:T(8,128)(2,1)S(1)}, u32[]{:S(2)}, u32[]{:S(2)}) collective-permute-start(bf16[2,512,128]{2,1,0:T(8,128)(2,1)S(1)} %pad_maximum_fusion.2), channel_id=1, source_target_pairs={{0,16},{8,24},{16,0},{24,8},{32,48},{40,56},{48,32},{56,40},{64,80... | collective-permute-start | bytes 786440 | tf_op jit(solution)/shard_map/ppermute | solution.py:37
  146.3 10.2 %collective-permute-start.11 = (bf16[2,512,128]{2,1,0:T(8,128)(2,1)S(1)}, bf16[2,512,128]{2,1,0:T(8,128)(2,1)S(1)}, u32[]{:S(2)}, u32[]{:S(2)}) collective-permute-start(bf16[2,512,128]{2,1,0:T(8,128)(2,1)S(1)} %pad_maximum_fusion.3), channel_id=1, source_target_pairs={{0,24},{8,0},{16,8},{24,16},{32,56},{40,32},{48,40},{56,48},{64,88... | collective-permute-start | bytes 786440 | tf_op jit(solution)/shard_map/ppermute | solution.py:37
  150.6 35.9 %all-to-all-start.5 = ((bf16[4,4,4,72,128]{4,3,1,2,0:T(8,128)(2,1)}), bf16[4,4,4,72,128]{4,3,1,2,0:T(8,128)(2,1)S(1)}, u32[]{:S(2)}, u32[]{:S(2)}) async-start(bf16[4,4,4,72,128]{4,3,1,2,0:T(8,128)(2,1)} %broadcast_in_dim.62), calls=%async_computation.5 | async-start | bytes 2359296 | tf_op jit(solution)/shard_map/all_to_all | solution.py:306
  154.2 2.3 %copy-start.14 = (bf16[2,512,128]{2,1,0:T(8,128)(2,1)}, bf16[2,512,128]{2,1,0:T(8,128)(2,1)S(1)}, u32[]{:S(2)}) copy-start(bf16[2,512,128]{2,1,0:T(8,128)(2,1)S(1)} %collective-permute-done.9.p1) | copy-start | bytes 786436
  154.2 2.3 %copy-start.15 = (bf16[2,512,128]{2,1,0:T(8,128)(2,1)}, bf16[2,512,128]{2,1,0:T(8,128)(2,1)S(1)}, u32[]{:S(2)}) copy-start(bf16[2,512,128]{2,1,0:T(8,128)(2,1)S(1)} %collective-permute-done.10.p2) | copy-start | bytes 786436
  156.5 0.7 copy-start.16
  163.3 13.1 %collective-permute-start.14 = (bf16[2,512,128]{2,1,0:T(8,128)(2,1)}, bf16[2,512,128]{2,1,0:T(8,128)(2,1)S(1)}, u32[]{:S(2)}, u32[]{:S(2)}) collective-permute-start(bf16[2,512,128]{2,1,0:T(8,128)(2,1)} %get-tuple-element.12), channel_id=1, source_target_pairs={{0,8},{8,16},{16,24},{24,0},{32,40},{40,48},{48,56},{56,32},{64,72... | collective-permute-start | bytes 786440 | tf_op jit(solution)/shard_map/ppermute | solution.py:37
  169.2 10.9 %collective-permute-start.13 = (bf16[2,512,128]{2,1,0:T(8,128)(2,1)}, bf16[2,512,128]{2,1,0:T(8,128)(2,1)S(1)}, u32[]{:S(2)}, u32[]{:S(2)}) collective-permute-start(bf16[2,512,128]{2,1,0:T(8,128)(2,1)} %get-tuple-element.11), channel_id=1, source_target_pairs={{0,16},{8,24},{16,0},{24,8},{32,48},{40,56},{48,32},{56,40},{64,80... | collective-permute-start | bytes 786440 | tf_op jit(solution)/shard_map/ppermute | solution.py:37
  172.7 10.4 %collective-permute-start.12 = (bf16[2,512,128]{2,1,0:T(8,128)(2,1)}, bf16[2,512,128]{2,1,0:T(8,128)(2,1)S(1)}, u32[]{:S(2)}, u32[]{:S(2)}) collective-permute-start(bf16[2,512,128]{2,1,0:T(8,128)(2,1)} %get-tuple-element.10), channel_id=1, source_target_pairs={{0,24},{8,0},{16,8},{24,16},{32,56},{40,32},{48,40},{56,48},{64,88... | collective-permute-start | bytes 786440 | tf_op jit(solution)/shard_map/ppermute | solution.py:37
  176.5 6.9 %copy-start.1 = (f32[3,512,128]{2,1,0:T(8,128)}, f32[3,512,128]{2,1,0:T(8,128)S(1)}, u32[]{:S(2)}) copy-start(f32[3,512,128]{2,1,0:T(8,128)S(1)} %convert_element_type.42) | copy-start | bytes 2359300
  183.4 17.4 %collective-permute-start.16 = (bf16[512,128]{1,0:T(8,128)(2,1)S(1)}, bf16[512,128]{1,0:T(8,128)(2,1)S(1)}, u32[]{:S(2)}, u32[]{:S(2)}) collective-permute-start(bf16[512,128]{1,0:T(8,128)(2,1)S(1)} %get-tuple-element.14), channel_id=1, source_target_pairs={{64,0},{72,8},{80,16},{88,24},{96,32},{104,40},{112,48},{120,56},{... | collective-permute-start | bytes 393224 | tf_op jit(solution)/shard_map/ppermute | solution.py:31
  184.7 16.1 %collective-permute-start.15 = (bf16[512,128]{1,0:T(8,128)(2,1)S(1)}, bf16[512,128]{1,0:T(8,128)(2,1)S(1)}, u32[]{:S(2)}, u32[]{:S(2)}) collective-permute-start(bf16[512,128]{1,0:T(8,128)(2,1)S(1)} %get-tuple-element.13), channel_id=1, source_target_pairs={{32,0},{40,8},{48,16},{56,24},{64,32},{72,40},{80,48},{88,56},{96,... | collective-permute-start | bytes 393224 | tf_op jit(solution)/shard_map/ppermute | solution.py:31

commit v2 on v1

v2 whole, which is shorter than its diff:
```python
import functools

import jax
import jax.numpy as jnp
from jax import lax
from jax.experimental import pallas as pl
from jax.experimental.pallas import tpu as pltpu
from jax.sharding import PartitionSpec as P

WINDOW = 4096
SCORE_SCALE = 1.0 / 12.0
SOFT_CAP = 50.0
DAMP_FACTOR = 0.1
LOG2E = 1.4426950408889634
NX = 4
NC = 4
BF = jnp.bfloat16
F32 = jnp.float32
NT = (((1,), (1,)), ((), ()))
INTERPRET = False


def vmem(n):
    return [pl.BlockSpec(memory_space=pltpu.VMEM) for _ in range(n)]


def shift_z(value, by, wrap):
    size = lax.axis_size("seq")
    pairs = [(i, (i + by * NX) % size) for i in range(size) if wrap or 0 <= i + by * NX < size]
    return lax.ppermute(value, "seq", pairs)


def x_groups():
    size = lax.axis_size("seq")
    return [[z * NX + x for x in range(NX)] for z in range(size // NX)]


def c_groups():
    size = lax.axis_size("seq")
    return [
        [(b * NC + c) * NX + x for c in range(NC)]
        for b in range(size // NX // NC)
        for x in range(NX)
    ]


def m_groups():
    size = lax.axis_size("seq")
    n_m = size // NX // NC
    return [[(m * NC + c) * NX + x for m in range(n_m)] for c in range(NC) for x in range(NX)]


def exchange(value, axis, groups=None):
    return lax.all_to_all(value, axis, 0, 0, axis_index_groups=groups)


def copies(value, count):
    return jnp.broadcast_to(value[None], (count,) + value.shape)


def attend_kernel(span, s_ref, q_ref, a_ref, far, near, back, last, kbuf, w, tot, adjt):
    rows, hd = far.shape
    s = s_ref[0]
    x = s & (NX - 1)
    kbuf[span] = far[...]
    for source in range(NX):
        k = (x - source) & (NX - 1)
        kbuf[k + NX] = near[source, 0]
        kbuf[k] = near[source, 1]
    tot[...] = jnp.zeros_like(tot)
    half = rows // 2

    def block(o, mode):
        for piece in range(2):
            lo = piece * half
            keys = kbuf[o, lo : lo + half, :]
            for m in range(2):
                raw = lax.dot_general(
                    keys, q_ref[:, m * hd : (m + 1) * hd], NT, preferred_element_type=F32
                )
                e = jnp.exp2(jnp.tanh(raw * (SCORE_SCALE / SOFT_CAP)) * (SOFT_CAP * LOG2E))
                if mode != 0:
                    key_i = lo + lax.broadcasted_iota(jnp.int32, e.shape, 0)
                    query_i = lax.broadcasted_iota(jnp.int32, e.shape, 1)
                    keep = key_i <= query_i if mode < 0 else key_i > query_i
                    e = jnp.where(keep, e, 0.0)
                tot[m] += jnp.sum(e.reshape(half // 8, 8, rows), axis=0)
                w[o, lo : lo + half, m * rows : (m + 1) * rows] = e.astype(BF)

    block(0, -1)

    def step(o, carry):
        block(o, 0)
        return carry

    lax.fori_loop(1, jnp.minimum(s, span - 1) + 1, step, 0)

    @pl.when(s >= span)
    def _():
        block(span, 1)

    @pl.when(s < span)
    def _():
        def clear(o, carry):
            w[o] = jnp.zeros(w.shape[1:], BF)
            return carry

        lax.fori_loop(s + 1, span + 1, clear, 0)

    for m in range(2):
        inv = 1.0 / jnp.sum(tot[m], axis=0, keepdims=True)
        turned = a_ref[:, m * hd : (m + 1) * hd].astype(F32).T
        adjt[:, m * rows : (m + 1) * rows] = (turned * inv).astype(BF)
    for o in range(span + 1):
        piece = lax.dot_general(w[o], adjt[...], NT, preferred_element_type=F32).astype(BF)
        if o == span:
            last[...] = piece
        else:
            back[(x - o) & (NX - 1), 1 - o // NX] = piece


def attend(s, q, a, far, near, span):
    rows, hd = far.shape
    return pl.pallas_call(
        functools.partial(attend_kernel, span),
        out_shape=(jax.ShapeDtypeStruct(near.shape, BF), jax.ShapeDtypeStruct(far.shape, BF)),
        in_specs=[pl.BlockSpec(memory_space=pltpu.SMEM)] + vmem(4),
        out_specs=tuple(vmem(2)),
        scratch_shapes=[
            pltpu.VMEM((span + 1, rows, hd), BF),
            pltpu.VMEM((span + 1, rows, 2 * rows), BF),
            pltpu.VMEM((2, 8, rows), F32),
            pltpu.VMEM((hd, 2 * rows), BF),
        ],
        interpret=INTERPRET,
        name="attend",
    )(s, q, a, far, near)


def pack_kernel(at_ref, act, adj, bg, eig, out):
    lq, hd = adj.shape
    heads = out.shape[0]
    kr = act.shape[1] // heads
    turned = jnp.dot(adj[...], bg[...], preferred_element_type=F32).astype(BF)
    total = jnp.sum(jnp.sum(eig[...].astype(F32), axis=0, keepdims=True), axis=1, keepdims=True)
    high = total.astype(BF).astype(F32)
    mid = (total - high).astype(BF).astype(F32)
    low = total - high - mid
    lane = lax.broadcasted_iota(jnp.int32, (lq, hd - kr), 1)
    tail = jnp.where(lane == 0, high, jnp.where(lane == 1, mid, jnp.where(lane == 2, low, 0.0)))
    out[0, :, :hd] = turned
    out[0, :, hd + kr :] = tail.astype(BF)
    for i in range(heads):

        @pl.when(at_ref[0] == i)
        def _():
            out[0, :, hd : hd + kr] = act[:, i * kr : (i + 1) * kr]

    for i in range(1, heads):
        out[i] = out[0]


def pack_query(at, act, adj, bg, eig, heads):
    lq, hd = adj.shape
    return pl.pallas_call(
        pack_kernel,
        out_shape=jax.ShapeDtypeStruct((heads, lq, 2 * hd), BF),
        in_specs=[pl.BlockSpec(memory_space=pltpu.SMEM)] + vmem(4),
        out_specs=vmem(1)[0],
        interpret=INTERPRET,
        name="pack_query",
    )(at, act, adj, bg, eig)


def rotate_query_kernel(hd, c_ref, pack, basis, out):
    kr = basis.shape[1]
    acc = None
    for m in range(basis.shape[0]):
        chunk = pack[2 * m + (c_ref[0] >> 1)][:, hd : hd + kr]
        term = jnp.dot(chunk, basis[m], preferred_element_type=F32)
        acc = term if acc is None else acc + term
    acc = acc.astype(BF)
    for i in range(out.shape[0]):
        out[i] = acc


def rotate_query(c, pack, basis, hd):
    return pl.pallas_call(
        functools.partial(rotate_query_kernel, hd),
        out_shape=jax.ShapeDtypeStruct((NX, pack.shape[1], basis.shape[2]), BF),
        in_specs=[pl.BlockSpec(memory_space=pltpu.SMEM)] + vmem(2),
        out_specs=vmem(1)[0],
        interpret=INTERPRET,
        name="rotate_query",
    )(c, pack, basis)


def spread_kernel(count, rq, pack, eig, basis, out, rq_t):
    hd = eig.shape[1]
    kr = basis.shape[1]
    g = pl.program_id(0)

    @pl.when(g == 0)
    def _():
        total = rq[0].astype(F32)
        for i in range(1, rq.shape[0]):
            total = total + rq[i].astype(F32)
        rq_t[...] = total.T.astype(BF)

    sums = pack[:, 0:1, hd + kr : hd + kr + 3].astype(F32)
    damping = jnp.sum(jnp.sum(sums, axis=0), axis=1, keepdims=True) * (DAMP_FACTOR / count)
    turned = pack[g][:, :hd]
    grad = jnp.dot(rq_t[...], turned, preferred_element_type=F32) * (1.0 / rq.shape[1])
    scaled = (grad / (eig[...].astype(F32) + damping)).astype(BF)
    for m in range(basis.shape[0]):
        out[0, m] = jnp.dot(basis[m], scaled, preferred_element_type=F32).astype(BF)


def spread(count, rq, pack, eig, basis, hd):
    heads = pack.shape[0]
    n_m, rows, cols = basis.shape
    return pl.pallas_call(
        functools.partial(spread_kernel, count),
        grid=(heads,),
        out_shape=jax.ShapeDtypeStruct((heads, n_m, rows, hd), BF),
        in_specs=[
            pl.BlockSpec(rq.shape, lambda g: (0, 0, 0)),
            pl.BlockSpec(pack.shape, lambda g: (0, 0, 0)),
            pl.BlockSpec((cols, hd), lambda g: (0, g)),
            pl.BlockSpec(basis.shape, lambda g: (0, 0, 0)),
        ],
        out_specs=pl.BlockSpec((1, n_m, rows, hd), lambda g: (g, 0, 0, 0)),
        scratch_shapes=[pltpu.VMEM((cols, rq.shape[1]), BF)],
        interpret=INTERPRET,
        name="spread",
    )(rq, pack, eig, basis)


def map_tokens_kernel(core_ref, n_ref, bg_ref, mine, partner, out, n_t):
    @pl.when(pl.program_id(0) == 0)
    def _():
        for g in range(n_ref.shape[0]):
            n_t[g] = n_ref[g].T

    acc = None
    for y in range(mine.shape[0]):
        for core, ref in ((core_ref[0], mine), (1 - core_ref[0], partner)):
            term = jnp.dot(n_t[2 * y + core], ref[y], preferred_element_type=F32)
            acc = term if acc is None else acc + term
    turned = jnp.dot(bg_ref[...], acc.astype(BF), preferred_element_type=F32)
    out[...] = turned.T


def map_tokens(core, n8, bg, mine, partner):
    n_y, cols, rows = mine.shape
    hd = bg.shape[0]
    steps = 4 if rows % 512 == 0 else 1
    tile = rows // steps
    return pl.pallas_call(
        map_tokens_kernel,
        grid=(steps,),
        out_shape=jax.ShapeDtypeStruct((rows, hd), F32),
        in_specs=[
            pl.BlockSpec(memory_space=pltpu.SMEM),
            pl.BlockSpec(n8.shape, lambda g: (0, 0, 0)),
            pl.BlockSpec(bg.shape, lambda g: (0, 0)),
            pl.BlockSpec((n_y, cols, tile), lambda g: (0, 0, g)),
            pl.BlockSpec((n_y, cols, tile), lambda g: (0, 0, g)),
        ],
        out_specs=pl.BlockSpec((tile, hd), lambda g: (g, 0)),
        scratch_shapes=[pltpu.VMEM((n8.shape[0], hd, cols), BF)],
        interpret=INTERPRET,
        name="map_tokens",
    )(core, n8, bg, mine, partner)


def on_device(
    act, query_rows, key_rows, out_adjoint, basis_input, basis_grad, eigvals, query_act, query_adj
):
    rows, cols = act.shape
    hd = basis_grad.shape[1]
    heads = lax.axis_size("head")
    n_m = lax.axis_size("seq") // NX // NC
    kr = basis_input.shape[0]
    span = WINDOW // rows
    s = lax.axis_index("seq")
    x = s & (NX - 1)
    c = (s >> 2) & (NC - 1)
    core = lax.axis_index("head") & 1
    ahead = jnp.arange(NX, dtype=jnp.int32) >= x

    key_1 = shift_z(key_rows, 1, False)
    key_2 = shift_z(key_rows, 2, False)
    basis = exchange(copies(basis_input, n_m), "seq", m_groups())
    at = (c & 1) * NX + x
    pack = pack_query(at[None], query_act, query_adj, basis_grad[0], eigvals, heads)
    pack = exchange(pack, "head")
    act_y = copies(act.T, heads // 2)
    act_y = exchange(act_y, "head", [list(range(k, heads, 2)) for k in range(2)])

    keys = jnp.where(
        ahead[:, None, None, None],
        jnp.stack([key_1, key_rows])[None],
        jnp.stack([key_2, key_1])[None],
    )
    keys, pack, basis = lax.optimization_barrier((keys, pack, basis))
    keys = exchange(keys, "seq", x_groups())
    rq = rotate_query(c[None], pack, basis, hd)
    rq = exchange(rq, "seq", x_groups())
    rq = copies(jnp.sum(rq.astype(F32), axis=0).astype(BF), NC)
    keys, rq = lax.optimization_barrier((keys, rq))

    rq = exchange(rq, "seq", c_groups())
    back, far = attend(s[None], query_rows, out_adjoint, key_2, keys, span)
    back, far, rq, act_y = lax.optimization_barrier((back, far, rq, act_y))

    back = exchange(back, "seq", x_groups())
    n = spread(float(cols * heads * eigvals.shape[1]), rq, pack, eigvals, basis, hd)
    n = exchange(n, "head")
    partner = lax.ppermute(act_y, "head", [(i, i ^ 1) for i in range(heads)])
    back = back.astype(F32)
    sum_0, sum_1, sum_2 = 0.0, 0.0, far.astype(F32)
    for source in range(NX):
        later = ahead[source]
        sum_0 = sum_0 + jnp.where(later, back[source, 1], 0.0)
        sum_1 = sum_1 + jnp.where(later, back[source, 0], back[source, 1])
        sum_2 = sum_2 + jnp.where(later, 0.0, back[source, 0])
    n = copies(jnp.sum(n.astype(F32), axis=0).astype(BF), NC)
    sum_0, sum_1, sum_2, n = lax.optimization_barrier(
        (sum_0, sum_1.astype(BF), sum_2.astype(BF), n)
    )

    got_1 = shift_z(sum_1, -1, False)
    got_2 = shift_z(sum_2, -2, False)
    n = copies(exchange(n, "seq", c_groups()), NX)
    n = exchange(n, "seq", x_groups())
    n = n.transpose(2, 1, 0, 3, 4).reshape(heads, cols, hd)
    mapped = map_tokens(core[None], n, basis_grad[0], act_y, partner)
    value_adjoint = sum_0 + got_1.astype(F32) + got_2.astype(F32)
    partial = jnp.sum(mapped * value_adjoint, axis=1)
    partial = exchange(copies(partial.reshape(rows // 128, 128), heads), "head")
    return jnp.sum(partial, axis=0).reshape(rows)


def solution(mesh):
    return jax.shard_map(
        on_device,
        mesh=mesh,
        in_specs=(
            P("seq", "head"),
            P("seq", "head"),
            P("seq", "head"),
            P("seq", "head"),
            P("seq", "head"),
            P("head", None, None),
            P("head", None),
            P(None, "head"),
            P(None, "head"),
        ),
        out_specs=P("seq"),
        check_vma=False,
    )
```

time: 219 us -> 236 us (1.078); the launches traced: 214 us -> 234 us
  blocking collectives: 25.6 us -> 89.3 us
  starting transfers between devices: 102 us -> 49.8 us
  waiting for transfers between devices: 40.3 us -> 51.9 us
  between operations: 5.93 us -> 0.18 us
  Pallas kernels: 22 us -> 24.6 us
    all_to_all x2 -> x6, blocking collectives: 25.6 us -> 89.3 us  [exchange(): return lax.all_to_all(value, axis, 0, 0, axis_index_groups=groups)]
    all_to_all x5, waiting for transfers between devices: 0.01 us -> 37.4 us  [exchange(): return lax.all_to_all(value, axis, 0, 0, axis_index_groups=groups)]
    ppermute x10 -> x1, starting transfers between devices: 34.8 us -> 2.66 us  [on_device(): partner = lax.ppermute(act_y, 'head', [(i, i ^ 1) for i in range(heads)])]
    ppermute x10 -> x1, waiting for transfers between devices: 24.7 us -> 0.01 us  [on_device(): partner = lax.ppermute(act_y, 'head', [(i, i ^ 1) for i in range(heads)])]
    ppermute x7 -> x4, starting transfers between devices: 30.4 us -> 8.4 us  [shift_z(): return lax.ppermute(value, 'seq', pairs)]
    reduce_sum x4 -> x2, other arithmetic: 4.11 us -> 1.2 us  [the longest x1 1.15 us: on_device(): n = copies(jnp.sum(n.astype(F32), axis=0).astype(BF), NC)]
    add x2 -> x1, other arithmetic: 0.72 us -> 3.38 us  [on_device(): sum_1 = sum_1 + jnp.where(later, back[source, 0], back[source, 1])]
    pallas_call x1 -> x2, Pallas kernels: 7.56 us -> 9.93 us  [the longest x1 7.44 us: spread(): pl.pallas_call(functools.partial(spread_kernel, count), grid=(heads,), ou...]
  transfers between devices with their start and end apart: 22 -> 10, of which waited for: 9 -> 5; matrix products, arithmetic and copies ran while one was open for 5% -> 5% of each run, Pallas kernels for 9% -> 5%
where the time goes in v2:
time: 236 us; the launch traced here: 234 us
  blocking collectives  89.3 us (38%)
  waiting for transfers between devices  51.9 us (22%)
  starting transfers between devices  49.8 us (21%)
  Pallas kernels  24.6 us (10%)
  other arithmetic  9.98 us (4%)
  local copies, waits for them, and re-layouts  8.44 us (4%)
    all_to_all x6, blocking collectives, exchange(): return lax.all_to_all(value, axis, 0, 0, axis_index_groups=groups)  89.3 us
    all_to_all x5, starting transfers between devices, exchange(): return lax.all_to_all(value, axis, 0, 0, axis_index_groups=groups)  38.7 us
    all_to_all x5, waiting for transfers between devices, exchange(): return lax.all_to_all(value, axis, 0, 0, axis_index_groups=groups)  37.4 us
    ppermute x4, waiting for transfers between devices, shift_z(): return lax.ppermute(value, 'seq', pairs)  14.5 us
    ppermute x4, starting transfers between devices, shift_z(): return lax.ppermute(value, 'seq', pairs)  8.4 us
    pallas_call x1, Pallas kernels, spread(): pl.pallas_call(functools.partial(spread_kernel, count), grid=(heads,), ou...  7.44 us
    pallas_call x1, Pallas kernels, attend(): pl.pallas_call(functools.partial(attend_kernel, span), out_shape=(jax.Sha...  6.36 us
    pallas_call x1, Pallas kernels, map_tokens(): pl.pallas_call(map_tokens_kernel, grid=(steps,), out_shape=jax.ShapeDtype...  6.3 us
  transfers between devices with their start and end apart: 10, of which 5 were waited for; matrix products, arithmetic and copies ran while one was open for 5% of the time, Pallas kernels for 5%

profile of v2, /device:TPU:1, one launch (start us, length us, event | category | flops | bytes accessed | tf_op | source)
XLA Modules:
  0.0 234.2 jit_solution(7656400680870580792)
XLA Ops:
  0.0 0.0 copy-start.8
  0.0 0.0 copy-start.6
  0.0 2.5 %pack_query.1 = bf16[8,64,256]{2,1,0:T(8,128)(2,1)} custom-call(s32[1]{0:T(128)} %bitcast.6.at_ref, bf16[64,576]{1,0:T(8,128)(2,1)} %act.1, bf16[64,128]{1,0:T(8,128)(2,1)} %adj.1, bf16[128,128]{1,0:T(8,128)(2,1)} %bitcast.41, bf16[576,1024]{1,0:T(8,128)(2,1)} %eig.3), custom_call_target="tpu_custom_call" | custom-call | tf_op jit(solution)/shard_map/pack_query/pallas_call | solution.py:165
  2.5 17.3 %all_to_all.55.pack = bf16[8,64,256]{2,1,0:T(8,128)(2,1)} all-to-all(bf16[8,64,256]{2,1,0:T(8,128)(2,1)} %pack_query.1), channel_id=1, replica_groups=mesh['seq'=64,'head'=8] {'head'}, dimensions={0} | all-to-all | bytes 524288 | tf_op jit(solution)/shard_map/all_to_all | solution.py:54
  19.8 0.0 copy-done.8
  19.8 0.8 broadcast_in_dim.94
  20.6 10.0 %all-to-all-start.1 = ((bf16[4,72,576]{2,1,0:T(8,128)(2,1)}), bf16[4,72,576]{2,1,0:T(8,128)(2,1)S(1)}, u32[]{:S(2)}, u32[]{:S(2)}) async-start(bf16[4,72,576]{2,1,0:T(8,128)(2,1)} %broadcast_in_dim.94), calls=%async_computation.1 | async-start | bytes 737280 | tf_op jit(solution)/shard_map/all_to_all | solution.py:54
  30.6 0.0 copy-done.6
  30.6 3.1 %collective-permute-start = (bf16[512,128]{1,0:T(8,128)(2,1)S(1)}, bf16[512,128]{1,0:T(8,128)(2,1)S(1)}, u32[]{:S(2)}, u32[]{:S(2)}) collective-permute-start(bf16[512,128]{1,0:T(8,128)(2,1)S(1)} %copy-done.6), channel_id=1, source_target_pairs={{0,64},{8,72},{16,80},{24,88},{32,96},{40,104},{48,112},{56,120},{... | collective-permute-start | bytes 393224 | tf_op jit(solution)/shard_map/ppermute | solution.py:30
  33.7 2.7 %collective-permute-start.1 = (bf16[512,128]{1,0:T(8,128)(2,1)S(1)}, bf16[512,128]{1,0:T(8,128)(2,1)S(1)}, u32[]{:S(2)}, u32[]{:S(2)}) collective-permute-start(bf16[512,128]{1,0:T(8,128)(2,1)S(1)} %copy-done.6), channel_id=1, source_target_pairs={{0,32},{8,40},{16,48},{24,56},{32,64},{40,72},{48,80},{56,88},{64,... | collective-permute-start | bytes 393224 | tf_op jit(solution)/shard_map/ppermute | solution.py:30
  36.5 3.0 %collective-permute-done.far = bf16[512,128]{1,0:T(8,128)(2,1)S(1)} collective-permute-done((bf16[512,128]{1,0:T(8,128)(2,1)S(1)}, bf16[512,128]{1,0:T(8,128)(2,1)S(1)}, u32[]{:S(2)}, u32[]{:S(2)}) %collective-permute-start) | collective-permute-done | bytes 131104 | tf_op jit(solution)/shard_map/ppermute | solution.py:30
  39.4 0.0 copy-start.5
  39.4 11.5 %collective-permute-done.1 = bf16[512,128]{1,0:T(8,128)(2,1)S(1)} collective-permute-done((bf16[512,128]{1,0:T(8,128)(2,1)S(1)}, bf16[512,128]{1,0:T(8,128)(2,1)S(1)}, u32[]{:S(2)}, u32[]{:S(2)}) %collective-permute-start.1) | collective-permute-done | bytes 131104 | tf_op jit(solution)/shard_map/ppermute | solution.py:30
  51.0 0.2 broadcast_select_fusion
  51.2 0.0 copy-start.4
  51.2 0.0 all-to-all-done.1.basis
  51.2 0.0 copy-start.1
  51.2 0.7 copy-done.1
  51.9 2.0 rotate_query.1
  54.0 10.1 %all_to_all.56 = bf16[4,64,576]{2,1,0:T(8,128)(2,1)S(1)} all-to-all(bf16[4,64,576]{2,1,0:T(8,128)(2,1)} %rotate_query.1), channel_id=1, replica_groups={{0,8,16,24},{32,40,48,56},{64,72,80,88},{96,104,112,120},{128,136,144,1..., dimensions={0} | all-to-all | bytes 589824 | tf_op jit(solution)/shard_map/all_to_all | solution.py:54
  64.1 14.6 %all_to_all.57.near = bf16[4,2,512,128]{3,2,1,0:T(8,128)(2,1)} all-to-all(bf16[4,2,512,128]{3,2,1,0:T(8,128)(2,1)S(1)} %broadcast_select_fusion), channel_id=1, replica_groups={{0,8,16,24},{32,40,48,56},{64,72,80,88},{96,104,112,120},{128,136,144,1..., dimensions={0} | all-to-all | bytes 2097152 | tf_op jit(solution)/shard_map/all_to_all | solution.py:54
  78.7 0.0 copy-done.5
  78.7 0.0 copy-done.4
  78.7 1.6 broadcast_in_dim.97
  80.3 3.6 %all-to-all-start.5 = ((bf16[4,576,512]{2,1,0:T(8,128)(2,1)}), bf16[4,576,512]{2,1,0:T(8,128)(2,1)S(1)}, u32[]{:S(2)}, u32[]{:S(2)}) async-start(bf16[4,576,512]{2,1,0:T(8,128)(2,1)} %broadcast_in_dim.97), calls=%async_computation.5 | async-start | bytes 4718592 | tf_op jit(solution)/shard_map/all_to_all | solution.py:54
  84.0 0.1 reduce_sum.42
  84.0 0.7 broadcast_in_dim.96
  84.8 16.9 %all-to-all-done.5.mine = bf16[4,576,512]{2,1,0:T(8,128)(2,1)S(1)} async-done(((bf16[4,576,512]{2,1,0:T(8,128)(2,1)}), bf16[4,576,512]{2,1,0:T(8,128)(2,1)S(1)}, u32[]{:S(2)}, u32[]{:S(2)}) %all-to-all-start.5) | async-done | bytes 2359328 | tf_op jit(solution)/shard_map/all_to_all | solution.py:54
  101.6 0.0 copy-start
  101.6 18.0 %all-to-all-start.4 = ((bf16[4,64,576]{2,1,0:T(8,128)(2,1)}), bf16[4,64,576]{2,1,0:T(8,128)(2,1)S(1)}, u32[]{:S(2)}, u32[]{:S(2)}) async-start(bf16[4,64,576]{2,1,0:T(8,128)(2,1)} %broadcast_in_dim.96), calls=%async_computation.4 | async-start | bytes 655360 | tf_op jit(solution)/shard_map/all_to_all | solution.py:54
  119.7 6.4 %attend.1 = (bf16[4,2,512,128]{3,2,1,0:T(8,128)(2,1)}, bf16[512,128]{1,0:T(8,128)(2,1)}) custom-call(s32[1]{0:T(128)} %bitcast.2.s_ref, bf16[512,256]{1,0:T(8,128)(2,1)} %q_ref.1, bf16[512,256]{1,0:T(8,128)(2,1)} %a_ref.1, bf16[512,128]{1,0:T(8,128)(2,1)} %copy-done.5, bf16[4,2,512,128]{3,2,1,0:T(8,128)(2,1)} %all_to_all.57.near), custom_call_target="tpu_custom_call" | custom-call | tf_op jit(solution)/shard_map/attend/pallas_call | solution.py:124
  126.0 0.0 all-to-all-done.4.rq
  126.0 0.0 copy-start.2
  126.0 0.7 copy-done.2
  126.8 7.4 %spread.1 = bf16[8,4,72,128]{3,2,1,0:T(8,128)(2,1)} custom-call(bf16[4,64,576]{2,1,0:T(8,128)(2,1)} %copy-done.2, bf16[8,64,256]{2,1,0:T(8,128)(2,1)} %all_to_all.55.pack, bf16[576,1024]{1,0:T(8,128)(2,1)} %eig.3, bf16[4,72,576]{2,1,0:T(8,128)(2,1)} %copy-done.1), custom_call_target="tpu_custom_call" | custom-call | tf_op jit(solution)/shard_map/spread/pallas_call | solution.py:222
  134.2 19.8 %all_to_all.58 = bf16[8,4,72,128]{3,2,1,0:T(8,128)(2,1)} all-to-all(bf16[8,4,72,128]{3,2,1,0:T(8,128)(2,1)} %spread.1), channel_id=1, replica_groups=mesh['seq'=64,'head'=8] {'head'}, dimensions={0} | all-to-all | bytes 1179648 | tf_op jit(solution)/shard_map/all_to_all | solution.py:54
  154.0 3.5 %all-to-all-start.6 = ((bf16[4,2,512,128]{3,2,1,0:T(8,128)(2,1)}), bf16[4,2,512,128]{3,2,1,0:T(8,128)(2,1)S(1)}, u32[]{:S(2)}, u32[]{:S(2)}) async-start(bf16[4,2,512,128]{3,2,1,0:T(8,128)(2,1)} %get-tuple-element.27), calls=%async_computation.6 | async-start | bytes 2097152 | tf_op jit(solution)/shard_map/all_to_all | solution.py:54
  157.5 0.0 copy-done
  157.5 2.7 %collective-permute-start.2 = (bf16[4,576,512]{2,1,0:T(8,128)(2,1)S(1)}, bf16[4,576,512]{2,1,0:T(8,128)(2,1)}, u32[]{:S(2)}, u32[]{:S(2)}) collective-permute-start(bf16[4,576,512]{2,1,0:T(8,128)(2,1)S(1)} %all-to-all-done.5.mine), channel_id=1, source_target_pairs={{0,1},{1,0},{2,3},{3,2},{4,5},{5,4},{6,7},{7,6},{8,9},{9,8},{10,11... | collective-permute-start | bytes 7077896 | tf_op jit(solution)/shard_map/ppermute | solution.py:320
  160.2 0.7 fusion.2
  160.9 1.1 reduce_sum.43
  162.0 9.9 %all-to-all-done.6 = bf16[4,2,512,128]{3,2,1,0:T(8,128)(2,1)S(1)} async-done(((bf16[4,2,512,128]{3,2,1,0:T(8,128)(2,1)}), bf16[4,2,512,128]{3,2,1,0:T(8,128)(2,1)S(1)}, u32[]{:S(2)}, u32[]{:S(2)}) %all-to-all-start.6) | async-done | bytes 1048608 | tf_op jit(solution)/shard_map/all_to_all | solution.py:54
  171.9 0.0 copy-start.7
  171.9 0.1 convert_element_type.20
  172.1 0.8 copy-done.7
  172.9 3.3 %fusion = bf16[512,128]{1,0:T(8,128)(2,1)} fusion(bf16[512,128]{1,0:T(8,128)(2,1)S(1)} %copy-done.7, f32[4,2,512,128]{3,2,1,0:T(8,128)S(1)} %convert_element_type.20, pred[]{:T(512)} %bitcast.12, pred[]{:T(512)} %bitcast.11, pred[]{:T(512)} %bitcast.10, pred[]{:T(512)} %bitcast.1), kind=kLoop, calls=%fused_computation.4 | loop fusion | flops 655360 | bytes 1310724 | tf_op jit(solution)/shard_map/convert_element_type | solution.py:330
  176.1 3.4 %fusion.1 = (bf16[512,128]{1,0:T(8,128)(2,1)}, f32[512,128]{1,0:T(8,128)}) fusion(f32[4,2,512,128]{3,2,1,0:T(8,128)S(1)} %convert_element_type.20, pred[]{:T(512)} %bitcast.12, pred[]{:T(512)} %bitcast.11, pred[]{:T(512)} %bitcast.10, pred[]{:T(512)} %bitcast.1), kind=kLoop, calls=%fused_computation.11 | loop fusion | flops 983040 | bytes 2490372 | tf_op jit(solution)/shard_map/add | solution.py:326
  179.5 16.2 %all_to_all.59 = bf16[4,4,72,128]{3,2,1,0:T(8,128)(2,1)S(1)} all-to-all(bf16[4,4,72,128]{3,2,1,0:T(8,128)(2,1)S(1)} %broadcast_in_dim.99), channel_id=1, replica_groups={{0,32,64,96},{8,40,72,104},{16,48,80,112},{24,56,88,120},{128,160,192,2..., dimensions={0} | all-to-all | bytes 589824 | tf_op jit(solution)/shard_map/all_to_all | solution.py:54
  195.8 1.2 broadcast_in_dim.100
  197.0 3.5 %all-to-all-start.9 = ((bf16[4,4,4,72,128]{4,3,1,2,0:T(8,128)(2,1)}), bf16[4,4,4,72,128]{4,3,1,2,0:T(8,128)(2,1)S(1)}, u32[]{:S(2)}, u32[]{:S(2)}) async-start(bf16[4,4,4,72,128]{4,3,1,2,0:T(8,128)(2,1)} %broadcast_in_dim.100), calls=%async_computation.9 | async-start | bytes 2359296 | tf_op jit(solution)/shard_map/all_to_all | solution.py:54
  200.5 1.3 collective-permute-start.3
  201.8 1.3 collective-permute-start.4
  203.1 10.6 %all-to-all-done.9 = bf16[4,4,4,72,128]{4,3,1,2,0:T(8,128)(2,1)S(1)} async-done(((bf16[4,4,4,72,128]{4,3,1,2,0:T(8,128)(2,1)}), bf16[4,4,4,72,128]{4,3,1,2,0:T(8,128)(2,1)S(1)}, u32[]{:S(2)}, u32[]{:S(2)}) %all-to-all-start.9) | async-done | bytes 1179680 | tf_op jit(solution)/shard_map/all_to_all | solution.py:54
  213.7 1.1 copy.15
  214.8 0.0 collective-permute-done.2.partner
  214.8 0.0 copy-start.3
  214.8 6.3 %map_tokens.1 = f32[512,128]{1,0:T(8,128)} custom-call(s32[1]{0:T(128)} %bitcast.core_ref, bf16[8,576,128]{2,1,0:T(8,128)(2,1)} %bitcast.37, bf16[128,128]{1,0:T(8,128)(2,1)} %bitcast.42, bf16[4,576,512]{2,1,0:T(8,128)(2,1)} %copy-done, bf16[4,576,512]{2,1,0:T(8,128)(2,1)} %collective-permute-done.2.partner), custom_call_target="tpu_custom_call" | custom-call | tf_op jit(solution)/shard_map/map_tokens/pallas_call | solution.py:259
  221.1 0.0 collective-permute-done.3
  221.1 0.0 collective-permute-done.4
  221.1 0.0 copy-done.3
  221.1 1.2 multiply_reduce_fusion
  222.3 11.3 %all_to_all.60 = f32[8,4,128]{2,1,0:T(4,128)S(1)} all-to-all(f32[8,4,128]{2,1,0:T(4,128)S(1)} %broadcast_in_dim.102), channel_id=1, replica_groups=mesh['seq'=64,'head'=8] {'head'}, dimensions={0} | all-to-all | bytes 32768 | tf_op jit(solution)/shard_map/all_to_all | solution.py:54
  233.6 0.6 reduce_sum.45
  (5 shorter events, 0.1 us)
Async XLA Ops:
  0.0 19.8 %copy-start.8 = (bf16[72,576]{1,0:T(8,128)(2,1)S(1)}, bf16[72,576]{1,0:T(8,128)(2,1)}, u32[]{:S(2)}) copy-start(bf16[72,576]{1,0:T(8,128)(2,1)} %param.13) | copy-start | bytes 248836
  0.0 30.6 %copy-start.6 = (bf16[512,128]{1,0:T(8,128)(2,1)S(1)}, bf16[512,128]{1,0:T(8,128)(2,1)}, u32[]{:S(2)}) copy-start(bf16[512,128]{1,0:T(8,128)(2,1)} %param.11) | copy-start | bytes 393220
  20.6 30.6 %all-to-all-start.1 = ((bf16[4,72,576]{2,1,0:T(8,128)(2,1)}), bf16[4,72,576]{2,1,0:T(8,128)(2,1)S(1)}, u32[]{:S(2)}, u32[]{:S(2)}) async-start(bf16[4,72,576]{2,1,0:T(8,128)(2,1)} %broadcast_in_dim.94), calls=%async_computation.1 | async-start | bytes 737280 | tf_op jit(solution)/shard_map/all_to_all | solution.py:54
  30.6 8.8 %collective-permute-start = (bf16[512,128]{1,0:T(8,128)(2,1)S(1)}, bf16[512,128]{1,0:T(8,128)(2,1)S(1)}, u32[]{:S(2)}, u32[]{:S(2)}) collective-permute-start(bf16[512,128]{1,0:T(8,128)(2,1)S(1)} %copy-done.6), channel_id=1, source_target_pairs={{0,64},{8,72},{16,80},{24,88},{32,96},{40,104},{48,112},{56,120},{... | collective-permute-start | bytes 393224 | tf_op jit(solution)/shard_map/ppermute | solution.py:30
  33.7 17.3 %collective-permute-start.1 = (bf16[512,128]{1,0:T(8,128)(2,1)S(1)}, bf16[512,128]{1,0:T(8,128)(2,1)S(1)}, u32[]{:S(2)}, u32[]{:S(2)}) collective-permute-start(bf16[512,128]{1,0:T(8,128)(2,1)S(1)} %copy-done.6), channel_id=1, source_target_pairs={{0,32},{8,40},{16,48},{24,56},{32,64},{40,72},{48,80},{56,88},{64,... | collective-permute-start | bytes 393224 | tf_op jit(solution)/shard_map/ppermute | solution.py:30
  39.4 39.3 %copy-start.5 = (bf16[512,128]{1,0:T(8,128)(2,1)}, bf16[512,128]{1,0:T(8,128)(2,1)S(1)}, u32[]{:S(2)}) copy-start(bf16[512,128]{1,0:T(8,128)(2,1)S(1)} %collective-permute-done.far) | copy-start | bytes 393220
  51.2 27.5 %copy-start.4 = (bf16[512,576]{0,1:T(8,128)(2,1)S(1)}, bf16[512,576]{0,1:T(8,128)(2,1)}, u32[]{:S(2)}) copy-start(bf16[512,576]{0,1:T(8,128)(2,1)} %param.9) | copy-start | bytes 1769476
  51.2 0.7 copy-start.1
  80.3 21.3 %all-to-all-start.5 = ((bf16[4,576,512]{2,1,0:T(8,128)(2,1)}), bf16[4,576,512]{2,1,0:T(8,128)(2,1)S(1)}, u32[]{:S(2)}, u32[]{:S(2)}) async-start(bf16[4,576,512]{2,1,0:T(8,128)(2,1)} %broadcast_in_dim.97), calls=%async_computation.5 | async-start | bytes 4718592 | tf_op jit(solution)/shard_map/all_to_all | solution.py:54
  101.6 55.9 %copy-start = (bf16[4,576,512]{2,1,0:T(8,128)(2,1)}, bf16[4,576,512]{2,1,0:T(8,128)(2,1)S(1)}, u32[]{:S(2)}) copy-start(bf16[4,576,512]{2,1,0:T(8,128)(2,1)S(1)} %all-to-all-done.5.mine) | copy-start | bytes 7077892
  101.6 24.4 %all-to-all-start.4 = ((bf16[4,64,576]{2,1,0:T(8,128)(2,1)}), bf16[4,64,576]{2,1,0:T(8,128)(2,1)S(1)}, u32[]{:S(2)}, u32[]{:S(2)}) async-start(bf16[4,64,576]{2,1,0:T(8,128)(2,1)} %broadcast_in_dim.96), calls=%async_computation.4 | async-start | bytes 655360 | tf_op jit(solution)/shard_map/all_to_all | solution.py:54
  126.0 0.7 copy-start.2
  154.0 17.9 %all-to-all-start.6 = ((bf16[4,2,512,128]{3,2,1,0:T(8,128)(2,1)}), bf16[4,2,512,128]{3,2,1,0:T(8,128)(2,1)S(1)}, u32[]{:S(2)}, u32[]{:S(2)}) async-start(bf16[4,2,512,128]{3,2,1,0:T(8,128)(2,1)} %get-tuple-element.27), calls=%async_computation.6 | async-start | bytes 2097152 | tf_op jit(solution)/shard_map/all_to_all | solution.py:54
  157.5 57.3 %collective-permute-start.2 = (bf16[4,576,512]{2,1,0:T(8,128)(2,1)S(1)}, bf16[4,576,512]{2,1,0:T(8,128)(2,1)}, u32[]{:S(2)}, u32[]{:S(2)}) collective-permute-start(bf16[4,576,512]{2,1,0:T(8,128)(2,1)S(1)} %all-to-all-done.5.mine), channel_id=1, source_target_pairs={{0,1},{1,0},{2,3},{3,2},{4,5},{5,4},{6,7},{7,6},{8,9},{9,8},{10,11... | collective-permute-start | bytes 7077896 | tf_op jit(solution)/shard_map/ppermute | solution.py:320
  171.9 0.9 copy-start.7
  197.0 16.7 %all-to-all-start.9 = ((bf16[4,4,4,72,128]{4,3,1,2,0:T(8,128)(2,1)}), bf16[4,4,4,72,128]{4,3,1,2,0:T(8,128)(2,1)S(1)}, u32[]{:S(2)}, u32[]{:S(2)}) async-start(bf16[4,4,4,72,128]{4,3,1,2,0:T(8,128)(2,1)} %broadcast_in_dim.100), calls=%async_computation.9 | async-start | bytes 2359296 | tf_op jit(solution)/shard_map/all_to_all | solution.py:54
  200.5 20.6 %collective-permute-start.3 = (bf16[512,128]{1,0:T(8,128)(2,1)}, bf16[512,128]{1,0:T(8,128)(2,1)}, u32[]{:S(2)}, u32[]{:S(2)}) collective-permute-start(bf16[512,128]{1,0:T(8,128)(2,1)} %get-tuple-element.33), channel_id=1, source_target_pairs={{32,0},{40,8},{48,16},{56,24},{64,32},{72,40},{80,48},{88,56},{96,... | collective-permute-start | bytes 393224 | tf_op jit(solution)/shard_map/ppermute | solution.py:30
  201.8 19.3 %collective-permute-start.4 = (bf16[512,128]{1,0:T(8,128)(2,1)}, bf16[512,128]{1,0:T(8,128)(2,1)}, u32[]{:S(2)}, u32[]{:S(2)}) collective-permute-start(bf16[512,128]{1,0:T(8,128)(2,1)} %fusion), channel_id=1, source_target_pairs={{64,0},{72,8},{80,16},{88,24},{96,32},{104,40},{112,48},{120,56},{... | collective-permute-start | bytes 393224 | tf_op jit(solution)/shard_map/ppermute | solution.py:30
  214.8 6.3 %copy-start.3 = (f32[512,128]{1,0:T(8,128)S(1)}, f32[512,128]{1,0:T(8,128)}, u32[]{:S(2)}) copy-start(f32[512,128]{1,0:T(8,128)} %get-tuple-element.32) | copy-start | bytes 786436

commit v3 on v2

v3 whole, which is shorter than its diff:
```python
import functools

import jax
import jax.numpy as jnp
from jax import lax
from jax.experimental import pallas as pl
from jax.experimental.pallas import tpu as pltpu
from jax.sharding import PartitionSpec as P


WINDOW = 4096
SCORE_SCALE = 1.0 / 12.0
SOFT_CAP = 50.0
DAMP_FACTOR = 0.1
LOG2E = 1.4426950408889634
NX = 4
NC = 4
BF = jnp.bfloat16
F32 = jnp.float32
NT = (((1,), (1,)), ((), ()))
INTERPRET = False


def vmem(n):
    return [pl.BlockSpec(memory_space=pltpu.VMEM) for _ in range(n)]


def held(values):
    return [pltpu.with_memory_space_constraint(v, pltpu.VMEM) for v in values]


def limit(mib):
    return pltpu.CompilerParams(vmem_limit_bytes=mib << 20)


def shift_z(value, by, wrap):
    size = lax.axis_size("seq")
    pairs = [(i, (i + by * NX) % size) for i in range(size) if wrap or 0 <= i + by * NX < size]
    return lax.ppermute(value, "seq", pairs)


def shift_x(value, by):
    size = lax.axis_size("seq")
    pairs = [(i, i // NX * NX + (i % NX + by) % NX) for i in range(size)]
    return lax.ppermute(value, "seq", pairs)


def shift_y(value, by):
    size = lax.axis_size("head")
    return lax.ppermute(value, "head", [(i, (i + 2 * by) % size) for i in range(size)])


def x_groups():
    size = lax.axis_size("seq")
    return [[z * NX + x for x in range(NX)] for z in range(size // NX)]


def c_groups():
    size = lax.axis_size("seq")
    return [
        [(b * NC + c) * NX + x for c in range(NC)]
        for b in range(size // NX // NC)
        for x in range(NX)
    ]


def m_groups():
    size = lax.axis_size("seq")
    n_m = size // NX // NC
    return [[(m * NC + c) * NX + x for m in range(n_m)] for c in range(NC) for x in range(NX)]


def exchange(value, axis, groups=None):
    return lax.all_to_all(value, axis, 0, 0, axis_index_groups=groups)


def copies(value, count):
    return jnp.broadcast_to(value[None], (count,) + value.shape)


def attend_kernel(span, s_ref, q_ref, a_ref, z2, z1, z0, p1, p2, p3, own, b1, b2, b3, kbuf, w, tot, adjt):
    rows, hd = z0.shape
    s = s_ref[0]
    pairs = (p1, p2, p3)
    kbuf[0] = z0[...]
    kbuf[4] = z1[...]
    kbuf[8] = z2[...]
    for k in range(1, 4):
        kbuf[k + 4] = pairs[k - 1][0]
        kbuf[k] = pairs[k - 1][1]
    tot[...] = jnp.zeros_like(tot)
    half = rows // 2

    def block(o, mode):
        for piece in range(2):
            lo = piece * half
            keys = kbuf[o, lo : lo + half, :]
            for m in range(2):
                raw = lax.dot_general(
                    keys, q_ref[:, m * hd : (m + 1) * hd], NT, preferred_element_type=F32
                )
                e = jnp.exp2(jnp.tanh(raw * (SCORE_SCALE / SOFT_CAP)) * (SOFT_CAP * LOG2E))
                if mode != 0:
                    key_i = lo + lax.broadcasted_iota(jnp.int32, e.shape, 0)
                    query_i = lax.broadcasted_iota(jnp.int32, e.shape, 1)
                    keep = key_i <= query_i if mode < 0 else key_i > query_i
                    e = jnp.where(keep, e, 0.0)
                tot[m] += jnp.sum(e.reshape(half // 8, 8, rows), axis=0)
                w[o, lo : lo + half, m * rows : (m + 1) * rows] = e.astype(BF)

    block(0, -1)

    def step(o, carry):
        block(o, 0)
        return carry

    lax.fori_loop(1, jnp.minimum(s, span - 1) + 1, step, 0)

    @pl.when(s >= span)
    def _():
        block(span, 1)

    @pl.when(s < span)
    def _():
        def clear(o, carry):
            w[o] = jnp.zeros(w.shape[1:], BF)
            return carry

        lax.fori_loop(s + 1, span + 1, clear, 0)

    for m in range(2):
        inv = 1.0 / jnp.sum(tot[m], axis=0, keepdims=True)
        turned = a_ref[:, m * hd : (m + 1) * hd].astype(F32).T
        adjt[:, m * rows : (m + 1) * rows] = (turned * inv).astype(BF)
    for o in range(span + 1):
        piece = lax.dot_general(w[o], adjt[...], NT, preferred_element_type=F32).astype(BF)
        if o % 4 == 0:
            own[2 - o // 4] = piece
        else:
            (b1, b2, b3)[o % 4 - 1][1 - o // 4] = piece


def attend(s, q, a, keys, pairs, span):
    rows, hd = keys[0].shape
    pair = jax.ShapeDtypeStruct((2, rows, hd), BF)
    return pl.pallas_call(
        functools.partial(attend_kernel, span),
        out_shape=(jax.ShapeDtypeStruct((3, rows, hd), BF), pair, pair, pair),
        in_specs=[pl.BlockSpec(memory_space=pltpu.SMEM)] + vmem(8),
        out_specs=tuple(vmem(4)),
        scratch_shapes=[
            pltpu.VMEM((span + 1, rows, hd), BF),
            pltpu.VMEM((span + 1, rows, 2 * rows), BF),
            pltpu.VMEM((2, 8, rows), F32),
            pltpu.VMEM((hd, 2 * rows), BF),
        ],
        interpret=INTERPRET,
        name="attend",
        compiler_params=limit(24),
    )(s, q, a, *held([*keys, *pairs]))


def pack_kernel(at_ref, act, adj, bg, eig, out):
    lq, hd = adj.shape
    heads = out.shape[0]
    kr = act.shape[1] // heads
    turned = jnp.dot(adj[...], bg[...], preferred_element_type=F32).astype(BF)
    total = jnp.sum(jnp.sum(eig[...].astype(F32), axis=0, keepdims=True), axis=1, keepdims=True)
    high = total.astype(BF).astype(F32)
    mid = (total - high).astype(BF).astype(F32)
    low = total - high - mid
    lane = lax.broadcasted_iota(jnp.int32, (lq, hd - kr), 1)
    tail = jnp.where(lane == 0, high, jnp.where(lane == 1, mid, jnp.where(lane == 2, low, 0.0)))
    out[0, :, :hd] = turned
    out[0, :, hd + kr :] = tail.astype(BF)
    for i in range(heads):

        @pl.when(at_ref[0] == i)
        def _():
            out[0, :, hd : hd + kr] = act[:, i * kr : (i + 1) * kr]

    for i in range(1, heads):
        out[i] = out[0]


def pack_query(at, act, adj, bg, eig, heads):
    lq, hd = adj.shape
    return pl.pallas_call(
        pack_kernel,
        out_shape=jax.ShapeDtypeStruct((heads, lq, 2 * hd), BF),
        in_specs=[pl.BlockSpec(memory_space=pltpu.SMEM)] + vmem(4),
        out_specs=vmem(1)[0],
        interpret=INTERPRET,
        name="pack_query",
        compiler_params=limit(16),
    )(at, act, adj, bg, eig)


def rotate_query_kernel(hd, c_ref, pack, basis, out):
    kr = basis.shape[1]
    acc = None
    for m in range(basis.shape[0]):
        chunk = pack[2 * m + (c_ref[0] >> 1)][:, hd : hd + kr]
        term = jnp.dot(chunk, basis[m], preferred_element_type=F32)
        acc = term if acc is None else acc + term
    acc = acc.astype(BF)
    for i in range(out.shape[0]):
        out[i] = acc


def rotate_query(c, pack, basis, hd):
    return pl.pallas_call(
        functools.partial(rotate_query_kernel, hd),
        out_shape=jax.ShapeDtypeStruct((NX, pack.shape[1], basis.shape[2]), BF),
        in_specs=[pl.BlockSpec(memory_space=pltpu.SMEM)] + vmem(2),
        out_specs=vmem(1)[0],
        interpret=INTERPRET,
        name="rotate_query",
        compiler_params=limit(16),
    )(c, *held([pack, basis]))


def spread_kernel(count, rq, pack, eig, basis, out, rq_t, rows_all, scaled):
    hd = out.shape[3]
    n_m, kr, _ = basis.shape
    per = out.shape[0]
    g = pl.program_id(0)

    @pl.when(g == 0)
    def _():
        total = rq[0].astype(F32)
        for i in range(1, rq.shape[0]):
            total = total + rq[i].astype(F32)
        rq_t[...] = total.T.astype(BF)
        for m in range(n_m):
            rows_all[m * kr : (m + 1) * kr, :] = basis[m].astype(F32)

    sums = pack[:, 0:1, hd + kr : hd + kr + 3].astype(F32)
    damping = jnp.sum(jnp.sum(sums, axis=0), axis=1, keepdims=True) * (DAMP_FACTOR / count)
    for i in range(per):
        turned = pack[g * per + i][:, :hd]
        grad = jnp.dot(rq_t[...], turned, preferred_element_type=F32) * (1.0 / rq.shape[1])
        eigs = eig[:, i * hd : (i + 1) * hd].astype(F32)
        scaled[:, i * hd : (i + 1) * hd] = (grad / (eigs + damping)).astype(BF)
    n = jnp.dot(rows_all[...].astype(BF), scaled[...], preferred_element_type=F32)
    for i in range(per):
        for m in range(n_m):
            out[i, m] = n[m * kr : (m + 1) * kr, i * hd : (i + 1) * hd].astype(BF)


def spread(count, rq, pack, eig, basis, hd):
    heads = pack.shape[0]
    n_m, rows, cols = basis.shape
    per = heads // 2
    return pl.pallas_call(
        functools.partial(spread_kernel, count),
        grid=(2,),
        out_shape=jax.ShapeDtypeStruct((heads, n_m, rows, hd), BF),
        in_specs=[
            *vmem(2),
            pl.BlockSpec((cols, per * hd), lambda g: (0, g)),
            *vmem(1),
        ],
        out_specs=pl.BlockSpec((per, n_m, rows, hd), lambda g: (g, 0, 0, 0)),
        scratch_shapes=[
            pltpu.VMEM((cols, rq.shape[1]), BF),
            pltpu.VMEM((n_m * rows, cols), F32),
            pltpu.VMEM((cols, per * hd), BF),
        ],
        interpret=INTERPRET,
        name="spread",
        compiler_params=limit(16),
    )(*held([rq, pack]), eig, *held([basis]))


def add_planes_kernel(x_ref, own, r1, r2, r3, out_0, out_1, out_2):
    near, mid, far = own[2].astype(F32), own[1].astype(F32), own[0].astype(F32)
    for k, ref in ((1, r1), (2, r2), (3, r3)):
        low, high = ref[0].astype(F32), ref[1].astype(F32)
        later = x_ref[0] + k < NX
        near = near + jnp.where(later, high, 0.0)
        mid = mid + jnp.where(later, low, high)
        far = far + jnp.where(later, 0.0, low)
    out_0[...] = near
    out_1[...] = mid.astype(BF)
    out_2[...] = far.astype(BF)


def add_planes(x, own, got):
    one = own.shape[1:]
    return pl.pallas_call(
        add_planes_kernel,
        out_shape=tuple(jax.ShapeDtypeStruct(one, t) for t in (F32, BF, BF)),
        in_specs=[pl.BlockSpec(memory_space=pltpu.SMEM)] + vmem(4),
        out_specs=tuple(vmem(3)),
        interpret=INTERPRET,
        name="add_planes",
        compiler_params=limit(16),
    )(x, own, *held(got))


def score_kernel(place_ref, n_ref, bg_ref, sum_0, got_1, got_2, partner, *refs):
    *mine, out = refs
    tile = out.shape[2]
    acc = None
    for i, ref in enumerate(mine):
        for at, part in ((place_ref[i], ref), (place_ref[i] ^ 1, partner.at[i])):
            term = jnp.dot(n_ref[at].T, part[...], preferred_element_type=F32)
            acc = term if acc is None else acc + term
    mapped = jnp.dot(bg_ref[...], acc.astype(BF), preferred_element_type=F32)
    adjoint = sum_0[...] + got_1[...].astype(F32) + got_2[...].astype(F32)
    total = jnp.sum(mapped * adjoint.T, axis=0, keepdims=True)
    for i in range(out.shape[1]):
        out[:, i, :] = jnp.broadcast_to(
            total[:, i * tile : (i + 1) * tile], (out.shape[0], tile)
        )


def score(place, n8, bg, sum_0, got_1, got_2, mine, partner):
    _, rows = mine[0].shape
    heads = n8.shape[0]
    tile = 128
    return pl.pallas_call(
        score_kernel,
        out_shape=jax.ShapeDtypeStruct((heads, rows // tile, tile), F32),
        in_specs=[pl.BlockSpec(memory_space=pltpu.SMEM)] + vmem(6 + len(mine)),
        out_specs=vmem(1)[0],
        interpret=INTERPRET,
        name="score",
        compiler_params=limit(16),
    )(place, *held([n8]), bg, *held([sum_0, got_1, got_2, partner, *mine]))


def on_device(
    act, query_rows, key_rows, out_adjoint, basis_input, basis_grad, eigvals, query_act, query_adj
):
    rows, cols = act.shape
    hd = basis_grad.shape[1]
    heads = lax.axis_size("head")
    n_y = heads // 2
    n_m = lax.axis_size("seq") // NX // NC
    span = WINDOW // rows
    tie = lax.optimization_barrier
    s = lax.axis_index("seq")
    h = lax.axis_index("head")
    x = s & (NX - 1)
    c = (s >> 2) & (NC - 1)
    ahead = [x + k < NX for k in range(NX)]

    key_1 = shift_z(key_rows, 1, False)
    key_2 = shift_z(key_rows, 2, False)
    basis = exchange(copies(basis_input, n_m), "seq", m_groups())
    at = (c & 1) * NX + x
    pack = pack_query(at[None], query_act, query_adj, basis_grad[0], eigvals, heads)
    act_t = act.T
    mine = [act_t] + [shift_y(act_t, j) for j in range(1, n_y)]
    key_1, key_2, basis, pack = tie((key_1, key_2, basis, pack))

    pack = exchange(pack, "head")
    pairs = []
    for k in range(1, NX):
        pair = jnp.stack([jnp.where(ahead[k], key_1, key_2), jnp.where(ahead[k], key_rows, key_1)])
        pairs.append(shift_x(pair, k))
    rq = rotate_query(c[None], pack, basis, hd)
    rq, pairs = tie((rq, pairs))

    rq = exchange(rq, "seq", x_groups())
    own, *back = attend(
        s[None], query_rows, out_adjoint, (key_2, key_1, key_rows), pairs, span
    )
    rq = copies(jnp.sum(rq.astype(F32), axis=0).astype(BF), NC)
    rq, own, back = tie((rq, own, back))
    rq = exchange(rq, "seq", c_groups())
    n = spread(float(cols * heads * eigvals.shape[1]), rq, pack, eigvals, basis, hd)
    n, back, mine = tie((n, back, mine))

    n = exchange(n, "head")
    got = [shift_x(back[k - 1], -k) for k in range(1, NX)]
    n = copies(jnp.sum(n.astype(F32), axis=0).astype(BF), NC)
    stacked = jnp.stack(mine)
    n, got, stacked = tie((n, got, stacked))

    n = exchange(n, "seq", c_groups())
    sum_0, sum_1, sum_2 = add_planes(x[None], own, got)
    got_1 = shift_z(sum_1, -1, False)
    got_2 = shift_z(sum_2, -2, False)
    n, stacked = tie((n, stacked))
    n = exchange(copies(n, NX), "seq", x_groups())
    partner = lax.ppermute(stacked, "head", [(i, i ^ 1) for i in range(heads)])
    n = n.transpose(2, 1, 0, 3, 4).reshape(heads, cols, hd)
    place = (h + 2 * (n_y - jnp.arange(n_y, dtype=jnp.int32))) & (heads - 1)
    partial = score(place, n, basis_grad[0], sum_0, got_1, got_2, mine, partner)
    partial = exchange(partial, "head")
    return jnp.sum(partial, axis=0).reshape(rows)


def solution(mesh):
    return jax.shard_map(
        on_device,
        mesh=mesh,
        in_specs=(
            P("seq", "head"),
            P("seq", "head"),
            P("seq", "head"),
            P("seq", "head"),
            P("seq", "head"),
            P("head", None, None),
            P("head", None),
            P(None, "head"),
            P(None, "head"),
        ),
        out_specs=P("seq"),
        check_vma=False,
    )
```

time: 236 us -> 210 us (0.89)
  blocking collectives: 89.3 us -> 42.3 us
  starting transfers between devices: 49.8 us -> 74.1 us
  Pallas kernels: 24.6 us -> 11.7 us
  local copies, waits for them, and re-layouts: 8.44 us -> 19.3 us
  other arithmetic: 9.98 us -> 4.78 us
  waiting for transfers between devices: 51.9 us -> 55.7 us
    all_to_all x6 -> x3, blocking collectives: 89.3 us -> 42.3 us  [exchange(): return lax.all_to_all(value, axis, 0, 0, axis_index_groups=groups)]
    ppermute x1 -> x10, waiting for transfers between devices: 0.01 us -> 30.5 us  [the longest x3 20.9 us: shift_y(): lax.ppermute(value, 'head', [(i, (i + 2 * by) % size) for i in range(size)])]
    ppermute x1 -> x10, starting transfers between devices: 2.66 us -> 31.8 us  [the longest x6 20 us: shift_x(): return lax.ppermute(value, 'seq', pairs)]
    all_to_all x5, waiting for transfers between devices: 37.4 us -> 14.2 us  [exchange(): return lax.all_to_all(value, axis, 0, 0, axis_index_groups=groups)]
    unnamed x18 -> x52, local copies, waits for them, and re-layouts: 2.24 us -> 14.3 us
    pallas_call x2 -> x3, Pallas kernels: 13.7 us -> 6.46 us  [the longest x1 3 us: score(): pl.pallas_call(score_kernel, out_shape=jax.ShapeDtypeStruct((heads, rows...]
    all_to_all x5, starting transfers between devices: 38.7 us -> 34 us  [exchange(): return lax.all_to_all(value, axis, 0, 0, axis_index_groups=groups)]
    ppermute x4, waiting for transfers between devices: 14.5 us -> 10.9 us  [shift_z(): return lax.ppermute(value, 'seq', pairs)]
  transfers between devices with their start and end apart: 10 -> 19, of which waited for: 5 -> 8; matrix products, arithmetic and copies ran while one was open for 5% -> 3% of each run, Pallas kernels for 5% -> 4%
where the time goes in v3:
time: 210 us; the launch traced here: 208 us
  starting transfers between devices  74.1 us (35%)
  waiting for transfers between devices  55.7 us (27%)
  blocking collectives  42.3 us (20%)
  local copies, waits for them, and re-layouts  19.3 us (9%)
  Pallas kernels  11.7 us (6%)
  other arithmetic  4.78 us (2%)
    all_to_all x3, blocking collectives, exchange(): return lax.all_to_all(value, axis, 0, 0, axis_index_groups=groups)  42.3 us
    all_to_all x5, starting transfers between devices, exchange(): return lax.all_to_all(value, axis, 0, 0, axis_index_groups=groups)  34 us
    ppermute x3, waiting for transfers between devices, shift_y(): lax.ppermute(value, 'head', [(i, (i + 2 * by) % size) for i in range(size)])  20.9 us
    ppermute x6, starting transfers between devices, shift_x(): return lax.ppermute(value, 'seq', pairs)  20 us
    unnamed x52, local copies, waits for them, and re-layouts  14.3 us
    all_to_all x5, waiting for transfers between devices, exchange(): return lax.all_to_all(value, axis, 0, 0, axis_index_groups=groups)  14.2 us
    ppermute x4, waiting for transfers between devices, shift_z(): return lax.ppermute(value, 'seq', pairs)  10.9 us
    ppermute x6, waiting for transfers between devices, shift_x(): return lax.ppermute(value, 'seq', pairs)  9.61 us
  transfers between devices with their start and end apart: 19, of which 8 were waited for; matrix products, arithmetic and copies ran while one was open for 3% of the time, Pallas kernels for 4%

profile of v3, /device:TPU:1, one launch (start us, length us, event | category | flops | bytes accessed | tf_op | source)
XLA Modules:
  0.0 208.3 jit_solution(10562394747915032720)
XLA Ops:
  0.0 1.7 broadcast_in_dim.17
  1.7 15.6 %all-to-all-start = ((bf16[4,72,576]{2,1,0:T(8,128)(2,1)}), bf16[4,72,576]{2,1,0:T(8,128)(2,1)S(1)}, u32[]{:S(2)}, u32[]{:S(2)}) async-start(bf16[4,72,576]{2,1,0:T(8,128)(2,1)} %broadcast_in_dim.17), calls=%async_computation | async-start | bytes 737280 | tf_op jit(solution)/shard_map/all_to_all | solution.py:74
  17.3 3.1 %collective-permute-start.1 = (bf16[512,128]{1,0:T(8,128)(2,1)}, bf16[512,128]{1,0:T(8,128)(2,1)S(1)}, u32[]{:S(2)}, u32[]{:S(2)}) collective-permute-start(bf16[512,128]{1,0:T(8,128)(2,1)} %z0.1), channel_id=1, source_target_pairs={{0,64},{8,72},{16,80},{24,88},{32,96},{40,104},{48,112},{56,120},{... | collective-permute-start | bytes 393224 | tf_op jit(solution)/shard_map/ppermute | solution.py:39
  20.4 2.7 %collective-permute-start = (bf16[512,128]{1,0:T(8,128)(2,1)}, bf16[512,128]{1,0:T(8,128)(2,1)S(1)}, u32[]{:S(2)}, u32[]{:S(2)}) collective-permute-start(bf16[512,128]{1,0:T(8,128)(2,1)} %z0.1), channel_id=1, source_target_pairs={{0,32},{8,40},{16,48},{24,56},{32,64},{40,72},{48,80},{56,88},{64,... | collective-permute-start | bytes 393224 | tf_op jit(solution)/shard_map/ppermute | solution.py:39
  23.1 0.0 copy-start
  23.1 1.3 copy-done
  24.4 0.8 copy-done.19
  25.1 0.9 copy-done.21
  26.0 0.7 copy-done.22
  26.7 0.4 pack_query.1
  27.1 0.0 copy-start.14
  27.2 10.9 %collective-permute-done.z1 = bf16[512,128]{1,0:T(8,128)(2,1)S(1)} collective-permute-done((bf16[512,128]{1,0:T(8,128)(2,1)}, bf16[512,128]{1,0:T(8,128)(2,1)S(1)}, u32[]{:S(2)}, u32[]{:S(2)}) %collective-permute-start) | collective-permute-done | bytes 131104 | tf_op jit(solution)/shard_map/ppermute | solution.py:39
  38.1 0.1 select_bitcast_fusion.1
  38.2 3.1 %collective-permute-start.2 = (bf16[2,512,128]{2,1,0:T(8,128)(2,1)S(1)}, bf16[2,512,128]{2,1,0:T(8,128)(2,1)S(1)}, u32[]{:S(2)}, u32[]{:S(2)}) collective-permute-start(bf16[2,512,128]{2,1,0:T(8,128)(2,1)S(1)} %pad_maximum_fusion.1), channel_id=1, source_target_pairs={{0,8},{8,16},{16,24},{24,0},{32,40},{40,48},{48,56},{56,32},{64,72... | collective-permute-start | bytes 786440 | tf_op jit(solution)/shard_map/ppermute | solution.py:45
  41.3 4.4 %collective-permute-start.3 = (bf16[2,512,128]{2,1,0:T(8,128)(2,1)S(1)}, bf16[2,512,128]{2,1,0:T(8,128)(2,1)S(1)}, u32[]{:S(2)}, u32[]{:S(2)}) collective-permute-start(bf16[2,512,128]{2,1,0:T(8,128)(2,1)S(1)} %pad_maximum_fusion.2), channel_id=1, source_target_pairs={{0,16},{8,24},{16,0},{24,8},{32,48},{40,56},{48,32},{56,40},{64,80... | collective-permute-start | bytes 786440 | tf_op jit(solution)/shard_map/ppermute | solution.py:45
  45.7 3.1 %collective-permute-start.4 = (bf16[2,512,128]{2,1,0:T(8,128)(2,1)S(1)}, bf16[2,512,128]{2,1,0:T(8,128)(2,1)S(1)}, u32[]{:S(2)}, u32[]{:S(2)}) collective-permute-start(bf16[2,512,128]{2,1,0:T(8,128)(2,1)S(1)} %pad_maximum_fusion.3), channel_id=1, source_target_pairs={{0,24},{8,0},{16,8},{24,16},{32,56},{40,32},{48,40},{56,48},{64,88... | collective-permute-start | bytes 786440 | tf_op jit(solution)/shard_map/ppermute | solution.py:45
  48.8 19.6 %all_to_all.40.pack = bf16[8,64,256]{2,1,0:T(8,128)(2,1)S(1)} all-to-all(bf16[8,64,256]{2,1,0:T(8,128)(2,1)S(1)} %pack_query.1), channel_id=1, replica_groups=mesh['seq'=64,'head'=8] {'head'}, dimensions={0} | all-to-all | bytes 524288 | tf_op jit(solution)/shard_map/all_to_all | solution.py:74
  68.4 1.0 rotate_query.1
  69.4 0.7 copy-done.4
  70.1 0.7 copy-done.15
  70.8 0.7 copy-done.17
  71.5 4.1 %all-to-all-start.2 = ((bf16[4,64,576]{2,1,0:T(8,128)(2,1)}), bf16[4,64,576]{2,1,0:T(8,128)(2,1)}, u32[]{:S(2)}, u32[]{:S(2)}) async-start(bf16[4,64,576]{2,1,0:T(8,128)(2,1)} %rotate_query.1), calls=%async_computation.2 | async-start | bytes 655360 | tf_op jit(solution)/shard_map/all_to_all | solution.py:74
  75.7 0.9 copy-done.8
  76.6 0.9 copy-done.10
  77.5 0.9 copy-done.13
  78.4 0.9 copy-done.16
  79.4 0.9 copy-done.18
  80.3 3.9 %attend.1 = (bf16[3,512,128]{2,1,0:T(8,128)(2,1)S(1)}, bf16[2,512,128]{2,1,0:T(8,128)(2,1)S(1)}, bf16[2,512,128]{2,1,0:T(8,128)(2,1)S(1)}, bf16[2,512,128]{2,1,0:T(8,128)(2,1)S(1)}) custom-call(s32[1]{0:T(128)} %bitcast.9.s_ref, bf16[512,256]{1,0:T(8,128)(2,1)S(1)} %copy-done.13, bf16[512,256]{1,0:T(8,128)(2,1)S(1)} %copy-done.14, ...), custom_call_target="tpu_custom_call" | custom-call | tf_op jit(solution)/shard_map/attend/pallas_call | solution.py:146
  84.2 0.7 copy-done.23
  84.9 0.7 copy-done.24
  85.6 0.7 copy-done.25
  86.3 1.2 reduce_sum.33
  87.5 0.8 broadcast_in_dim.19
  88.2 6.1 %all-to-all-start.3 = ((bf16[4,64,576]{2,1,0:T(8,128)(2,1)}), bf16[4,64,576]{2,1,0:T(8,128)(2,1)}, u32[]{:S(2)}, u32[]{:S(2)}) async-start(bf16[4,64,576]{2,1,0:T(8,128)(2,1)} %broadcast_in_dim.19), calls=%async_computation.3 | async-start | bytes 655360 | tf_op jit(solution)/shard_map/all_to_all | solution.py:74
  94.3 2.8 %collective-permute-start.7 = (bf16[576,512]{1,0:T(8,128)(2,1)S(1)}, bf16[576,512]{1,0:T(8,128)(2,1)S(1)}, u32[]{:S(2)}, u32[]{:S(2)}) collective-permute-start(bf16[576,512]{1,0:T(8,128)(2,1)S(1)} %bitcast.26), channel_id=1, source_target_pairs={{0,6},{1,7},{2,0},{3,1},{4,2},{5,3},{6,4},{7,5},{8,14},{9,15},{10,... | collective-permute-start | bytes 1769480 | tf_op jit(solution)/shard_map/ppermute | solution.py:50
  97.1 3.1 %collective-permute-start.6 = (bf16[576,512]{1,0:T(8,128)(2,1)S(1)}, bf16[576,512]{1,0:T(8,128)(2,1)S(1)}, u32[]{:S(2)}, u32[]{:S(2)}) collective-permute-start(bf16[576,512]{1,0:T(8,128)(2,1)S(1)} %bitcast.27), channel_id=1, source_target_pairs={{0,4},{1,5},{2,6},{3,7},{4,0},{5,1},{6,2},{7,3},{8,12},{9,13},{10,... | collective-permute-start | bytes 1769480 | tf_op jit(solution)/shard_map/ppermute | solution.py:50
  100.2 1.9 collective-permute-start.5
  102.1 1.0 all-to-all-done.3.rq
  103.2 0.9 copy-done.5
  104.1 2.6 %spread.1 = bf16[8,4,72,128]{3,2,1,0:T(8,128)(2,1)S(1)} custom-call(bf16[4,64,576]{2,1,0:T(8,128)(2,1)} %all-to-all-done.3.rq, bf16[8,64,256]{2,1,0:T(8,128)(2,1)S(1)} %copy-done.5, bf16[576,1024]{1,0:T(8,128)(2,1)S(1)} %copy-done.1, bf16[4,72,576]{2,1,0:T(8,128)(2,1)S(1)} %all-to-all-done.basis), custom_call_target="tpu_custom_call" | custom-call | tf_op jit(solution)/shard_map/spread/pallas_call | solution.py:255
  106.8 0.8 copy-done.3
  107.6 2.2 %collective-permute-done.7.refs_3_ = bf16[576,512]{1,0:T(8,128)(2,1)S(1)} collective-permute-done((bf16[576,512]{1,0:T(8,128)(2,1)S(1)}, bf16[576,512]{1,0:T(8,128)(2,1)S(1)}, u32[]{:S(2)}, u32[]{:S(2)}) %collective-permute-start.7) | collective-permute-done | bytes 589856 | tf_op jit(solution)/shard_map/ppermute | solution.py:50
  109.8 4.1 %collective-permute-done.6.refs_2_ = bf16[576,512]{1,0:T(8,128)(2,1)S(1)} collective-permute-done((bf16[576,512]{1,0:T(8,128)(2,1)S(1)}, bf16[576,512]{1,0:T(8,128)(2,1)S(1)}, u32[]{:S(2)}, u32[]{:S(2)}) %collective-permute-start.6) | collective-permute-done | bytes 589856 | tf_op jit(solution)/shard_map/ppermute | solution.py:50
  113.8 14.7 %collective-permute-done.5.refs_1_ = bf16[576,512]{1,0:T(8,128)(2,1)} collective-permute-done((bf16[576,512]{1,0:T(8,128)(2,1)S(1)}, bf16[576,512]{1,0:T(8,128)(2,1)}, u32[]{:S(2)}, u32[]{:S(2)}) %collective-permute-start.5) | collective-permute-done | bytes 589856 | tf_op jit(solution)/shard_map/ppermute | solution.py:50
  128.5 3.9 %all-to-all-start.4 = ((bf16[8,4,72,128]{3,2,1,0:T(8,128)(2,1)}), bf16[8,4,72,128]{3,2,1,0:T(8,128)(2,1)S(1)}, u32[]{:S(2)}, u32[]{:S(2)}) async-start(bf16[8,4,72,128]{3,2,1,0:T(8,128)(2,1)} %copy-done.3), calls=%async_computation.4 | async-start | bytes 1179648 | tf_op jit(solution)/shard_map/all_to_all | solution.py:74
  132.4 4.5 %collective-permute-start.8 = (bf16[2,512,128]{2,1,0:T(8,128)(2,1)}, bf16[2,512,128]{2,1,0:T(8,128)(2,1)S(1)}, u32[]{:S(2)}, u32[]{:S(2)}) collective-permute-start(bf16[2,512,128]{2,1,0:T(8,128)(2,1)} %copy-done.25), channel_id=1, source_target_pairs={{0,24},{8,0},{16,8},{24,16},{32,56},{40,32},{48,40},{56,48},{64,88... | collective-permute-start | bytes 786440 | tf_op jit(solution)/shard_map/ppermute | solution.py:45
  137.0 2.5 %collective-permute-start.9 = (bf16[2,512,128]{2,1,0:T(8,128)(2,1)}, bf16[2,512,128]{2,1,0:T(8,128)(2,1)S(1)}, u32[]{:S(2)}, u32[]{:S(2)}) collective-permute-start(bf16[2,512,128]{2,1,0:T(8,128)(2,1)} %copy-done.24), channel_id=1, source_target_pairs={{0,16},{8,24},{16,0},{24,8},{32,48},{40,56},{48,32},{56,40},{64,80... | collective-permute-start | bytes 786440 | tf_op jit(solution)/shard_map/ppermute | solution.py:45
  139.4 2.5 %collective-permute-start.10 = (bf16[2,512,128]{2,1,0:T(8,128)(2,1)}, bf16[2,512,128]{2,1,0:T(8,128)(2,1)S(1)}, u32[]{:S(2)}, u32[]{:S(2)}) collective-permute-start(bf16[2,512,128]{2,1,0:T(8,128)(2,1)} %copy-done.23), channel_id=1, source_target_pairs={{0,8},{8,16},{16,24},{24,0},{32,40},{40,48},{48,56},{56,32},{64,72... | collective-permute-start | bytes 786440 | tf_op jit(solution)/shard_map/ppermute | solution.py:45
  141.9 2.8 %pad_maximum_fusion = bf16[4,576,512]{2,1,0:T(8,128)(2,1)} fusion(bf16[1,576,512]{2,1,0:T(8,128)(2,1)S(1)} %bitcast.31, bf16[1,576,512]{2,1,0:T(8,128)(2,1)S(1)} %bitcast.32, bf16[1,576,512]{2,1,0:T(8,128)(2,1)} %bitcast.12, bf16[1,576,512]{2,1,0:T(8,128)(2,1)S(1)} %bitcast.29), kind=kLoop, calls=%fused_computation | loop fusion | flops 3538944 | bytes 4718592 | tf_op jit(solution)/shard_map/stack | solution.py:380
  144.7 0.1 reduce_sum.34
  144.8 3.5 %collective-permute-done.8.r1 = bf16[2,512,128]{2,1,0:T(8,128)(2,1)S(1)} collective-permute-done((bf16[2,512,128]{2,1,0:T(8,128)(2,1)}, bf16[2,512,128]{2,1,0:T(8,128)(2,1)S(1)}, u32[]{:S(2)}, u32[]{:S(2)}) %collective-permute-start.8) | collective-permute-done | bytes 262176 | tf_op jit(solution)/shard_map/ppermute | solution.py:45
  148.3 6.1 %collective-permute-done.10.r3 = bf16[2,512,128]{2,1,0:T(8,128)(2,1)S(1)} collective-permute-done((bf16[2,512,128]{2,1,0:T(8,128)(2,1)}, bf16[2,512,128]{2,1,0:T(8,128)(2,1)S(1)}, u32[]{:S(2)}, u32[]{:S(2)}) %collective-permute-start.10) | collective-permute-done | bytes 262176 | tf_op jit(solution)/shard_map/ppermute | solution.py:45
  154.5 12.9 %all_to_all.41 = bf16[4,4,72,128]{3,2,1,0:T(8,128)(2,1)S(1)} all-to-all(bf16[4,4,72,128]{3,2,1,0:T(8,128)(2,1)S(1)} %broadcast_in_dim.41), channel_id=1, replica_groups={{0,32,64,96},{8,40,72,104},{16,48,80,112},{24,56,88,120},{128,160,192,2..., dimensions={0} | all-to-all | bytes 589824 | tf_op jit(solution)/shard_map/all_to_all | solution.py:74
  167.4 3.9 %collective-permute-start.13 = (bf16[4,576,512]{2,1,0:T(8,128)(2,1)}, bf16[4,576,512]{2,1,0:T(8,128)(2,1)}, u32[]{:S(2)}, u32[]{:S(2)}) collective-permute-start(bf16[4,576,512]{2,1,0:T(8,128)(2,1)} %pad_maximum_fusion), channel_id=1, source_target_pairs={{0,1},{1,0},{2,3},{3,2},{4,5},{5,4},{6,7},{7,6},{8,9},{9,8},{10,11... | collective-permute-start | bytes 7077896 | tf_op jit(solution)/shard_map/ppermute | solution.py:389
  171.4 1.2 broadcast_in_dim.42
  172.5 4.3 %all-to-all-start.6 = ((bf16[4,4,4,72,128]{4,3,1,2,0:T(8,128)(2,1)}), bf16[4,4,4,72,128]{4,3,1,2,0:T(8,128)(2,1)}, u32[]{:S(2)}, u32[]{:S(2)}) async-start(bf16[4,4,4,72,128]{4,3,1,2,0:T(8,128)(2,1)} %broadcast_in_dim.42), calls=%async_computation.6 | async-start | bytes 2359296 | tf_op jit(solution)/shard_map/all_to_all | solution.py:74
  176.9 0.8 add_planes.1
  177.7 1.3 collective-permute-start.11
  179.0 1.3 collective-permute-start.12
  180.3 13.2 %all-to-all-done.6 = bf16[4,4,4,72,128]{4,3,1,2,0:T(8,128)(2,1)} async-done(((bf16[4,4,4,72,128]{4,3,1,2,0:T(8,128)(2,1)}), bf16[4,4,4,72,128]{4,3,1,2,0:T(8,128)(2,1)}, u32[]{:S(2)}, u32[]{:S(2)}) %all-to-all-start.6) | async-done | bytes 1179680 | tf_op jit(solution)/shard_map/all_to_all | solution.py:74
  193.5 1.4 copy.11
  194.9 3.0 %score.1 = f32[8,4,128]{2,1,0:T(4,128)S(1)} custom-call(s32[4]{0:T(128)S(1)} %add_and_fusion.place_ref, bf16[8,576,128]{2,1,0:T(8,128)(2,1)S(1)} %bitcast.25, bf16[128,128]{1,0:T(8,128)(2,1)S(1)} %bitcast.34, f32[512,128]{1,0:T(8,128)S(1)} %get-tuple-element.71.sum_0, bf16[512,128]{1,0:T(8,128)(2,1)S(1)} %collective-permute-done.11.got_1, ...), custom_call_target="tpu_custom_call" | custom-call | tf_op jit(solution)/shard_map/score/pallas_call | solution.py:323
  197.9 9.8 %all_to_all.42 = f32[8,4,128]{2,1,0:T(4,128)S(1)} all-to-all(f32[8,4,128]{2,1,0:T(4,128)S(1)} %score.1), channel_id=1, replica_groups=mesh['seq'=64,'head'=8] {'head'}, dimensions={0} | all-to-all | bytes 32768 | tf_op jit(solution)/shard_map/all_to_all | solution.py:74
  207.7 0.6 reduce_sum.35
  (50 shorter events, 0.2 us)
Async XLA Ops:
  0.0 38.1 %copy-start.6 = (bf16[512,128]{1,0:T(8,128)(2,1)S(1)}, bf16[512,128]{1,0:T(8,128)(2,1)}, u32[]{:S(2)}) copy-start(bf16[512,128]{1,0:T(8,128)(2,1)} %z0.1) | copy-start | bytes 393220
  1.7 36.4 %all-to-all-start = ((bf16[4,72,576]{2,1,0:T(8,128)(2,1)}), bf16[4,72,576]{2,1,0:T(8,128)(2,1)S(1)}, u32[]{:S(2)}, u32[]{:S(2)}) async-start(bf16[4,72,576]{2,1,0:T(8,128)(2,1)} %broadcast_in_dim.17), calls=%async_computation | async-start | bytes 737280 | tf_op jit(solution)/shard_map/all_to_all | solution.py:74
  17.3 9.8 %collective-permute-start.1 = (bf16[512,128]{1,0:T(8,128)(2,1)}, bf16[512,128]{1,0:T(8,128)(2,1)S(1)}, u32[]{:S(2)}, u32[]{:S(2)}) collective-permute-start(bf16[512,128]{1,0:T(8,128)(2,1)} %z0.1), channel_id=1, source_target_pairs={{0,64},{8,72},{16,80},{24,88},{32,96},{40,104},{48,112},{56,120},{... | collective-permute-start | bytes 393224 | tf_op jit(solution)/shard_map/ppermute | solution.py:39
  20.4 17.7 %collective-permute-start = (bf16[512,128]{1,0:T(8,128)(2,1)}, bf16[512,128]{1,0:T(8,128)(2,1)S(1)}, u32[]{:S(2)}, u32[]{:S(2)}) collective-permute-start(bf16[512,128]{1,0:T(8,128)(2,1)} %z0.1), channel_id=1, source_target_pairs={{0,32},{8,40},{16,48},{24,56},{32,64},{40,72},{48,80},{56,88},{64,... | collective-permute-start | bytes 393224 | tf_op jit(solution)/shard_map/ppermute | solution.py:39
  23.1 1.3 copy-start
  24.4 0.8 copy-start.19
  25.1 0.9 copy-start.21
  26.0 0.7 copy-start.22
  27.1 48.5 %copy-start.14 = (bf16[512,256]{1,0:T(8,128)(2,1)S(1)}, bf16[512,256]{1,0:T(8,128)(2,1)}, u32[]{:S(2)}) copy-start(bf16[512,256]{1,0:T(8,128)(2,1)} %a_ref.1) | copy-start | bytes 786436
  27.2 41.3 %copy-start.7 = (bf16[512,128]{1,0:T(8,128)(2,1)}, bf16[512,128]{1,0:T(8,128)(2,1)S(1)}, u32[]{:S(2)}) copy-start(bf16[512,128]{1,0:T(8,128)(2,1)S(1)} %collective-permute-done.1.z2) | copy-start | bytes 393220
  38.1 30.4 %copy-start.9 = (bf16[512,128]{1,0:T(8,128)(2,1)}, bf16[512,128]{1,0:T(8,128)(2,1)S(1)}, u32[]{:S(2)}) copy-start(bf16[512,128]{1,0:T(8,128)(2,1)S(1)} %collective-permute-done.z1) | copy-start | bytes 393220
  38.2 32.0 %collective-permute-start.2 = (bf16[2,512,128]{2,1,0:T(8,128)(2,1)S(1)}, bf16[2,512,128]{2,1,0:T(8,128)(2,1)S(1)}, u32[]{:S(2)}, u32[]{:S(2)}) collective-permute-start(bf16[2,512,128]{2,1,0:T(8,128)(2,1)S(1)} %pad_maximum_fusion.1), channel_id=1, source_target_pairs={{0,8},{8,16},{16,24},{24,0},{32,40},{40,48},{48,56},{56,32},{64,72... | collective-permute-start | bytes 786440 | tf_op jit(solution)/shard_map/ppermute | solution.py:45
  41.3 28.8 %collective-permute-start.3 = (bf16[2,512,128]{2,1,0:T(8,128)(2,1)S(1)}, bf16[2,512,128]{2,1,0:T(8,128)(2,1)S(1)}, u32[]{:S(2)}, u32[]{:S(2)}) collective-permute-start(bf16[2,512,128]{2,1,0:T(8,128)(2,1)S(1)} %pad_maximum_fusion.2), channel_id=1, source_target_pairs={{0,16},{8,24},{16,0},{24,8},{32,48},{40,56},{48,32},{56,40},{64,80... | collective-permute-start | bytes 786440 | tf_op jit(solution)/shard_map/ppermute | solution.py:45
  45.7 25.1 %collective-permute-start.4 = (bf16[2,512,128]{2,1,0:T(8,128)(2,1)S(1)}, bf16[2,512,128]{2,1,0:T(8,128)(2,1)S(1)}, u32[]{:S(2)}, u32[]{:S(2)}) collective-permute-start(bf16[2,512,128]{2,1,0:T(8,128)(2,1)S(1)} %pad_maximum_fusion.3), channel_id=1, source_target_pairs={{0,24},{8,0},{16,8},{24,16},{32,56},{40,32},{48,40},{56,48},{64,88... | collective-permute-start | bytes 786440 | tf_op jit(solution)/shard_map/ppermute | solution.py:45
  68.4 25.9 %copy-start.2 = (bf16[512,576]{0,1:T(8,128)(2,1)S(1)}, bf16[512,576]{0,1:T(8,128)(2,1)}, u32[]{:S(2)}) copy-start(bf16[512,576]{0,1:T(8,128)(2,1)} %param.9) | copy-start | bytes 1769476
  68.4 34.7 %copy-start.1 = (bf16[576,1024]{1,0:T(8,128)(2,1)S(1)}, bf16[576,1024]{1,0:T(8,128)(2,1)}, u32[]{:S(2)}) copy-start(bf16[576,1024]{1,0:T(8,128)(2,1)} %eig.3) | copy-start | bytes 3538948
  69.4 0.7 copy-start.4
  70.1 0.7 copy-start.15
  70.8 0.7 copy-start.17
  71.5 14.8 %all-to-all-start.2 = ((bf16[4,64,576]{2,1,0:T(8,128)(2,1)}), bf16[4,64,576]{2,1,0:T(8,128)(2,1)}, u32[]{:S(2)}, u32[]{:S(2)}) async-start(bf16[4,64,576]{2,1,0:T(8,128)(2,1)} %rotate_query.1), calls=%async_computation.2 | async-start | bytes 655360 | tf_op jit(solution)/shard_map/all_to_all | solution.py:74
  75.7 0.9 copy-start.8
  76.6 0.9 copy-start.10
  77.5 0.9 copy-start.13
  78.4 0.9 copy-start.16
  79.4 0.9 copy-start.18
  84.2 0.7 copy-start.23
  84.9 0.7 copy-start.24
  85.6 0.7 copy-start.25
  86.3 8.0 %copy-start.11 = (bf16[3,512,128]{2,1,0:T(8,128)(2,1)}, bf16[3,512,128]{2,1,0:T(8,128)(2,1)S(1)}, u32[]{:S(2)}) copy-start(bf16[3,512,128]{2,1,0:T(8,128)(2,1)S(1)} %get-tuple-element.67.own) | copy-start | bytes 1179652
  88.2 14.9 %all-to-all-start.3 = ((bf16[4,64,576]{2,1,0:T(8,128)(2,1)}), bf16[4,64,576]{2,1,0:T(8,128)(2,1)}, u32[]{:S(2)}, u32[]{:S(2)}) async-start(bf16[4,64,576]{2,1,0:T(8,128)(2,1)} %broadcast_in_dim.19), calls=%async_computation.3 | async-start | bytes 655360 | tf_op jit(solution)/shard_map/all_to_all | solution.py:74
  94.3 15.4 %collective-permute-start.7 = (bf16[576,512]{1,0:T(8,128)(2,1)S(1)}, bf16[576,512]{1,0:T(8,128)(2,1)S(1)}, u32[]{:S(2)}, u32[]{:S(2)}) collective-permute-start(bf16[576,512]{1,0:T(8,128)(2,1)S(1)} %bitcast.26), channel_id=1, source_target_pairs={{0,6},{1,7},{2,0},{3,1},{4,2},{5,3},{6,4},{7,5},{8,14},{9,15},{10,... | collective-permute-start | bytes 1769480 | tf_op jit(solution)/shard_map/ppermute | solution.py:50
  97.1 16.7 %collective-permute-start.6 = (bf16[576,512]{1,0:T(8,128)(2,1)S(1)}, bf16[576,512]{1,0:T(8,128)(2,1)S(1)}, u32[]{:S(2)}, u32[]{:S(2)}) collective-permute-start(bf16[576,512]{1,0:T(8,128)(2,1)S(1)} %bitcast.27), channel_id=1, source_target_pairs={{0,4},{1,5},{2,6},{3,7},{4,0},{5,1},{6,2},{7,3},{8,12},{9,13},{10,... | collective-permute-start | bytes 1769480 | tf_op jit(solution)/shard_map/ppermute | solution.py:50
  100.2 28.3 %collective-permute-start.5 = (bf16[576,512]{1,0:T(8,128)(2,1)S(1)}, bf16[576,512]{1,0:T(8,128)(2,1)}, u32[]{:S(2)}, u32[]{:S(2)}) collective-permute-start(bf16[576,512]{1,0:T(8,128)(2,1)S(1)} %bitcast.28), channel_id=1, source_target_pairs={{0,2},{1,3},{2,4},{3,5},{4,6},{5,7},{6,0},{7,1},{8,10},{9,11},{10,... | collective-permute-start | bytes 1769480 | tf_op jit(solution)/shard_map/ppermute | solution.py:50
  103.2 1.0 copy-start.5
  106.8 0.8 copy-start.3
  128.5 16.2 %all-to-all-start.4 = ((bf16[8,4,72,128]{3,2,1,0:T(8,128)(2,1)}), bf16[8,4,72,128]{3,2,1,0:T(8,128)(2,1)S(1)}, u32[]{:S(2)}, u32[]{:S(2)}) async-start(bf16[8,4,72,128]{3,2,1,0:T(8,128)(2,1)} %copy-done.3), calls=%async_computation.4 | async-start | bytes 1179648 | tf_op jit(solution)/shard_map/all_to_all | solution.py:74
  132.4 15.8 %collective-permute-start.8 = (bf16[2,512,128]{2,1,0:T(8,128)(2,1)}, bf16[2,512,128]{2,1,0:T(8,128)(2,1)S(1)}, u32[]{:S(2)}, u32[]{:S(2)}) collective-permute-start(bf16[2,512,128]{2,1,0:T(8,128)(2,1)} %copy-done.25), channel_id=1, source_target_pairs={{0,24},{8,0},{16,8},{24,16},{32,56},{40,32},{48,40},{56,48},{64,88... | collective-permute-start | bytes 786440 | tf_op jit(solution)/shard_map/ppermute | solution.py:45
  137.0 11.3 %collective-permute-start.9 = (bf16[2,512,128]{2,1,0:T(8,128)(2,1)}, bf16[2,512,128]{2,1,0:T(8,128)(2,1)S(1)}, u32[]{:S(2)}, u32[]{:S(2)}) collective-permute-start(bf16[2,512,128]{2,1,0:T(8,128)(2,1)} %copy-done.24), channel_id=1, source_target_pairs={{0,16},{8,24},{16,0},{24,8},{32,48},{40,56},{48,32},{56,40},{64,80... | collective-permute-start | bytes 786440 | tf_op jit(solution)/shard_map/ppermute | solution.py:45
  139.4 15.0 %collective-permute-start.10 = (bf16[2,512,128]{2,1,0:T(8,128)(2,1)}, bf16[2,512,128]{2,1,0:T(8,128)(2,1)S(1)}, u32[]{:S(2)}, u32[]{:S(2)}) collective-permute-start(bf16[2,512,128]{2,1,0:T(8,128)(2,1)} %copy-done.23), channel_id=1, source_target_pairs={{0,8},{8,16},{16,24},{24,0},{32,40},{40,48},{48,56},{56,32},{64,72... | collective-permute-start | bytes 786440 | tf_op jit(solution)/shard_map/ppermute | solution.py:45
  167.4 9.5 %copy-start.12 = (bf16[3,512,128]{2,1,0:T(8,128)(2,1)S(1)}, bf16[3,512,128]{2,1,0:T(8,128)(2,1)}, u32[]{:S(2)}) copy-start(bf16[3,512,128]{2,1,0:T(8,128)(2,1)} %copy-done.11) | copy-start | bytes 1179652
  167.4 27.5 %collective-permute-start.13 = (bf16[4,576,512]{2,1,0:T(8,128)(2,1)}, bf16[4,576,512]{2,1,0:T(8,128)(2,1)}, u32[]{:S(2)}, u32[]{:S(2)}) collective-permute-start(bf16[4,576,512]{2,1,0:T(8,128)(2,1)} %pad_maximum_fusion), channel_id=1, source_target_pairs={{0,1},{1,0},{2,3},{3,2},{4,5},{5,4},{6,7},{7,6},{8,9},{9,8},{10,11... | collective-permute-start | bytes 7077896 | tf_op jit(solution)/shard_map/ppermute | solution.py:389
  172.5 20.9 %all-to-all-start.6 = ((bf16[4,4,4,72,128]{4,3,1,2,0:T(8,128)(2,1)}), bf16[4,4,4,72,128]{4,3,1,2,0:T(8,128)(2,1)}, u32[]{:S(2)}, u32[]{:S(2)}) async-start(bf16[4,4,4,72,128]{4,3,1,2,0:T(8,128)(2,1)} %broadcast_in_dim.42), calls=%async_computation.6 | async-start | bytes 2359296 | tf_op jit(solution)/shard_map/all_to_all | solution.py:74
  176.8 18.1 %copy-start.20 = (bf16[1,128,128]{2,1,0:T(8,128)(2,1)S(1)}, bf16[1,128,128]{2,1,0:T(8,128)(2,1)}, u32[]{:S(2)}) copy-start(bf16[1,128,128]{2,1,0:T(8,128)(2,1)} %param.14) | copy-start | bytes 98308
  177.7 17.2 %collective-permute-start.11 = (bf16[512,128]{1,0:T(8,128)(2,1)}, bf16[512,128]{1,0:T(8,128)(2,1)S(1)}, u32[]{:S(2)}, u32[]{:S(2)}) collective-permute-start(bf16[512,128]{1,0:T(8,128)(2,1)} %get-tuple-element.72), channel_id=1, source_target_pairs={{32,0},{40,8},{48,16},{56,24},{64,32},{72,40},{80,48},{88,56},{96,... | collective-permute-start | bytes 393224 | tf_op jit(solution)/shard_map/ppermute | solution.py:39
  179.0 15.9 %collective-permute-start.12 = (bf16[512,128]{1,0:T(8,128)(2,1)S(1)}, bf16[512,128]{1,0:T(8,128)(2,1)S(1)}, u32[]{:S(2)}, u32[]{:S(2)}) collective-permute-start(bf16[512,128]{1,0:T(8,128)(2,1)S(1)} %get-tuple-element.73), channel_id=1, source_target_pairs={{64,0},{72,8},{80,16},{88,24},{96,32},{104,40},{112,48},{120,56},{... | collective-permute-start | bytes 393224 | tf_op jit(solution)/shard_map/ppermute | solution.py:39

commit v4 on v3

--- a/solution.py
+++ b/solution.py
@@ -62,12 +62,6 @@
         for b in range(size // NX // NC)
         for x in range(NX)
     ]
-
-
-def m_groups():
-    size = lax.axis_size("seq")
-    n_m = size // NX // NC
-    return [[(m * NC + c) * NX + x for m in range(n_m)] for c in range(NC) for x in range(NX)]
 
 
 def exchange(value, axis, groups=None):
@@ -156,8 +150,7 @@
         ],
         interpret=INTERPRET,
         name="attend",
-        compiler_params=limit(24),
-    )(s, q, a, *held([*keys, *pairs]))
+    )(s, q, a, *keys, *pairs)
 
 
 def pack_kernel(at_ref, act, adj, bg, eig, out):
@@ -192,37 +185,36 @@
         out_specs=vmem(1)[0],
         interpret=INTERPRET,
         name="pack_query",
-        compiler_params=limit(16),
     )(at, act, adj, bg, eig)
 
 
-def rotate_query_kernel(hd, c_ref, pack, basis, out):
-    kr = basis.shape[1]
+def rotate_query_kernel(hd, h_ref, pack, *refs):
+    *basis, out = refs
     acc = None
-    for m in range(basis.shape[0]):
-        chunk = pack[2 * m + (c_ref[0] >> 1)][:, hd : hd + kr]
-        term = jnp.dot(chunk, basis[m], preferred_element_type=F32)
+    for j, block in enumerate(basis):
+        chunk = pack[h_ref[j]][:, hd : hd + block.shape[0]]
+        term = jnp.dot(chunk, block[...], preferred_element_type=F32)
         acc = term if acc is None else acc + term
     acc = acc.astype(BF)
     for i in range(out.shape[0]):
         out[i] = acc
 
 
-def rotate_query(c, pack, basis, hd):
+def rotate_query(h_index, pack, basis, hd):
     return pl.pallas_call(
         functools.partial(rotate_query_kernel, hd),
-        out_shape=jax.ShapeDtypeStruct((NX, pack.shape[1], basis.shape[2]), BF),
-        in_specs=[pl.BlockSpec(memory_space=pltpu.SMEM)] + vmem(2),
+        out_shape=jax.ShapeDtypeStruct((NX, pack.shape[1], basis[0].shape[1]), BF),
+        in_specs=[pl.BlockSpec(memory_space=pltpu.SMEM)] + vmem(1 + len(basis)),
         out_specs=vmem(1)[0],
         interpret=INTERPRET,
         name="rotate_query",
-        compiler_params=limit(16),
-    )(c, *held([pack, basis]))
-
-
-def spread_kernel(count, rq, pack, eig, basis, out, rq_t, rows_all, scaled):
+    )(h_index, pack, *basis)
+
+
+def spread_kernel(count, rq, pack, eig, *refs):
+    *basis, out, rq_t, rows_all, scaled = refs
     hd = out.shape[3]
-    n_m, kr, _ = basis.shape
+    kr, _ = basis[0].shape
     per = out.shape[0]
     g = pl.program_id(0)
 
@@ -232,8 +224,8 @@
         for i in range(1, rq.shape[0]):
             total = total + rq[i].astype(F32)
         rq_t[...] = total.T.astype(BF)
-        for m in range(n_m):
-            rows_all[m * kr : (m + 1) * kr, :] = basis[m].astype(F32)
+        for j, block in enumerate(basis):
+            rows_all[j * kr : (j + 1) * kr, :] = block[...].astype(F32)
 
     sums = pack[:, 0:1, hd + kr : hd + kr + 3].astype(F32)
     damping = jnp.sum(jnp.sum(sums, axis=0), axis=1, keepdims=True) * (DAMP_FACTOR / count)
@@ -244,23 +236,25 @@
         scaled[:, i * hd : (i + 1) * hd] = (grad / (eigs + damping)).astype(BF)
     n = jnp.dot(rows_all[...].astype(BF), scaled[...], preferred_element_type=F32)
     for i in range(per):
-        for m in range(n_m):
-            out[i, m] = n[m * kr : (m + 1) * kr, i * hd : (i + 1) * hd].astype(BF)
+        for j in range(len(basis)):
+            out[i, j] = n[j * kr : (j + 1) * kr, i * hd : (i + 1) * hd].astype(BF)
 
 
 def spread(count, rq, pack, eig, basis, hd):
     heads = pack.shape[0]
-    n_m, rows, cols = basis.shape
+    n_m = len(basis)
+    rows, cols = basis[0].shape
     per = heads // 2
     return pl.pallas_call(
         functools.partial(spread_kernel, count),
         grid=(2,),
         out_shape=jax.ShapeDtypeStruct((heads, n_m, rows, hd), BF),
         in_specs=[
-            *vmem(2),
+            *vmem(1),
+            pl.BlockSpec(pack.shape, lambda g: (0, 0, 0)),
             pl.BlockSpec((cols, per * hd), lambda g: (0, g)),
-            *vmem(1),
-        ],
+        ]
+        + [pl.BlockSpec((rows, cols), lambda g: (0, 0)) for _ in basis],
         out_specs=pl.BlockSpec((per, n_m, rows, hd), lambda g: (g, 0, 0, 0)),
         scratch_shapes=[
             pltpu.VMEM((cols, rq.shape[1]), BF),
@@ -269,8 +263,7 @@
         ],
         interpret=INTERPRET,
         name="spread",
-        compiler_params=limit(16),
-    )(*held([rq, pack]), eig, *held([basis]))
+    )(*held([rq]), pack, eig, *basis)
 
 
 def add_planes_kernel(x_ref, own, r1, r2, r3, out_0, out_1, out_2):
@@ -295,7 +288,6 @@
         out_specs=tuple(vmem(3)),
         interpret=INTERPRET,
         name="add_planes",
-        compiler_params=limit(16),
     )(x, own, *held(got))
 
 
@@ -344,51 +336,50 @@
     s = lax.axis_index("seq")
     h = lax.axis_index("head")
     x = s & (NX - 1)
-    c = (s >> 2) & (NC - 1)
+    z = s >> 2
+    c = z & (NC - 1)
     ahead = [x + k < NX for k in range(NX)]
+    j = jnp.arange(n_m, dtype=jnp.int32)
 
     key_1 = shift_z(key_rows, 1, False)
     key_2 = shift_z(key_rows, 2, False)
-    basis = exchange(copies(basis_input, n_m), "seq", m_groups())
     at = (c & 1) * NX + x
     pack = pack_query(at[None], query_act, query_adj, basis_grad[0], eigvals, heads)
-    act_t = act.T
-    mine = [act_t] + [shift_y(act_t, j) for j in range(1, n_y)]
-    key_1, key_2, basis, pack = tie((key_1, key_2, basis, pack))
-
     pack = exchange(pack, "head")
+    basis = [basis_input] + [shift_z(basis_input, -NC * i, True) for i in range(1, n_m)]
+    h_index = ((z + NC * j) & (n_m * NC - 1)) >> 1
+    rq = rotate_query(h_index, pack, basis, hd)
+    rq, key_1, key_2 = tie((rq, key_1, key_2))
+
+    rq = exchange(rq, "seq", x_groups())
     pairs = []
     for k in range(1, NX):
         pair = jnp.stack([jnp.where(ahead[k], key_1, key_2), jnp.where(ahead[k], key_rows, key_1)])
         pairs.append(shift_x(pair, k))
-    rq = rotate_query(c[None], pack, basis, hd)
-    rq, pairs = tie((rq, pairs))
-
-    rq = exchange(rq, "seq", x_groups())
+    rq = copies(jnp.sum(rq.astype(F32), axis=0).astype(BF), NC)
+    rq = exchange(rq, "seq", c_groups())
+    act_t = act.T
+    mine = [act_t] + [shift_y(act_t, i) for i in range(1, n_y)]
+    pairs = tie(pairs)
     own, *back = attend(
         s[None], query_rows, out_adjoint, (key_2, key_1, key_rows), pairs, span
     )
-    rq = copies(jnp.sum(rq.astype(F32), axis=0).astype(BF), NC)
     rq, own, back = tie((rq, own, back))
-    rq = exchange(rq, "seq", c_groups())
+
     n = spread(float(cols * heads * eigvals.shape[1]), rq, pack, eigvals, basis, hd)
-    n, back, mine = tie((n, back, mine))
-
     n = exchange(n, "head")
     got = [shift_x(back[k - 1], -k) for k in range(1, NX)]
     n = copies(jnp.sum(n.astype(F32), axis=0).astype(BF), NC)
     stacked = jnp.stack(mine)
-    n, got, stacked = tie((n, got, stacked))
-
     n = exchange(n, "seq", c_groups())
     sum_0, sum_1, sum_2 = add_planes(x[None], own, got)
     got_1 = shift_z(sum_1, -1, False)
     got_2 = shift_z(sum_2, -2, False)
-    n, stacked = tie((n, stacked))
     n = exchange(copies(n, NX), "seq", x_groups())
     partner = lax.ppermute(stacked, "head", [(i, i ^ 1) for i in range(heads)])
     n = n.transpose(2, 1, 0, 3, 4).reshape(heads, cols, hd)
-    place = (h + 2 * (n_y - jnp.arange(n_y, dtype=jnp.int32))) & (heads - 1)
+    of = (h + 2 * (n_y - jnp.arange(n_y, dtype=jnp.int32))) & (heads - 1)
+    place = 2 * (((of >> 1) - (z >> 2)) & (n_m - 1)) + (of & 1)
     partial = score(place, n, basis_grad[0], sum_0, got_1, got_2, mine, partner)
     partial = exchange(partial, "head")
     return jnp.sum(partial, axis=0).reshape(rows)

time: 210 us -> 202 us (0.962)
  local copies, waits for them, and re-layouts: 19.3 us -> 5.51 us
  starting transfers between devices: 74.1 us -> 83.3 us
  Pallas kernels: 11.7 us -> 19.2 us
  blocking collectives: 42.3 us -> 36.7 us
  waiting for transfers between devices: 55.7 us -> 51.8 us
    ppermute x4 -> x7, starting transfers between devices: 8.32 us -> 29 us  [shift_z(): return lax.ppermute(value, 'seq', pairs)]
    all_to_all x5 -> x4, waiting for transfers between devices: 14.2 us -> 0.01 us  [exchange(): return lax.all_to_all(value, axis, 0, 0, axis_index_groups=groups)]
    unnamed x52 -> x26, local copies, waits for them, and re-layouts: 14.3 us -> 2.12 us
    ppermute x4 -> x7, waiting for transfers between devices: 10.9 us -> 22.8 us  [shift_z(): return lax.ppermute(value, 'seq', pairs)]
    all_to_all x5 -> x4, starting transfers between devices: 34 us -> 22.1 us  [exchange(): return lax.all_to_all(value, axis, 0, 0, axis_index_groups=groups)]
    ppermute x3, waiting for transfers between devices: 20.9 us -> 11 us  [shift_y(): lax.ppermute(value, 'head', [(i, (i + 2 * by) % size) for i in range(size)])]
    ppermute x6, waiting for transfers between devices: 9.61 us -> 18 us  [shift_x(): return lax.ppermute(value, 'seq', pairs)]
    all_to_all x3, blocking collectives: 42.3 us -> 36.7 us  [exchange(): return lax.all_to_all(value, axis, 0, 0, axis_index_groups=groups)]
  transfers between devices with their start and end apart: 19 -> 21, of which waited for: 8 -> 8; matrix products, arithmetic and copies ran while one was open for 3% -> 3% of each run, Pallas kernels for 4% -> 7%
where the time goes in v4:
time: 202 us; the launch traced here: 200 us
  starting transfers between devices  83.3 us (41%)
  waiting for transfers between devices  51.8 us (26%)
  blocking collectives  36.7 us (18%)
  Pallas kernels  19.2 us (10%)
  local copies, waits for them, and re-layouts  5.51 us (3%)
  other arithmetic  3.18 us (2%)
    all_to_all x3, blocking collectives, exchange(): return lax.all_to_all(value, axis, 0, 0, axis_index_groups=groups)  36.7 us
    ppermute x7, starting transfers between devices, shift_z(): return lax.ppermute(value, 'seq', pairs)  29 us
    ppermute x7, waiting for transfers between devices, shift_z(): return lax.ppermute(value, 'seq', pairs)  22.8 us
    all_to_all x4, starting transfers between devices, exchange(): return lax.all_to_all(value, axis, 0, 0, axis_index_groups=groups)  22.1 us
    ppermute x6, starting transfers between devices, shift_x(): return lax.ppermute(value, 'seq', pairs)  20.4 us
    ppermute x6, waiting for transfers between devices, shift_x(): return lax.ppermute(value, 'seq', pairs)  18 us
    ppermute x3, waiting for transfers between devices, shift_y(): lax.ppermute(value, 'head', [(i, (i + 2 * by) % size) for i in range(size)])  11 us
    ppermute x3, starting transfers between devices, shift_y(): lax.ppermute(value, 'head', [(i, (i + 2 * by) % size) for i in range(size)])  9.43 us
  transfers between devices with their start and end apart: 21, of which 8 were waited for; matrix products, arithmetic and copies ran while one was open for 3% of the time, Pallas kernels for 7%

profile of v4, /device:TPU:1, one launch (start us, length us, event | category | flops | bytes accessed | tf_op | source)
XLA Modules:
  0.0 200.2 jit_solution(5318825796501464944)
XLA Ops:
  0.0 2.5 %pack_query.1 = bf16[8,64,256]{2,1,0:T(8,128)(2,1)} custom-call(s32[1]{0:T(128)} %bitcast.at_ref, bf16[64,576]{1,0:T(8,128)(2,1)} %act.1, bf16[64,128]{1,0:T(8,128)(2,1)} %adj.1, bf16[128,128]{1,0:T(8,128)(2,1)} %bitcast.34, bf16[576,1024]{1,0:T(8,128)(2,1)} %eig.3), custom_call_target="tpu_custom_call" | custom-call | tf_op jit(solution)/shard_map/pack_query/pallas_call | solution.py:181
  2.5 10.2 %all-to-all-start = ((bf16[8,64,256]{2,1,0:T(8,128)(2,1)}), bf16[8,64,256]{2,1,0:T(8,128)(2,1)S(1)}, u32[]{:S(2)}, u32[]{:S(2)}) async-start(bf16[8,64,256]{2,1,0:T(8,128)(2,1)} %pack_query.1), calls=%async_computation | async-start | bytes 524288 | tf_op jit(solution)/shard_map/all_to_all | solution.py:68
  12.7 1.3 collective-permute-start.4
  14.0 3.0 %collective-permute-start.3 = (bf16[512,128]{1,0:T(8,128)(2,1)}, bf16[512,128]{1,0:T(8,128)(2,1)S(1)}, u32[]{:S(2)}, u32[]{:S(2)}) collective-permute-start(bf16[512,128]{1,0:T(8,128)(2,1)} %z0.1), channel_id=1, source_target_pairs={{0,32},{8,40},{16,48},{24,56},{32,64},{40,72},{48,80},{56,88},{64,... | collective-permute-start | bytes 393224 | tf_op jit(solution)/shard_map/ppermute | solution.py:39
  17.0 8.8 %collective-permute-start.2 = (bf16[72,576]{1,0:T(8,128)(2,1)}, bf16[72,576]{1,0:T(8,128)(2,1)S(1)}, u32[]{:S(2)}, u32[]{:S(2)}) collective-permute-start(bf16[72,576]{1,0:T(8,128)(2,1)} %refs_0_.3), channel_id=1, source_target_pairs={{0,128},{8,136},{16,144},{24,152},{32,160},{40,168},{48,176},{56,1... | collective-permute-start | bytes 248840 | tf_op jit(solution)/shard_map/ppermute | solution.py:39
  25.8 7.9 %collective-permute-start.1 = (bf16[72,576]{1,0:T(8,128)(2,1)}, bf16[72,576]{1,0:T(8,128)(2,1)S(1)}, u32[]{:S(2)}, u32[]{:S(2)}) collective-permute-start(bf16[72,576]{1,0:T(8,128)(2,1)} %refs_0_.3), channel_id=1, source_target_pairs={{0,256},{8,264},{16,272},{24,280},{32,288},{40,296},{48,304},{56,3... | collective-permute-start | bytes 248840 | tf_op jit(solution)/shard_map/ppermute | solution.py:39
  33.8 5.2 %collective-permute-start = (bf16[72,576]{1,0:T(8,128)(2,1)}, bf16[72,576]{1,0:T(8,128)(2,1)S(1)}, u32[]{:S(2)}, u32[]{:S(2)}) collective-permute-start(bf16[72,576]{1,0:T(8,128)(2,1)} %refs_0_.3), channel_id=1, source_target_pairs={{0,384},{8,392},{16,400},{24,408},{32,416},{40,424},{48,432},{56,4... | collective-permute-start | bytes 248840 | tf_op jit(solution)/shard_map/ppermute | solution.py:39
  39.0 0.6 and_shift-right-arithmetic_fusion.h_ref
  39.5 0.0 collective-permute-done.2.refs_3_
  39.5 9.3 %collective-permute-done.1.refs_2_ = bf16[72,576]{1,0:T(8,128)(2,1)S(1)} collective-permute-done((bf16[72,576]{1,0:T(8,128)(2,1)}, bf16[72,576]{1,0:T(8,128)(2,1)S(1)}, u32[]{:S(2)}, u32[]{:S(2)}) %collective-permute-start.1) | collective-permute-done | bytes 82976 | tf_op jit(solution)/shard_map/ppermute | solution.py:39
  48.8 4.3 %collective-permute-done.refs_1_ = bf16[72,576]{1,0:T(8,128)(2,1)S(1)} collective-permute-done((bf16[72,576]{1,0:T(8,128)(2,1)}, bf16[72,576]{1,0:T(8,128)(2,1)S(1)}, u32[]{:S(2)}, u32[]{:S(2)}) %collective-permute-start) | collective-permute-done | bytes 82976 | tf_op jit(solution)/shard_map/ppermute | solution.py:39
  53.1 0.0 all-to-all-done.pack
  53.2 0.6 copy-done.9
  53.8 0.7 copy-done.3
  54.5 2.1 %rotate_query.1 = bf16[4,64,576]{2,1,0:T(8,128)(2,1)} custom-call(s32[4]{0:T(128)} %and_shift-right-arithmetic_fusion.h_ref, bf16[8,64,256]{2,1,0:T(8,128)(2,1)} %copy-done.3, bf16[72,576]{1,0:T(8,128)(2,1)} %refs_0_.3, bf16[72,576]{1,0:T(8,128)(2,1)} %copy-done.9, bf16[72,576]{1,0:T(8,128)(2,1)} %copy-done.8, bf16[72,576]{1,0:T(8,128)(2,1)} %copy-done.7), custom_call_target="tpu_custom_call" | custom-call | tf_op jit(solution)/shard_map/rotate_query/pallas_call | solution.py:204
  56.6 0.0 collective-permute-done.4.z2
  56.6 0.0 collective-permute-done.3.z1
  56.6 4.2 %all-to-all-start.1 = ((bf16[4,64,576]{2,1,0:T(8,128)(2,1)}), bf16[4,64,576]{2,1,0:T(8,128)(2,1)S(1)}, u32[]{:S(2)}, u32[]{:S(2)}) async-start(bf16[4,64,576]{2,1,0:T(8,128)(2,1)} %rotate_query.1), calls=%async_computation.1 | async-start | bytes 655360 | tf_op jit(solution)/shard_map/all_to_all | solution.py:68
  60.8 4.5 %collective-permute-start.15 = (bf16[576,512]{1,0:T(8,128)(2,1)S(1)}, bf16[576,512]{1,0:T(8,128)(2,1)S(1)}, u32[]{:S(2)}, u32[]{:S(2)}) collective-permute-start(bf16[576,512]{1,0:T(8,128)(2,1)S(1)} %bitcast.26), channel_id=1, source_target_pairs={{0,6},{1,7},{2,0},{3,1},{4,2},{5,3},{6,4},{7,5},{8,14},{9,15},{10,... | collective-permute-start | bytes 1769480 | tf_op jit(solution)/shard_map/ppermute | solution.py:50
  65.3 2.5 %collective-permute-start.14 = (bf16[576,512]{1,0:T(8,128)(2,1)S(1)}, bf16[576,512]{1,0:T(8,128)(2,1)S(1)}, u32[]{:S(2)}, u32[]{:S(2)}) collective-permute-start(bf16[576,512]{1,0:T(8,128)(2,1)S(1)} %bitcast.27), channel_id=1, source_target_pairs={{0,4},{1,5},{2,6},{3,7},{4,0},{5,1},{6,2},{7,3},{8,12},{9,13},{10,... | collective-permute-start | bytes 1769480 | tf_op jit(solution)/shard_map/ppermute | solution.py:50
  67.8 2.5 %collective-permute-start.13 = (bf16[576,512]{1,0:T(8,128)(2,1)S(1)}, bf16[576,512]{1,0:T(8,128)(2,1)S(1)}, u32[]{:S(2)}, u32[]{:S(2)}) collective-permute-start(bf16[576,512]{1,0:T(8,128)(2,1)S(1)} %bitcast.28), channel_id=1, source_target_pairs={{0,2},{1,3},{2,4},{3,5},{4,6},{5,7},{6,0},{7,1},{8,10},{9,11},{10,... | collective-permute-start | bytes 1769480 | tf_op jit(solution)/shard_map/ppermute | solution.py:50
  70.3 0.0 all-to-all-done.1
  70.3 0.1 reduce_sum.33
  70.4 0.7 broadcast_in_dim.13
  71.1 3.5 %all-to-all-start.2 = ((bf16[4,64,576]{2,1,0:T(8,128)(2,1)}), bf16[4,64,576]{2,1,0:T(8,128)(2,1)S(1)}, u32[]{:S(2)}, u32[]{:S(2)}) async-start(bf16[4,64,576]{2,1,0:T(8,128)(2,1)} %broadcast_in_dim.13), calls=%async_computation.2 | async-start | bytes 655360 | tf_op jit(solution)/shard_map/all_to_all | solution.py:68
  74.6 0.1 select_bitcast_fusion.1
  74.7 3.4 %collective-permute-start.5 = (bf16[2,512,128]{2,1,0:T(8,128)(2,1)S(1)}, bf16[2,512,128]{2,1,0:T(8,128)(2,1)S(1)}, u32[]{:S(2)}, u32[]{:S(2)}) collective-permute-start(bf16[2,512,128]{2,1,0:T(8,128)(2,1)S(1)} %pad_maximum_fusion.1), channel_id=1, source_target_pairs={{0,8},{8,16},{16,24},{24,0},{32,40},{40,48},{48,56},{56,32},{64,72... | collective-permute-start | bytes 786440 | tf_op jit(solution)/shard_map/ppermute | solution.py:45
  78.1 4.3 %collective-permute-start.6 = (bf16[2,512,128]{2,1,0:T(8,128)(2,1)S(1)}, bf16[2,512,128]{2,1,0:T(8,128)(2,1)}, u32[]{:S(2)}, u32[]{:S(2)}) collective-permute-start(bf16[2,512,128]{2,1,0:T(8,128)(2,1)S(1)} %pad_maximum_fusion.2), channel_id=1, source_target_pairs={{0,16},{8,24},{16,0},{24,8},{32,48},{40,56},{48,32},{56,40},{64,80... | collective-permute-start | bytes 786440 | tf_op jit(solution)/shard_map/ppermute | solution.py:45
  82.5 0.0 collective-permute-done.15.refs_3_
  82.5 3.1 %collective-permute-start.7 = (bf16[2,512,128]{2,1,0:T(8,128)(2,1)S(1)}, bf16[2,512,128]{2,1,0:T(8,128)(2,1)S(1)}, u32[]{:S(2)}, u32[]{:S(2)}) collective-permute-start(bf16[2,512,128]{2,1,0:T(8,128)(2,1)S(1)} %pad_maximum_fusion.3), channel_id=1, source_target_pairs={{0,24},{8,0},{16,8},{24,16},{32,56},{40,32},{48,40},{56,48},{64,88... | collective-permute-start | bytes 786440 | tf_op jit(solution)/shard_map/ppermute | solution.py:45
  85.6 0.0 collective-permute-done.14.refs_2_
  85.6 11.0 %collective-permute-done.13.refs_1_ = bf16[576,512]{1,0:T(8,128)(2,1)S(1)} collective-permute-done((bf16[576,512]{1,0:T(8,128)(2,1)S(1)}, bf16[576,512]{1,0:T(8,128)(2,1)S(1)}, u32[]{:S(2)}, u32[]{:S(2)}) %collective-permute-start.13) | collective-permute-done | bytes 589856 | tf_op jit(solution)/shard_map/ppermute | solution.py:50
  96.6 1.7 pad_maximum_fusion
  98.3 2.4 %collective-permute-start.16 = (bf16[4,576,512]{2,1,0:T(8,128)(2,1)}, bf16[4,576,512]{2,1,0:T(8,128)(2,1)}, u32[]{:S(2)}, u32[]{:S(2)}) collective-permute-start(bf16[4,576,512]{2,1,0:T(8,128)(2,1)} %pad_maximum_fusion), channel_id=1, source_target_pairs={{0,1},{1,0},{2,3},{3,2},{4,5},{5,4},{6,7},{7,6},{8,9},{9,8},{10,11... | collective-permute-start | bytes 7077896 | tf_op jit(solution)/shard_map/ppermute | solution.py:379
  100.7 0.0 collective-permute-done.5.p1
  100.7 0.0 collective-permute-done.6.p2
  100.8 0.0 collective-permute-done.7.p3
  100.8 0.7 copy-done.10
  101.4 0.1 copy-done.11
  101.5 6.1 %attend.1 = (bf16[3,512,128]{2,1,0:T(8,128)(2,1)}, bf16[2,512,128]{2,1,0:T(8,128)(2,1)}, bf16[2,512,128]{2,1,0:T(8,128)(2,1)}, bf16[2,512,128]{2,1,0:T(8,128)(2,1)}) custom-call(s32[1]{0:T(128)} %bitcast.2.s_ref, bf16[512,256]{1,0:T(8,128)(2,1)} %q_ref.1, bf16[512,256]{1,0:T(8,128)(2,1)} %a_ref.1, bf16[512,128]{1,0:T(8,128)(2,1)} %copy-done.5, ...), custom_call_target="tpu_custom_call" | custom-call | tf_op jit(solution)/shard_map/attend/pallas_call | solution.py:140
  107.7 0.0 all-to-all-done.2.rq
  107.7 3.6 %spread.1 = bf16[8,4,72,128]{3,2,1,0:T(8,128)(2,1)} custom-call(bf16[4,64,576]{2,1,0:T(8,128)(2,1)S(1)} %all-to-all-done.2.rq, bf16[8,64,256]{2,1,0:T(8,128)(2,1)} %copy-done.3, bf16[576,1024]{1,0:T(8,128)(2,1)} %eig.3, bf16[72,576]{1,0:T(8,128)(2,1)} %refs_0_.3, bf16[72,576]{1,0:T(8,128)(2,1)} %copy-done.9, bf16[72,576]{1,0:T(8,128)(2,1)} %copy-done.8, ...), custom_call_target="tpu_custom_call" | custom-call | tf_op jit(solution)/shard_map/spread/pallas_call | solution.py:248
  111.3 15.0 %all_to_all.35 = bf16[8,4,72,128]{3,2,1,0:T(8,128)(2,1)S(1)} all-to-all(bf16[8,4,72,128]{3,2,1,0:T(8,128)(2,1)} %spread.1), channel_id=1, replica_groups=mesh['seq'=64,'head'=8] {'head'}, dimensions={0} | all-to-all | bytes 1179648 | tf_op jit(solution)/shard_map/all_to_all | solution.py:68
  126.3 0.1 reduce_sum.34
  126.4 13.5 %all_to_all.36 = bf16[4,4,72,128]{3,2,1,0:T(8,128)(2,1)S(1)} all-to-all(bf16[4,4,72,128]{3,2,1,0:T(8,128)(2,1)S(1)} %broadcast_in_dim.30), channel_id=1, replica_groups={{0,32,64,96},{8,40,72,104},{16,48,80,112},{24,56,88,120},{128,160,192,2..., dimensions={0} | all-to-all | bytes 589824 | tf_op jit(solution)/shard_map/all_to_all | solution.py:68
  140.0 1.2 broadcast_in_dim.31
  141.2 4.3 %all-to-all-start.5 = ((bf16[4,4,4,72,128]{4,3,1,2,0:T(8,128)(2,1)}), bf16[4,4,4,72,128]{4,3,1,2,0:T(8,128)(2,1)}, u32[]{:S(2)}, u32[]{:S(2)}) async-start(bf16[4,4,4,72,128]{4,3,1,2,0:T(8,128)(2,1)} %broadcast_in_dim.31), calls=%async_computation.5 | async-start | bytes 2359296 | tf_op jit(solution)/shard_map/all_to_all | solution.py:68
  145.5 0.0 copy-start.2
  145.5 4.8 %collective-permute-start.8 = (bf16[2,512,128]{2,1,0:T(8,128)(2,1)}, bf16[2,512,128]{2,1,0:T(8,128)(2,1)S(1)}, u32[]{:S(2)}, u32[]{:S(2)}) collective-permute-start(bf16[2,512,128]{2,1,0:T(8,128)(2,1)} %get-tuple-element.35), channel_id=1, source_target_pairs={{0,24},{8,0},{16,8},{24,16},{32,56},{40,32},{48,40},{56,48},{64,88... | collective-permute-start | bytes 786440 | tf_op jit(solution)/shard_map/ppermute | solution.py:45
  150.3 2.3 %collective-permute-start.9 = (bf16[2,512,128]{2,1,0:T(8,128)(2,1)}, bf16[2,512,128]{2,1,0:T(8,128)(2,1)S(1)}, u32[]{:S(2)}, u32[]{:S(2)}) collective-permute-start(bf16[2,512,128]{2,1,0:T(8,128)(2,1)} %get-tuple-element.36), channel_id=1, source_target_pairs={{0,16},{8,24},{16,0},{24,8},{32,48},{40,56},{48,32},{56,40},{64,80... | collective-permute-start | bytes 786440 | tf_op jit(solution)/shard_map/ppermute | solution.py:45
  152.6 2.5 %collective-permute-start.10 = (bf16[2,512,128]{2,1,0:T(8,128)(2,1)S(1)}, bf16[2,512,128]{2,1,0:T(8,128)(2,1)S(1)}, u32[]{:S(2)}, u32[]{:S(2)}) collective-permute-start(bf16[2,512,128]{2,1,0:T(8,128)(2,1)S(1)} %copy-done.12), channel_id=1, source_target_pairs={{0,8},{8,16},{16,24},{24,0},{32,40},{40,48},{48,56},{56,32},{64,72... | collective-permute-start | bytes 786440 | tf_op jit(solution)/shard_map/ppermute | solution.py:45
  155.1 8.1 %collective-permute-done.8.r1 = bf16[2,512,128]{2,1,0:T(8,128)(2,1)S(1)} collective-permute-done((bf16[2,512,128]{2,1,0:T(8,128)(2,1)}, bf16[2,512,128]{2,1,0:T(8,128)(2,1)S(1)}, u32[]{:S(2)}, u32[]{:S(2)}) %collective-permute-start.8) | collective-permute-done | bytes 262176 | tf_op jit(solution)/shard_map/ppermute | solution.py:45
  163.2 1.5 collective-permute-done.9.r2
  164.7 8.4 %collective-permute-done.10.r3 = bf16[2,512,128]{2,1,0:T(8,128)(2,1)S(1)} collective-permute-done((bf16[2,512,128]{2,1,0:T(8,128)(2,1)S(1)}, bf16[2,512,128]{2,1,0:T(8,128)(2,1)S(1)}, u32[]{:S(2)}, u32[]{:S(2)}) %collective-permute-start.10) | collective-permute-done | bytes 262176 | tf_op jit(solution)/shard_map/ppermute | solution.py:45
  173.1 2.0 add_planes.1
  175.1 1.4 collective-permute-start.11
  176.5 1.3 collective-permute-start.12
  177.8 0.0 all-to-all-done.5
  177.8 1.4 copy.11
  179.2 1.9 collective-permute-done.11.got_1
  181.1 7.3 %collective-permute-done.12.got_2 = bf16[512,128]{1,0:T(8,128)(2,1)S(1)} collective-permute-done((bf16[512,128]{1,0:T(8,128)(2,1)}, bf16[512,128]{1,0:T(8,128)(2,1)S(1)}, u32[]{:S(2)}, u32[]{:S(2)}) %collective-permute-start.12) | collective-permute-done | bytes 131104 | tf_op jit(solution)/shard_map/ppermute | solution.py:39
  188.5 2.9 %score.1 = f32[8,4,128]{2,1,0:T(4,128)S(1)} custom-call(s32[4]{0:T(128)S(1)} %and_add_fusion.place_ref, bf16[8,576,128]{2,1,0:T(8,128)(2,1)S(1)} %bitcast.25, bf16[128,128]{1,0:T(8,128)(2,1)S(1)} %bitcast.35, f32[512,128]{1,0:T(8,128)S(1)} %copy-done.1, bf16[512,128]{1,0:T(8,128)(2,1)S(1)} %collective-permute-done.11.got_1, ...), custom_call_target="tpu_custom_call" | custom-call | tf_op jit(solution)/shard_map/score/pallas_call | solution.py:315
  191.3 8.2 %all_to_all.37 = f32[8,4,128]{2,1,0:T(4,128)S(1)} all-to-all(f32[8,4,128]{2,1,0:T(4,128)S(1)} %score.1), channel_id=1, replica_groups=mesh['seq'=64,'head'=8] {'head'}, dimensions={0} | all-to-all | bytes 32768 | tf_op jit(solution)/shard_map/all_to_all | solution.py:68
  199.6 0.6 reduce_sum.35
  (28 shorter events, 0.2 us)
Async XLA Ops:
  0.0 60.8 %copy-start = (bf16[512,576]{0,1:T(8,128)(2,1)S(1)}, bf16[512,576]{0,1:T(8,128)(2,1)}, u32[]{:S(2)}) copy-start(bf16[512,576]{0,1:T(8,128)(2,1)} %param.9) | copy-start | bytes 1769476
  0.0 74.6 %copy-start.4 = (bf16[512,128]{1,0:T(8,128)(2,1)S(1)}, bf16[512,128]{1,0:T(8,128)(2,1)}, u32[]{:S(2)}) copy-start(bf16[512,128]{1,0:T(8,128)(2,1)} %z0.1) | copy-start | bytes 393220
  2.5 50.6 %all-to-all-start = ((bf16[8,64,256]{2,1,0:T(8,128)(2,1)}), bf16[8,64,256]{2,1,0:T(8,128)(2,1)S(1)}, u32[]{:S(2)}, u32[]{:S(2)}) async-start(bf16[8,64,256]{2,1,0:T(8,128)(2,1)} %pack_query.1), calls=%async_computation | async-start | bytes 524288 | tf_op jit(solution)/shard_map/all_to_all | solution.py:68
  12.7 43.9 %collective-permute-start.4 = (bf16[512,128]{1,0:T(8,128)(2,1)}, bf16[512,128]{1,0:T(8,128)(2,1)S(1)}, u32[]{:S(2)}, u32[]{:S(2)}) collective-permute-start(bf16[512,128]{1,0:T(8,128)(2,1)} %z0.1), channel_id=1, source_target_pairs={{0,64},{8,72},{16,80},{24,88},{32,96},{40,104},{48,112},{56,120},{... | collective-permute-start | bytes 393224 | tf_op jit(solution)/shard_map/ppermute | solution.py:39
  14.0 42.6 %collective-permute-start.3 = (bf16[512,128]{1,0:T(8,128)(2,1)}, bf16[512,128]{1,0:T(8,128)(2,1)S(1)}, u32[]{:S(2)}, u32[]{:S(2)}) collective-permute-start(bf16[512,128]{1,0:T(8,128)(2,1)} %z0.1), channel_id=1, source_target_pairs={{0,32},{8,40},{16,48},{24,56},{32,64},{40,72},{48,80},{56,88},{64,... | collective-permute-start | bytes 393224 | tf_op jit(solution)/shard_map/ppermute | solution.py:39
  17.0 22.5 %collective-permute-start.2 = (bf16[72,576]{1,0:T(8,128)(2,1)}, bf16[72,576]{1,0:T(8,128)(2,1)S(1)}, u32[]{:S(2)}, u32[]{:S(2)}) collective-permute-start(bf16[72,576]{1,0:T(8,128)(2,1)} %refs_0_.3), channel_id=1, source_target_pairs={{0,128},{8,136},{16,144},{24,152},{32,160},{40,168},{48,176},{56,1... | collective-permute-start | bytes 248840 | tf_op jit(solution)/shard_map/ppermute | solution.py:39
  25.8 23.0 %collective-permute-start.1 = (bf16[72,576]{1,0:T(8,128)(2,1)}, bf16[72,576]{1,0:T(8,128)(2,1)S(1)}, u32[]{:S(2)}, u32[]{:S(2)}) collective-permute-start(bf16[72,576]{1,0:T(8,128)(2,1)} %refs_0_.3), channel_id=1, source_target_pairs={{0,256},{8,264},{16,272},{24,280},{32,288},{40,296},{48,304},{56,3... | collective-permute-start | bytes 248840 | tf_op jit(solution)/shard_map/ppermute | solution.py:39
  33.8 19.4 %collective-permute-start = (bf16[72,576]{1,0:T(8,128)(2,1)}, bf16[72,576]{1,0:T(8,128)(2,1)S(1)}, u32[]{:S(2)}, u32[]{:S(2)}) collective-permute-start(bf16[72,576]{1,0:T(8,128)(2,1)} %refs_0_.3), channel_id=1, source_target_pairs={{0,384},{8,392},{16,400},{24,408},{32,416},{40,424},{48,432},{56,4... | collective-permute-start | bytes 248840 | tf_op jit(solution)/shard_map/ppermute | solution.py:39
  39.5 13.6 %copy-start.7 = (bf16[72,576]{1,0:T(8,128)(2,1)}, bf16[72,576]{1,0:T(8,128)(2,1)S(1)}, u32[]{:S(2)}) copy-start(bf16[72,576]{1,0:T(8,128)(2,1)S(1)} %collective-permute-done.2.refs_3_) | copy-start | bytes 248836
  48.8 4.3 %copy-start.8 = (bf16[72,576]{1,0:T(8,128)(2,1)}, bf16[72,576]{1,0:T(8,128)(2,1)S(1)}, u32[]{:S(2)}) copy-start(bf16[72,576]{1,0:T(8,128)(2,1)S(1)} %collective-permute-done.1.refs_2_) | copy-start | bytes 248836
  53.1 0.6 copy-start.9
  53.8 0.7 copy-start.3
  56.6 25.9 %copy-start.5 = (bf16[512,128]{1,0:T(8,128)(2,1)}, bf16[512,128]{1,0:T(8,128)(2,1)S(1)}, u32[]{:S(2)}) copy-start(bf16[512,128]{1,0:T(8,128)(2,1)S(1)} %collective-permute-done.4.z2) | copy-start | bytes 393220
  56.6 25.9 %copy-start.6 = (bf16[512,128]{1,0:T(8,128)(2,1)}, bf16[512,128]{1,0:T(8,128)(2,1)S(1)}, u32[]{:S(2)}) copy-start(bf16[512,128]{1,0:T(8,128)(2,1)S(1)} %collective-permute-done.3.z1) | copy-start | bytes 393220
  56.6 13.7 %all-to-all-start.1 = ((bf16[4,64,576]{2,1,0:T(8,128)(2,1)}), bf16[4,64,576]{2,1,0:T(8,128)(2,1)S(1)}, u32[]{:S(2)}, u32[]{:S(2)}) async-start(bf16[4,64,576]{2,1,0:T(8,128)(2,1)} %rotate_query.1), calls=%async_computation.1 | async-start | bytes 655360 | tf_op jit(solution)/shard_map/all_to_all | solution.py:68
  60.8 21.7 %collective-permute-start.15 = (bf16[576,512]{1,0:T(8,128)(2,1)S(1)}, bf16[576,512]{1,0:T(8,128)(2,1)S(1)}, u32[]{:S(2)}, u32[]{:S(2)}) collective-permute-start(bf16[576,512]{1,0:T(8,128)(2,1)S(1)} %bitcast.26), channel_id=1, source_target_pairs={{0,6},{1,7},{2,0},{3,1},{4,2},{5,3},{6,4},{7,5},{8,14},{9,15},{10,... | collective-permute-start | bytes 1769480 | tf_op jit(solution)/shard_map/ppermute | solution.py:50
  65.3 20.3 %collective-permute-start.14 = (bf16[576,512]{1,0:T(8,128)(2,1)S(1)}, bf16[576,512]{1,0:T(8,128)(2,1)S(1)}, u32[]{:S(2)}, u32[]{:S(2)}) collective-permute-start(bf16[576,512]{1,0:T(8,128)(2,1)S(1)} %bitcast.27), channel_id=1, source_target_pairs={{0,4},{1,5},{2,6},{3,7},{4,0},{5,1},{6,2},{7,3},{8,12},{9,13},{10,... | collective-permute-start | bytes 1769480 | tf_op jit(solution)/shard_map/ppermute | solution.py:50
  67.8 28.8 %collective-permute-start.13 = (bf16[576,512]{1,0:T(8,128)(2,1)S(1)}, bf16[576,512]{1,0:T(8,128)(2,1)S(1)}, u32[]{:S(2)}, u32[]{:S(2)}) collective-permute-start(bf16[576,512]{1,0:T(8,128)(2,1)S(1)} %bitcast.28), channel_id=1, source_target_pairs={{0,2},{1,3},{2,4},{3,5},{4,6},{5,7},{6,0},{7,1},{8,10},{9,11},{10,... | collective-permute-start | bytes 1769480 | tf_op jit(solution)/shard_map/ppermute | solution.py:50
  71.1 36.6 %all-to-all-start.2 = ((bf16[4,64,576]{2,1,0:T(8,128)(2,1)}), bf16[4,64,576]{2,1,0:T(8,128)(2,1)S(1)}, u32[]{:S(2)}, u32[]{:S(2)}) async-start(bf16[4,64,576]{2,1,0:T(8,128)(2,1)} %broadcast_in_dim.13), calls=%async_computation.2 | async-start | bytes 655360 | tf_op jit(solution)/shard_map/all_to_all | solution.py:68
  74.7 26.0 %collective-permute-start.5 = (bf16[2,512,128]{2,1,0:T(8,128)(2,1)S(1)}, bf16[2,512,128]{2,1,0:T(8,128)(2,1)S(1)}, u32[]{:S(2)}, u32[]{:S(2)}) collective-permute-start(bf16[2,512,128]{2,1,0:T(8,128)(2,1)S(1)} %pad_maximum_fusion.1), channel_id=1, source_target_pairs={{0,8},{8,16},{16,24},{24,0},{32,40},{40,48},{48,56},{56,32},{64,72... | collective-permute-start | bytes 786440 | tf_op jit(solution)/shard_map/ppermute | solution.py:45
  78.1 22.6 %collective-permute-start.6 = (bf16[2,512,128]{2,1,0:T(8,128)(2,1)S(1)}, bf16[2,512,128]{2,1,0:T(8,128)(2,1)}, u32[]{:S(2)}, u32[]{:S(2)}) collective-permute-start(bf16[2,512,128]{2,1,0:T(8,128)(2,1)S(1)} %pad_maximum_fusion.2), channel_id=1, source_target_pairs={{0,16},{8,24},{16,0},{24,8},{32,48},{40,56},{48,32},{56,40},{64,80... | collective-permute-start | bytes 786440 | tf_op jit(solution)/shard_map/ppermute | solution.py:45
  82.5 18.3 %collective-permute-start.7 = (bf16[2,512,128]{2,1,0:T(8,128)(2,1)S(1)}, bf16[2,512,128]{2,1,0:T(8,128)(2,1)S(1)}, u32[]{:S(2)}, u32[]{:S(2)}) collective-permute-start(bf16[2,512,128]{2,1,0:T(8,128)(2,1)S(1)} %pad_maximum_fusion.3), channel_id=1, source_target_pairs={{0,24},{8,0},{16,8},{24,16},{32,56},{40,32},{48,40},{56,48},{64,88... | collective-permute-start | bytes 786440 | tf_op jit(solution)/shard_map/ppermute | solution.py:45
  98.3 90.1 %collective-permute-start.16 = (bf16[4,576,512]{2,1,0:T(8,128)(2,1)}, bf16[4,576,512]{2,1,0:T(8,128)(2,1)}, u32[]{:S(2)}, u32[]{:S(2)}) collective-permute-start(bf16[4,576,512]{2,1,0:T(8,128)(2,1)} %pad_maximum_fusion), channel_id=1, source_target_pairs={{0,1},{1,0},{2,3},{3,2},{4,5},{5,4},{6,7},{7,6},{8,9},{9,8},{10,11... | collective-permute-start | bytes 7077896 | tf_op jit(solution)/shard_map/ppermute | solution.py:379
  100.7 0.7 copy-start.10
  100.8 0.8 copy-start.11
  139.9 12.7 %copy-start.12 = (bf16[2,512,128]{2,1,0:T(8,128)(2,1)S(1)}, bf16[2,512,128]{2,1,0:T(8,128)(2,1)}, u32[]{:S(2)}) copy-start(bf16[2,512,128]{2,1,0:T(8,128)(2,1)} %get-tuple-element.37) | copy-start | bytes 786436
  141.2 36.7 %all-to-all-start.5 = ((bf16[4,4,4,72,128]{4,3,1,2,0:T(8,128)(2,1)}), bf16[4,4,4,72,128]{4,3,1,2,0:T(8,128)(2,1)}, u32[]{:S(2)}, u32[]{:S(2)}) async-start(bf16[4,4,4,72,128]{4,3,1,2,0:T(8,128)(2,1)} %broadcast_in_dim.31), calls=%async_computation.5 | async-start | bytes 2359296 | tf_op jit(solution)/shard_map/all_to_all | solution.py:68
  145.5 43.0 %copy-start.2 = (bf16[1,128,128]{2,1,0:T(8,128)(2,1)S(1)}, bf16[1,128,128]{2,1,0:T(8,128)(2,1)}, u32[]{:S(2)}) copy-start(bf16[1,128,128]{2,1,0:T(8,128)(2,1)} %param.14) | copy-start | bytes 98308
  145.5 17.7 %collective-permute-start.8 = (bf16[2,512,128]{2,1,0:T(8,128)(2,1)}, bf16[2,512,128]{2,1,0:T(8,128)(2,1)S(1)}, u32[]{:S(2)}, u32[]{:S(2)}) collective-permute-start(bf16[2,512,128]{2,1,0:T(8,128)(2,1)} %get-tuple-element.35), channel_id=1, source_target_pairs={{0,24},{8,0},{16,8},{24,16},{32,56},{40,32},{48,40},{56,48},{64,88... | collective-permute-start | bytes 786440 | tf_op jit(solution)/shard_map/ppermute | solution.py:45
  150.3 14.4 %collective-permute-start.9 = (bf16[2,512,128]{2,1,0:T(8,128)(2,1)}, bf16[2,512,128]{2,1,0:T(8,128)(2,1)S(1)}, u32[]{:S(2)}, u32[]{:S(2)}) collective-permute-start(bf16[2,512,128]{2,1,0:T(8,128)(2,1)} %get-tuple-element.36), channel_id=1, source_target_pairs={{0,16},{8,24},{16,0},{24,8},{32,48},{40,56},{48,32},{56,40},{64,80... | collective-permute-start | bytes 786440 | tf_op jit(solution)/shard_map/ppermute | solution.py:45
  152.6 20.5 %collective-permute-start.10 = (bf16[2,512,128]{2,1,0:T(8,128)(2,1)S(1)}, bf16[2,512,128]{2,1,0:T(8,128)(2,1)S(1)}, u32[]{:S(2)}, u32[]{:S(2)}) collective-permute-start(bf16[2,512,128]{2,1,0:T(8,128)(2,1)S(1)} %copy-done.12), channel_id=1, source_target_pairs={{0,8},{8,16},{16,24},{24,0},{32,40},{40,48},{48,56},{56,32},{64,72... | collective-permute-start | bytes 786440 | tf_op jit(solution)/shard_map/ppermute | solution.py:45
  175.1 13.4 %copy-start.1 = (f32[512,128]{1,0:T(8,128)S(1)}, f32[512,128]{1,0:T(8,128)}, u32[]{:S(2)}) copy-start(f32[512,128]{1,0:T(8,128)} %get-tuple-element.38.sum_0) | copy-start | bytes 786436
  175.1 6.0 %collective-permute-start.11 = (bf16[512,128]{1,0:T(8,128)(2,1)}, bf16[512,128]{1,0:T(8,128)(2,1)S(1)}, u32[]{:S(2)}, u32[]{:S(2)}) collective-permute-start(bf16[512,128]{1,0:T(8,128)(2,1)} %get-tuple-element.39), channel_id=1, source_target_pairs={{32,0},{40,8},{48,16},{56,24},{64,32},{72,40},{80,48},{88,56},{96,... | collective-permute-start | bytes 393224 | tf_op jit(solution)/shard_map/ppermute | solution.py:39
  176.5 11.9 %collective-permute-start.12 = (bf16[512,128]{1,0:T(8,128)(2,1)}, bf16[512,128]{1,0:T(8,128)(2,1)S(1)}, u32[]{:S(2)}, u32[]{:S(2)}) collective-permute-start(bf16[512,128]{1,0:T(8,128)(2,1)} %get-tuple-element.40), channel_id=1, source_target_pairs={{64,0},{72,8},{80,16},{88,24},{96,32},{104,40},{112,48},{120,56},{... | collective-permute-start | bytes 393224 | tf_op jit(solution)/shard_map/ppermute | solution.py:39
